TPU v7x, 32 devices: a whole 2x2x4 slice. The times are simulated.
32 devices in a mesh: gx: 4 (over y, core), gy: 8 (over z, x).
Axes of the slice: x: 2, y: 2, z: 4, core: 2. Of those that a mesh axis runs over, the one named last changes fastest.
Arguments:
- points: bfloat16 [32768, 64], P(('gx', 'gy')), may hold values from -25 to 25
- solution: float32 [32768, 32], P(('gx', 'gy')), may hold values from -6 to 6
- residual: float32 [32768, 32], P(('gx', 'gy')), may hold values from -36 to 36
- near_leaves: int32 [64, 4], P(('gx', 'gy')), may hold values from 0 to 63, as said below
- node_skeleton: int32 [32, 128], P(('gx', 'gy')), may hold values from 0 to 1023, as said below
- upper_skeleton: int32 [31, 128], replicated, may hold values from 0 to 255, as said below
- far_nodes: int32 [64, 16], P(('gx', 'gy')), may hold values from 0 to 62, as said below
Outputs:
- solution_next: float32 [32768, 32], P(('gx', 'gy'))
- residual_next: float32 [32768, 32], P(('gx', 'gy'))
- matvec_image: float32 [32768, 32], P(('gx', 'gy'))
Inputs may be any that keep to these rules, and one draw needn't show every extreme that they name: `near_leaves`: leaves are numbered in point order, 2 to a device in the flat device order. A leaf's 4 near leaves are distinct and lie on other devices of its gx row; the near leaves named by one device's leaves are all distinct, at most 2 of them lie on any one other device, and exactly 2 on some. `node_skeleton`: each row holds 128 distinct positions among its device's 1024 points. `upper_skeleton`: row u holds 128 distinct positions among the 256 skeleton points of nodes 2u+1 and 2u+2, those of 2u+1 first. `far_nodes`: each row holds 16 distinct tree nodes.
All inputs are finite; a program needn't handle non-finite values.
Results may differ from a plain program's by a relative error of at most 0.0033.
Values may be sent and summed in bfloat16 or wider, within the bound.
No kernel may reach another device: no remote copies, remote signals or barrier semaphores. Data moves between devices by JAX's collectives and lax.ppermute only.
A program may use at most 128 MiB of HBM per device.

v0:
```python
import functools
import math

import jax
import jax.numpy as jnp
from jax import lax
from jax.experimental import pallas as pl
from jax.experimental.pallas import tpu as pltpu
from jax.sharding import PartitionSpec as P


LAMBDA_RIDGE = 1.0
FULL = lax.Precision.HIGHEST
BF = jnp.bfloat16
F32 = jnp.float32
EXTRA = 16
GROUP = 16
NT = (((1,), (1,)), ((), ()))


def vmem(count):
    return [pl.BlockSpec(memory_space=pltpu.VMEM)] * count


def pieces(value):
    high = value.astype(BF).astype(F32)
    rest = value - high
    middle = rest.astype(BF).astype(F32)
    return high, middle, (rest - middle).astype(BF).astype(F32)


def square_rows(points):
    wide = points.astype(F32)
    return jnp.sum(wide * wide, axis=0, keepdims=True)


def left_block(points):
    count = points.shape[1]
    wide = points.astype(F32)
    square = jnp.sum(wide * wide, axis=0, keepdims=True)
    extra = jnp.concatenate(
        [*pieces(square), jnp.ones((3, count), F32), jnp.zeros((EXTRA - 6, count), F32)], axis=0
    )
    return jnp.concatenate([-2.0 * wide, extra], axis=0).T.astype(BF)


def right_extra(points):
    count = points.shape[1]
    return jnp.concatenate(
        [jnp.ones((3, count), F32), *pieces(square_rows(points)), jnp.zeros((EXTRA - 6, count), F32)],
        axis=0,
    ).astype(BF)


def kernel_of(left, right, depth):
    distance = jnp.dot(left, right, preferred_element_type=F32)
    return jnp.exp2(distance * (-0.5 * math.log2(math.e) / depth))


def skeleton_body(pick_ref, points_ref, residual_ref, block_ref, left_ref):
    depth, count = points_ref.shape
    rank = pick_ref.shape[1]
    points = points_ref[...]
    onehot = (lax.broadcasted_iota(jnp.int32, (count, rank), 0) == pick_ref[...]).astype(F32).astype(BF)
    chosen = jnp.dot(points, onehot, preferred_element_type=F32).astype(BF)
    right = jnp.concatenate([points, right_extra(points)], axis=0)
    tile = kernel_of(left_block(chosen), right, depth).astype(BF)
    weights = lax.dot_general(
        residual_ref[...].astype(BF), tile, NT, preferred_element_type=F32
    ) * (1.0 / math.sqrt(count))
    block = jnp.concatenate([chosen, weights.astype(BF)], axis=0)
    for copy in range(block_ref.shape[0]):
        block_ref[copy] = block
    left_ref[...] = left_block(points)


def tree_nodes(depth, upper_ref, tree_ref, nodes):
    rank = upper_ref.shape[1]
    lanes = lax.broadcasted_iota(jnp.int32, (2 * rank, rank), 0)
    both = [jnp.concatenate([tree_ref[2 * n + 1], tree_ref[2 * n + 2]], axis=1) for n in nodes]
    picks = [(lanes == upper_ref[pl.ds(n, 1), :]).astype(F32).astype(BF) for n in nodes]
    chosen = [
        jnp.dot(b[:depth], pick, preferred_element_type=F32).astype(BF) for b, pick in zip(both, picks)
    ]
    left = [left_block(points) for points in chosen]
    tiles = [kernel_of(l, b[: depth + EXTRA], depth).astype(BF) for l, b in zip(left, both)]
    ones = jnp.ones((EXTRA, 2 * rank), F32).astype(BF)
    values = [jnp.concatenate([b[depth + EXTRA :], ones], axis=0) for b in both]
    sums = [
        lax.dot_general(v, tile, NT, preferred_element_type=F32) for v, tile in zip(values, tiles)
    ]
    width = values[0].shape[0] - EXTRA
    weights = [(s[:width] / s[width : width + 1]).astype(BF) for s in sums]
    blocks = [
        jnp.concatenate([points, right_extra(points), w], axis=0)
        for points, w in zip(chosen, weights)
    ]
    for node, block in zip(nodes, blocks):
        tree_ref[node] = block


def tree_body(leaf_dev, depth, far_ref, upper_ref, left_ref, own_ref, *refs):
    part_refs, out_ref, tree_ref, acc = refs[:-3], refs[-3], refs[-2], refs[-1]
    row_total = len(part_refs)
    column_total = part_refs[0].shape[0]
    low = row_total * column_total - 1
    mine = lax.axis_index("gx")
    for slot, part_ref in enumerate(part_refs):
        first = low + lax.bitwise_xor(mine, slot) * column_total
        blocks = [part_ref[column] for column in range(column_total)]
        extras = [right_extra(block[:depth]) for block in blocks]
        for column, (block, extra) in enumerate(zip(blocks, extras)):
            tree_ref[first + column, :depth] = block[:depth]
            tree_ref[first + column, depth : depth + EXTRA] = extra
            tree_ref[first + column, depth + EXTRA :] = block[depth:]
    while low:
        low = (low - 1) // 2
        count = low + 1
        size = min(count, GROUP)

        def level(step, carry, low=low, size=size):
            tree_nodes(depth, upper_ref, tree_ref, [low + step * size + k for k in range(size)])
            return carry

        if count == size:
            level(0, 0)
        else:
            lax.fori_loop(0, count // size, level, 0)

    leaf = left_ref.shape[0] // leaf_dev
    rank = tree_ref.shape[2]
    far = far_ref.shape[1]
    for at in range(leaf_dev):
        where = slice(at * leaf, (at + 1) * leaf)
        own = own_ref[:, where]
        right = jnp.concatenate([own[:depth], right_extra(own[:depth])], axis=0)
        tile = kernel_of(left_ref[where], right, depth).astype(BF)
        acc[...] = lax.dot_general(tile, own[depth:], NT, preferred_element_type=F32) * (
            rank / math.sqrt(leaf)
        )

        def step(group, carry, at=at, where=where):
            nodes = [tree_ref[far_ref[at, 4 * group + k]] for k in range(4)]
            both = jnp.concatenate(nodes, axis=1)
            tile = kernel_of(left_ref[where], both[: depth + EXTRA], depth).astype(BF)
            acc[...] += lax.dot_general(tile, both[depth + EXTRA :], NT, preferred_element_type=F32)
            return carry

        lax.fori_loop(0, far // 4, step, 0)
        out_ref[:, where] = acc[...].T * (1.0 / rank)


def near_body(leaf_dev, depth, near_ref, left_ref, part_ref, residual_ref, *refs):
    block_refs = refs[:-5]
    image_ref, small_ref, held, sems, acc = refs[-5:]
    leaf = left_ref.shape[0] // leaf_dev
    near = near_ref.shape[1]
    mine = lax.axis_index("gy")
    columns = len(block_refs) + 1
    total = leaf_dev * near
    for request in range(total):
        wanted = near_ref[request // near, request % near]
        slot = lax.bitwise_xor(lax.rem(wanted // leaf_dev, columns), mine)
        inner = lax.rem(wanted, leaf_dev)
        for at, block_ref in enumerate(block_refs):

            @pl.when(slot == at + 1)
            def _(block_ref=block_ref, inner=inner, request=request):
                source = block_ref.at[:, pl.ds(pl.multiple_of(inner * leaf, leaf), leaf)]
                pltpu.make_async_copy(source, held.at[request], sems.at[request]).start()

    for at in range(leaf_dev):
        acc[...] = jnp.zeros_like(acc)

        def step(place, carry, at=at):
            request = at * near + place
            pltpu.make_async_copy(
                block_refs[0].at[:, :leaf], held.at[request], sems.at[request]
            ).wait()
            block = held[request]
            right = jnp.concatenate([block[:depth], right_extra(block[:depth])], axis=0)
            tile = kernel_of(left_ref[at * leaf : (at + 1) * leaf], right, depth).astype(BF)
            acc[...] += lax.dot_general(tile, block[depth:], NT, preferred_element_type=F32)
            return carry

        lax.fori_loop(0, near, step, 0)
        where = slice(at * leaf, (at + 1) * leaf)
        image_ref[:, where] = (
            LAMBDA_RIDGE * residual_ref[:, where]
            + part_ref[:, where]
            + acc[...].T * (1.0 / math.sqrt(leaf))
        )
    image = image_ref[...]
    gram = lax.dot_general(image, image, NT, precision=FULL, preferred_element_type=F32)
    cross = lax.dot_general(image, residual_ref[...], NT, precision=FULL, preferred_element_type=F32)
    half = gram.shape[0] // 2
    packed = jnp.concatenate([gram[:half], gram[half:], cross[:half], cross[half:]], axis=1)

    def copy(at, carry):
        small_ref[at] = packed
        return carry

    lax.fori_loop(0, small_ref.shape[0], copy, 0, unroll=8)


def solve_body(small_ref, solution_ref, residual_ref, image_ref, solution_out, residual_out):
    order = solution_ref.shape[0]
    packed = small_ref[0]
    for at in range(1, small_ref.shape[0]):
        packed = packed + small_ref[at]
    gram = jnp.concatenate([packed[:, :order], packed[:, order : 2 * order]], axis=0)
    cross = jnp.concatenate([packed[:, 2 * order : 3 * order], packed[:, 3 * order :]], axis=0)
    work = jnp.concatenate([gram, cross], axis=1)
    rows = lax.broadcasted_iota(jnp.int32, (order, 1), 0)
    for column in range(order):
        row = work[column : column + 1]
        inverse = 1.0 / jnp.sqrt(row[:, column : column + 1])
        factor = jnp.where(rows == column, 0.0, work[:, column : column + 1] * inverse)
        work = work - factor * (row * inverse)
    eye = (rows == lax.broadcasted_iota(jnp.int32, (order, order), 1)).astype(F32)
    diagonal = jnp.sum(work[:, :order] * eye, axis=1, keepdims=True)
    coeffs = (work[:, order:] / diagonal).T
    solution_out[...] = solution_ref[...] + jnp.dot(coeffs, residual_ref[...], precision=FULL, preferred_element_type=F32)
    residual_out[...] = residual_ref[...] - jnp.dot(coeffs, image_ref[...], precision=FULL, preferred_element_type=F32)


def step_of(points, solution, residual, near_leaves, node_skeleton, upper_skeleton, far_nodes):
    row_total = lax.axis_size("gx")
    column_total = lax.axis_size("gy")
    device_total = row_total * column_total
    leaf_dev = near_leaves.shape[0]
    near = near_leaves.shape[1]
    count, depth = points.shape
    width = residual.shape[1]
    leaf = count // leaf_dev
    rank = node_skeleton.shape[1]
    points_t = points.T
    residual_t = residual.T
    solution_t = solution.T
    near_block = jnp.concatenate([points_t, residual_t.astype(BF)], axis=0)
    near_blocks = [
        lax.ppermute(near_block, "gy", [(i, i ^ step) for i in range(column_total)])
        for step in range(1, column_total)
    ]
    deep = depth + EXTRA

    blocks, left = pl.pallas_call(
        skeleton_body,
        out_shape=(
            jax.ShapeDtypeStruct((column_total, depth + width, rank), BF),
            jax.ShapeDtypeStruct((count, deep), BF),
        ),
        in_specs=vmem(3),
        out_specs=tuple(vmem(2)),
        name="skeleton",
    )(node_skeleton, points_t, residual_t)
    mine = lax.all_to_all(blocks, "gy", 0, 0)
    parts = [mine]
    step = row_total // 2
    while step:
        swap = [(i, i ^ step) for i in range(row_total)]
        stacked = jnp.stack(parts) if len(parts) > 1 else parts[0][None]
        got = lax.ppermute(stacked, "gx", swap)
        parts = parts + [got[i] for i in range(len(parts))]
        step //= 2
    order = [0]
    step = row_total // 2
    while step:
        order = order + [o ^ step for o in order]
        step //= 2
    parts = [part for _, part in sorted(zip(order, parts), key=lambda pair: pair[0])]
    partial_t = pl.pallas_call(
        functools.partial(tree_body, leaf_dev, depth),
        out_shape=jax.ShapeDtypeStruct((width, count), F32),
        in_specs=[pl.BlockSpec(memory_space=pltpu.SMEM), *vmem(3 + row_total)],
        out_specs=vmem(1)[0],
        scratch_shapes=[
            pltpu.VMEM((2 * device_total - 1, deep + width, rank), BF),
            pltpu.VMEM((leaf, width), F32),
        ],
        name="tree",
    )(far_nodes, upper_skeleton, left, near_block, *parts)
    image_t, small = pl.pallas_call(
        functools.partial(near_body, leaf_dev, depth),
        out_shape=(
            jax.ShapeDtypeStruct((width, count), F32),
            jax.ShapeDtypeStruct((device_total, width // 2, 4 * width), F32),
        ),
        in_specs=[
            pl.BlockSpec(memory_space=pltpu.SMEM),
            *vmem(3 + column_total - 1),
        ],
        out_specs=tuple(vmem(2)),
        scratch_shapes=[
            pltpu.VMEM((leaf_dev * near, depth + width, leaf), BF),
            pltpu.SemaphoreType.DMA((leaf_dev * near,)),
            pltpu.VMEM((leaf, width), F32),
        ],
        name="near",
    )(near_leaves, left, partial_t, residual_t, *near_blocks)
    small = lax.all_to_all(small, ("gx", "gy"), 0, 0)
    solution_next, residual_next = pl.pallas_call(
        solve_body,
        out_shape=(jax.ShapeDtypeStruct((width, count), F32),) * 2,
        in_specs=vmem(4),
        out_specs=tuple(vmem(2)),
        name="solve",
    )(small, solution_t, residual_t, image_t)
    return (solution_next.T, residual_next.T, image_t.T)


def solution(mesh):
    split = P(("gx", "gy"), None)
    return jax.shard_map(
        step_of,
        mesh=mesh,
        in_specs=(split, split, split, split, split, P(), split),
        out_specs=(split, split, split),
        check_vma=False,
    )
```

profile of v0, /device:TPU:0, one launch (start us, length us, event | category | flops | bytes accessed | tf_op | source)
XLA Modules:
  0.0 91.8 jit_solution(2283298388685528096)
XLA Ops:
  0.6 2.4 %skeleton.1 = (bf16[8,96,128]{2,1,0:T(8,128)(2,1)}, bf16[1024,80]{1,0:T(8,128)(2,1)}) custom-call(s32[1,128]{1,0:T(1,128)} %pick_ref.1, bf16[64,1024]{1,0:T(8,128)(2,1)} %bitcast.19, f32[32,1024]{1,0:T(8,128)} %bitcast.13), custom_call_target="tpu_custom_call" | custom-call | tf_op jit(solution)/shard_map/skeleton/pallas_call | solution.py:247
  3.0 15.2 %all_to_all.10.refs_0_ = bf16[8,96,128]{2,1,0:T(8,128)(2,1)S(1)} all-to-all(bf16[8,96,128]{2,1,0:T(8,128)(2,1)} %get-tuple-element.10), channel_id=1, replica_groups=mesh['gx'=4,'gy'=8] {'gy'}, dimensions={0} | all-to-all | bytes 393216 | tf_op jit(solution)/shard_map/all_to_all | solution.py:257
  18.2 0.0 copy-start.1
  18.2 0.0 copy-start
  18.2 1.5 %collective-permute-start = (bf16[1,8,96,128]{3,2,1,0:T(8,128)(2,1)S(1)}, bf16[1,8,96,128]{3,2,1,0:T(8,128)(2,1)S(1)}, u32[]{:S(2)}, u32[]{:S(2)}) collective-permute-start(bf16[1,8,96,128]{3,2,1,0:T(8,128)(2,1)S(1)} %bitcast.16), channel_id=1, source_target_pairs={{0,16},{8,24},{16,0},{24,8},{1,17},{9,25},{17,1},{25,9},{2,18},{10... | collective-permute-start | bytes 589832 | tf_op jit(solution)/shard_map/ppermute | solution.py:263
  19.7 4.2 %collective-permute-done = bf16[1,8,96,128]{3,2,1,0:T(8,128)(2,1)S(1)} collective-permute-done((bf16[1,8,96,128]{3,2,1,0:T(8,128)(2,1)S(1)}, bf16[1,8,96,128]{3,2,1,0:T(8,128)(2,1)S(1)}, u32[]{:S(2)}, u32[]{:S(2)}) %collective-permute-start) | collective-permute-done | bytes 196640 | tf_op jit(solution)/shard_map/ppermute | solution.py:263
  23.9 0.0 copy-start.3
  23.9 0.0 copy-done.1
  23.9 0.6 copy-done.3
  24.6 0.0 copy-start.4
  24.6 0.0 collective-permute-start.1
  24.6 0.0 copy-done
  24.6 0.9 copy-done.4
  25.5 0.0 copy-start.2
  25.5 1.1 %collective-permute-start.2 = (bf16[96,1024]{1,0:T(8,128)(2,1)S(1)}, bf16[96,1024]{1,0:T(8,128)(2,1)S(1)}, u32[]{:S(2)}, u32[]{:S(2)}) collective-permute-start(bf16[96,1024]{1,0:T(8,128)(2,1)S(1)} %pad_maximum_fusion.1.own_ref), channel_id=1, source_target_pairs={{0,1},{1,0},{2,3},{3,2},{4,5},{5,4},{6,7},{7,6},{8,9},{9,8},{10,11... | collective-permute-start | bytes 589832 | tf_op jit(solution)/shard_map/ppermute | solution.py:242
  26.6 0.3 collective-permute-start.3
  26.9 2.1 %collective-permute-start.4 = (bf16[96,1024]{1,0:T(8,128)(2,1)S(1)}, bf16[96,1024]{1,0:T(8,128)(2,1)S(1)}, u32[]{:S(2)}, u32[]{:S(2)}) collective-permute-start(bf16[96,1024]{1,0:T(8,128)(2,1)S(1)} %pad_maximum_fusion.1.own_ref), channel_id=1, source_target_pairs={{0,3},{1,2},{2,1},{3,0},{4,7},{5,6},{6,5},{7,4},{8,11},{9,10},{10,... | collective-permute-start | bytes 589832 | tf_op jit(solution)/shard_map/ppermute | solution.py:242
  29.0 0.7 collective-permute-start.5
  29.8 2.4 %collective-permute-done.2.refs_0_ = bf16[96,1024]{1,0:T(8,128)(2,1)S(1)} collective-permute-done((bf16[96,1024]{1,0:T(8,128)(2,1)S(1)}, bf16[96,1024]{1,0:T(8,128)(2,1)S(1)}, u32[]{:S(2)}, u32[]{:S(2)}) %collective-permute-start.2) | collective-permute-done | bytes 196640 | tf_op jit(solution)/shard_map/ppermute | solution.py:242
  32.2 0.0 copy-start.5
  32.2 0.3 collective-permute-start.6
  32.5 8.0 %collective-permute-done.3.refs_1_ = bf16[96,1024]{1,0:T(8,128)(2,1)S(1)} collective-permute-done((bf16[96,1024]{1,0:T(8,128)(2,1)S(1)}, bf16[96,1024]{1,0:T(8,128)(2,1)S(1)}, u32[]{:S(2)}, u32[]{:S(2)}) %collective-permute-start.3) | collective-permute-done | bytes 196640 | tf_op jit(solution)/shard_map/ppermute | solution.py:242
  40.5 0.0 copy-start.6
  40.5 2.4 %collective-permute-start.7 = (bf16[96,1024]{1,0:T(8,128)(2,1)S(1)}, bf16[96,1024]{1,0:T(8,128)(2,1)S(1)}, u32[]{:S(2)}, u32[]{:S(2)}) collective-permute-start(bf16[96,1024]{1,0:T(8,128)(2,1)S(1)} %pad_maximum_fusion.1.own_ref), channel_id=1, source_target_pairs={{0,6},{1,7},{2,4},{3,5},{4,2},{5,3},{6,0},{7,1},{8,14},{9,15},{10,... | collective-permute-start | bytes 589832 | tf_op jit(solution)/shard_map/ppermute | solution.py:242
  42.8 0.0 collective-permute-done.1
  42.8 1.5 %collective-permute-start.8 = (bf16[96,1024]{1,0:T(8,128)(2,1)S(1)}, bf16[96,1024]{1,0:T(8,128)(2,1)S(1)}, u32[]{:S(2)}, u32[]{:S(2)}) collective-permute-start(bf16[96,1024]{1,0:T(8,128)(2,1)S(1)} %pad_maximum_fusion.1.own_ref), channel_id=1, source_target_pairs={{0,7},{1,6},{2,5},{3,4},{4,3},{5,2},{6,1},{7,0},{8,15},{9,14},{10,... | collective-permute-start | bytes 589832 | tf_op jit(solution)/shard_map/ppermute | solution.py:242
  44.3 0.8 slice_bitcast_fusion
  45.1 0.0 copy-done.2
  45.1 0.0 copy-done.5
  45.1 0.0 copy-done.6
  45.1 9.2 %tree.1.part_ref = f32[32,1024]{1,0:T(8,128)} custom-call(s32[2,16]{1,0:T(2,128)} %far_ref.1, s32[31,128]{1,0:T(8,128)} %upper_ref.1, bf16[1024,80]{1,0:T(8,128)(2,1)} %get-tuple-element.9.left_ref, bf16[96,1024]{1,0:T(8,128)(2,1)} %copy-done.2, bf16[8,96,128]{2,1,0:T(8,128)(2,1)} %copy-done.1, bf16[8,96,128]{2,1,0:T(8,128)(2,1)} %get-tuple-element.16.refs_1_, ...), custom_call_target="tpu_custom_call" | custom-call | tf_op jit(solution)/shard_map/tree/pallas_call | solution.py:272
  54.4 0.0 collective-permute-done.4.refs_2_
  54.4 0.0 copy-start.7
  54.4 0.0 collective-permute-done.5.refs_3_
  54.4 0.0 copy-start.8
  54.4 3.8 %collective-permute-done.6.refs_4_ = bf16[96,1024]{1,0:T(8,128)(2,1)S(1)} collective-permute-done((bf16[96,1024]{1,0:T(8,128)(2,1)S(1)}, bf16[96,1024]{1,0:T(8,128)(2,1)S(1)}, u32[]{:S(2)}, u32[]{:S(2)}) %collective-permute-start.6) | collective-permute-done | bytes 196640 | tf_op jit(solution)/shard_map/ppermute | solution.py:242
  58.1 0.0 copy-start.9
  58.1 0.0 collective-permute-done.7.refs_5_
  58.1 0.0 copy-start.10
  58.2 0.0 collective-permute-done.8.refs_6_
  58.2 0.0 copy-done.7
  58.2 0.0 copy-done.8
  58.2 0.7 copy-done.9
  58.8 0.1 copy-done.10
  58.9 0.7 copy-done.11
  59.6 6.8 %near.1 = (f32[32,1024]{1,0:T(8,128)}, f32[32,16,128]{2,1,0:T(8,128)}) custom-call(s32[2,4]{1,0:T(2,128)} %near_ref.1, bf16[1024,80]{1,0:T(8,128)(2,1)} %get-tuple-element.9.left_ref, f32[32,1024]{1,0:T(8,128)} %tree.1.part_ref, f32[32,1024]{1,0:T(8,128)} %bitcast.14, bf16[96,1024]{1,0:T(8,128)(2,1)} %copy-done.5, bf16[96,1024]{1,0:T(8,128)(2,1)} %copy-done.6, ...), custom_call_target="tpu_custom_call" | custom-call | tf_op jit(solution)/shard_map/near/pallas_call | solution.py:283
  66.4 19.8 %all_to_all.11.small_ref = f32[32,16,128]{2,1,0:T(8,128)} all-to-all(f32[32,16,128]{2,1,0:T(8,128)} %get-tuple-element.11), channel_id=1, replica_groups=mesh['gx'=4,'gy'=8] {'gx','gy'}, dimensions={0} | all-to-all | bytes 524288 | tf_op jit(solution)/shard_map/all_to_all | solution.py:301
  86.2 5.5 %solve.1 = (f32[32,1024]{1,0:T(8,128)}, f32[32,1024]{1,0:T(8,128)}) custom-call(f32[32,16,128]{2,1,0:T(8,128)} %all_to_all.11.small_ref, f32[32,1024]{1,0:T(8,128)} %bitcast.21, f32[32,1024]{1,0:T(8,128)} %bitcast.15, f32[32,1024]{1,0:T(8,128)} %get-tuple-element.12.image_ref), custom_call_target="tpu_custom_call" | custom-call | tf_op jit(solution)/shard_map/solve/pallas_call | solution.py:302
  (4 shorter events, 0.1 us)
Async XLA Ops:
  18.2 5.7 %copy-start.1 = (bf16[8,96,128]{2,1,0:T(8,128)(2,1)}, bf16[8,96,128]{2,1,0:T(8,128)(2,1)S(1)}, u32[]{:S(2)}) copy-start(bf16[8,96,128]{2,1,0:T(8,128)(2,1)S(1)} %all_to_all.10.refs_0_) | copy-start | bytes 589828
  18.2 6.3 %copy-start = (f32[1024,32]{0,1:T(8,128)S(1)}, f32[1024,32]{0,1:T(8,128)}, u32[]{:S(2)}) copy-start(f32[1024,32]{0,1:T(8,128)} %param.9) | copy-start | bytes 393220
  18.2 5.7 %collective-permute-start = (bf16[1,8,96,128]{3,2,1,0:T(8,128)(2,1)S(1)}, bf16[1,8,96,128]{3,2,1,0:T(8,128)(2,1)S(1)}, u32[]{:S(2)}, u32[]{:S(2)}) collective-permute-start(bf16[1,8,96,128]{3,2,1,0:T(8,128)(2,1)S(1)} %bitcast.16), channel_id=1, source_target_pairs={{0,16},{8,24},{16,0},{24,8},{1,17},{9,25},{17,1},{25,9},{2,18},{10... | collective-permute-start | bytes 589832 | tf_op jit(solution)/shard_map/ppermute | solution.py:263
  23.9 0.7 copy-start.3
  24.6 0.9 copy-start.4
  24.6 18.3 %collective-permute-start.1 = (bf16[2,8,96,128]{3,2,1,0:T(8,128)(2,1)S(1)}, bf16[2,8,96,128]{3,2,1,0:T(8,128)(2,1)S(1)}, u32[]{:S(2)}, u32[]{:S(2)}) collective-permute-start(bf16[2,8,96,128]{3,2,1,0:T(8,128)(2,1)S(1)} %pad_maximum_fusion), channel_id=1, source_target_pairs={{0,8},{8,0},{16,24},{24,16},{1,9},{9,1},{17,25},{25,17},{2,10},{10... | collective-permute-start | bytes 1179656 | tf_op jit(solution)/shard_map/ppermute | solution.py:263
  25.5 19.6 %copy-start.2 = (bf16[96,1024]{1,0:T(8,128)(2,1)}, bf16[96,1024]{1,0:T(8,128)(2,1)S(1)}, u32[]{:S(2)}) copy-start(bf16[96,1024]{1,0:T(8,128)(2,1)S(1)} %pad_maximum_fusion.1.own_ref) | copy-start | bytes 589828
  25.5 6.7 %collective-permute-start.2 = (bf16[96,1024]{1,0:T(8,128)(2,1)S(1)}, bf16[96,1024]{1,0:T(8,128)(2,1)S(1)}, u32[]{:S(2)}, u32[]{:S(2)}) collective-permute-start(bf16[96,1024]{1,0:T(8,128)(2,1)S(1)} %pad_maximum_fusion.1.own_ref), channel_id=1, source_target_pairs={{0,1},{1,0},{2,3},{3,2},{4,5},{5,4},{6,7},{7,6},{8,9},{9,8},{10,11... | collective-permute-start | bytes 589832 | tf_op jit(solution)/shard_map/ppermute | solution.py:242
  26.6 13.8 %collective-permute-start.3 = (bf16[96,1024]{1,0:T(8,128)(2,1)S(1)}, bf16[96,1024]{1,0:T(8,128)(2,1)S(1)}, u32[]{:S(2)}, u32[]{:S(2)}) collective-permute-start(bf16[96,1024]{1,0:T(8,128)(2,1)S(1)} %pad_maximum_fusion.1.own_ref), channel_id=1, source_target_pairs={{0,2},{1,3},{2,0},{3,1},{4,6},{5,7},{6,4},{7,5},{8,10},{9,11},{10,... | collective-permute-start | bytes 589832 | tf_op jit(solution)/shard_map/ppermute | solution.py:242
  26.9 27.4 %collective-permute-start.4 = (bf16[96,1024]{1,0:T(8,128)(2,1)S(1)}, bf16[96,1024]{1,0:T(8,128)(2,1)S(1)}, u32[]{:S(2)}, u32[]{:S(2)}) collective-permute-start(bf16[96,1024]{1,0:T(8,128)(2,1)S(1)} %pad_maximum_fusion.1.own_ref), channel_id=1, source_target_pairs={{0,3},{1,2},{2,1},{3,0},{4,7},{5,6},{6,5},{7,4},{8,11},{9,10},{10,... | collective-permute-start | bytes 589832 | tf_op jit(solution)/shard_map/ppermute | solution.py:242
  29.0 25.3 %collective-permute-start.5 = (bf16[96,1024]{1,0:T(8,128)(2,1)S(1)}, bf16[96,1024]{1,0:T(8,128)(2,1)S(1)}, u32[]{:S(2)}, u32[]{:S(2)}) collective-permute-start(bf16[96,1024]{1,0:T(8,128)(2,1)S(1)} %pad_maximum_fusion.1.own_ref), channel_id=1, source_target_pairs={{0,4},{1,5},{2,6},{3,7},{4,0},{5,1},{6,2},{7,3},{8,12},{9,13},{10,... | collective-permute-start | bytes 589832 | tf_op jit(solution)/shard_map/ppermute | solution.py:242
  32.2 12.9 %copy-start.5 = (bf16[96,1024]{1,0:T(8,128)(2,1)}, bf16[96,1024]{1,0:T(8,128)(2,1)S(1)}, u32[]{:S(2)}) copy-start(bf16[96,1024]{1,0:T(8,128)(2,1)S(1)} %collective-permute-done.2.refs_0_) | copy-start | bytes 589828
  32.2 25.9 %collective-permute-start.6 = (bf16[96,1024]{1,0:T(8,128)(2,1)S(1)}, bf16[96,1024]{1,0:T(8,128)(2,1)S(1)}, u32[]{:S(2)}, u32[]{:S(2)}) collective-permute-start(bf16[96,1024]{1,0:T(8,128)(2,1)S(1)} %pad_maximum_fusion.1.own_ref), channel_id=1, source_target_pairs={{0,5},{1,4},{2,7},{3,6},{4,1},{5,0},{6,3},{7,2},{8,13},{9,12},{10,... | collective-permute-start | bytes 589832 | tf_op jit(solution)/shard_map/ppermute | solution.py:242
  40.5 4.7 %copy-start.6 = (bf16[96,1024]{1,0:T(8,128)(2,1)}, bf16[96,1024]{1,0:T(8,128)(2,1)S(1)}, u32[]{:S(2)}) copy-start(bf16[96,1024]{1,0:T(8,128)(2,1)S(1)} %collective-permute-done.3.refs_1_) | copy-start | bytes 589828
  40.5 17.7 %collective-permute-start.7 = (bf16[96,1024]{1,0:T(8,128)(2,1)S(1)}, bf16[96,1024]{1,0:T(8,128)(2,1)S(1)}, u32[]{:S(2)}, u32[]{:S(2)}) collective-permute-start(bf16[96,1024]{1,0:T(8,128)(2,1)S(1)} %pad_maximum_fusion.1.own_ref), channel_id=1, source_target_pairs={{0,6},{1,7},{2,4},{3,5},{4,2},{5,3},{6,0},{7,1},{8,14},{9,15},{10,... | collective-permute-start | bytes 589832 | tf_op jit(solution)/shard_map/ppermute | solution.py:242
  42.8 15.3 %collective-permute-start.8 = (bf16[96,1024]{1,0:T(8,128)(2,1)S(1)}, bf16[96,1024]{1,0:T(8,128)(2,1)S(1)}, u32[]{:S(2)}, u32[]{:S(2)}) collective-permute-start(bf16[96,1024]{1,0:T(8,128)(2,1)S(1)} %pad_maximum_fusion.1.own_ref), channel_id=1, source_target_pairs={{0,7},{1,6},{2,5},{3,4},{4,3},{5,2},{6,1},{7,0},{8,15},{9,14},{10,... | collective-permute-start | bytes 589832 | tf_op jit(solution)/shard_map/ppermute | solution.py:242
  54.4 3.8 %copy-start.7 = (bf16[96,1024]{1,0:T(8,128)(2,1)}, bf16[96,1024]{1,0:T(8,128)(2,1)S(1)}, u32[]{:S(2)}) copy-start(bf16[96,1024]{1,0:T(8,128)(2,1)S(1)} %collective-permute-done.4.refs_2_) | copy-start | bytes 589828
  54.4 3.8 %copy-start.8 = (bf16[96,1024]{1,0:T(8,128)(2,1)}, bf16[96,1024]{1,0:T(8,128)(2,1)S(1)}, u32[]{:S(2)}) copy-start(bf16[96,1024]{1,0:T(8,128)(2,1)S(1)} %collective-permute-done.5.refs_3_) | copy-start | bytes 589828
  58.1 0.7 copy-start.9
  58.1 0.7 copy-start.10
  58.9 0.7 copy-start.11
where the time goes:
time: 92.2 us; the launch traced here: 91.8 us
  blocking collectives  35 us (38%)
  Pallas kernels  24 us (26%)
  waiting for transfers between devices  18.3 us (20%)
  starting transfers between devices  9.96 us (11%)
  local copies, waits for them, and re-layouts  3.73 us (4%)
    all_to_all x1, blocking collectives, step_of(): small = lax.all_to_all(small, ('gx', 'gy'), 0, 0)  19.8 us
    all_to_all x1, blocking collectives, step_of(): mine = lax.all_to_all(blocks, 'gy', 0, 0)  15.2 us
    ppermute x7, waiting for transfers between devices, step_of(): lax.ppermute(near_block, 'gy', [(i, i ^ step) for i in range(column_total)])  14.2 us
    pallas_call x1, Pallas kernels, step_of(): pl.pallas_call(functools.partial(tree_body, leaf_dev, depth), out_shape=j...  9.22 us
    ppermute x7, starting transfers between devices, step_of(): lax.ppermute(near_block, 'gy', [(i, i ^ step) for i in range(column_total)])  8.44 us
    pallas_call x1, Pallas kernels, step_of(): pl.pallas_call(functools.partial(near_body, leaf_dev, depth), out_shape=(...  6.83 us
    pallas_call x1, Pallas kernels, step_of(): pl.pallas_call(solve_body, out_shape=(jax.ShapeDtypeStruct((width, count)...  5.55 us
    ppermute x2, waiting for transfers between devices, step_of(): got = lax.ppermute(stacked, 'gx', swap)  4.15 us
  transfers between devices with their start and end apart: 9, of which 4 were waited for; matrix products, arithmetic and copies ran while one was open for 1% of the time, Pallas kernels for 10%

commit v1 on v0

--- a/solution.py
+++ b/solution.py
@@ -15,6 +15,7 @@
 F32 = jnp.float32
 EXTRA = 16
 GROUP = 16
+GRANT = 24 * 2**20
 NT = (((1,), (1,)), ((), ()))
 
 
@@ -238,10 +239,18 @@
     residual_t = residual.T
     solution_t = solution.T
     near_block = jnp.concatenate([points_t, residual_t.astype(BF)], axis=0)
-    near_blocks = [
-        lax.ppermute(near_block, "gy", [(i, i ^ step) for i in range(column_total)])
-        for step in range(1, column_total)
-    ]
+    top = column_total // 2
+    near_blocks = {}
+
+    def send(step, block):
+        return lax.ppermute(block, "gy", [(i, i ^ step) for i in range(column_total)])
+
+    near_blocks[top] = send(top, near_block)
+    for step in [*range(top + 2, column_total, 2), *range(1, top)]:
+        near_blocks[step] = send(step, near_block)
+    if top > 1:
+        for step in range(top, column_total, 2):
+            near_blocks[step + 1] = send(1, near_blocks[step])
     deep = depth + EXTRA
 
     blocks, left = pl.pallas_call(
@@ -252,23 +261,17 @@
         ),
         in_specs=vmem(3),
         out_specs=tuple(vmem(2)),
-        name="skeleton",
+        compiler_params=pltpu.CompilerParams(vmem_limit_bytes=GRANT),
+    name="skeleton",
     )(node_skeleton, points_t, residual_t)
     mine = lax.all_to_all(blocks, "gy", 0, 0)
-    parts = [mine]
+    parts = {0: mine}
     step = row_total // 2
     while step:
         swap = [(i, i ^ step) for i in range(row_total)]
-        stacked = jnp.stack(parts) if len(parts) > 1 else parts[0][None]
-        got = lax.ppermute(stacked, "gx", swap)
-        parts = parts + [got[i] for i in range(len(parts))]
+        parts.update({slot ^ step: lax.ppermute(part, "gx", swap) for slot, part in parts.items()})
         step //= 2
-    order = [0]
-    step = row_total // 2
-    while step:
-        order = order + [o ^ step for o in order]
-        step //= 2
-    parts = [part for _, part in sorted(zip(order, parts), key=lambda pair: pair[0])]
+    parts = [parts[slot] for slot in range(row_total)]
     partial_t = pl.pallas_call(
         functools.partial(tree_body, leaf_dev, depth),
         out_shape=jax.ShapeDtypeStruct((width, count), F32),
@@ -278,7 +281,8 @@
             pltpu.VMEM((2 * device_total - 1, deep + width, rank), BF),
             pltpu.VMEM((leaf, width), F32),
         ],
-        name="tree",
+        compiler_params=pltpu.CompilerParams(vmem_limit_bytes=GRANT),
+    name="tree",
     )(far_nodes, upper_skeleton, left, near_block, *parts)
     image_t, small = pl.pallas_call(
         functools.partial(near_body, leaf_dev, depth),
@@ -296,14 +300,16 @@
             pltpu.SemaphoreType.DMA((leaf_dev * near,)),
             pltpu.VMEM((leaf, width), F32),
         ],
+        compiler_params=pltpu.CompilerParams(vmem_limit_bytes=GRANT),
         name="near",
-    )(near_leaves, left, partial_t, residual_t, *near_blocks)
+    )(near_leaves, left, partial_t, residual_t, *[near_blocks[step] for step in range(1, column_total)])
     small = lax.all_to_all(small, ("gx", "gy"), 0, 0)
     solution_next, residual_next = pl.pallas_call(
         solve_body,
         out_shape=(jax.ShapeDtypeStruct((width, count), F32),) * 2,
         in_specs=vmem(4),
         out_specs=tuple(vmem(2)),
+        compiler_params=pltpu.CompilerParams(vmem_limit_bytes=GRANT),
         name="solve",
     )(small, solution_t, residual_t, image_t)
     return (solution_next.T, residual_next.T, image_t.T)

time: 92.2 us -> 78.1 us (0.85)
  Pallas kernels: 24 us -> 18.6 us
  blocking collectives: 35 us -> 30.2 us
  waiting for transfers between devices: 18.3 us -> 14 us
  starting transfers between devices: 9.96 us -> 11.7 us
  local copies, waits for them, and re-layouts: 3.73 us -> 2.49 us
    all_to_all x1, blocking collectives: 19.8 us -> 15.2 us  [step_of(): small = lax.all_to_all(small, ('gx', 'gy'), 0, 0)]
    ppermute x9 -> x10, waiting for transfers between devices: 18.3 us -> 14 us  [the longest x7 12.7 us: send(): lax.ppermute(block, 'gy', [(i, i ^ step) for i in range(column_total)])]
    ppermute x9 -> x10, starting transfers between devices: 9.96 us -> 11.7 us  [the longest x7 10.1 us: send(): lax.ppermute(block, 'gy', [(i, i ^ step) for i in range(column_total)])]
    pallas_call x1, Pallas kernels: 2.36 us -> 0.66 us  [step_of(): pl.pallas_call(skeleton_body, out_shape=(jax.ShapeDtypeStruct((column_tot...]
    pallas_call x1, Pallas kernels: 9.22 us -> 7.8 us  [step_of(): pl.pallas_call(functools.partial(tree_body, leaf_dev, depth), out_shape=j...]
    pallas_call x1, Pallas kernels: 5.55 us -> 4.43 us  [step_of(): pl.pallas_call(solve_body, out_shape=(jax.ShapeDtypeStruct((width, count)...]
    pallas_call x1, Pallas kernels: 6.83 us -> 5.75 us  [step_of(): pl.pallas_call(functools.partial(near_body, leaf_dev, depth), out_shape=(...]
    unnamed x24 -> x20, local copies, waits for them, and re-layouts: 2.95 us -> 2.49 us
  transfers between devices with their start and end apart: 9 -> 10, of which waited for: 4 -> 4; matrix products, arithmetic and copies ran while one was open for 1% -> 0% of each run, Pallas kernels for 10% -> 10%
where the time goes in v1:
time: 78.1 us; the launch traced here: 77.8 us
  blocking collectives  30.2 us (39%)
  Pallas kernels  18.6 us (24%)
  waiting for transfers between devices  14 us (18%)
  starting transfers between devices  11.7 us (15%)
  local copies, waits for them, and re-layouts  2.49 us (3%)
    all_to_all x1, blocking collectives, step_of(): small = lax.all_to_all(small, ('gx', 'gy'), 0, 0)  15.2 us
    all_to_all x1, blocking collectives, step_of(): mine = lax.all_to_all(blocks, 'gy', 0, 0)  15 us
    ppermute x7, waiting for transfers between devices, send(): lax.ppermute(block, 'gy', [(i, i ^ step) for i in range(column_total)])  12.7 us
    ppermute x7, starting transfers between devices, send(): lax.ppermute(block, 'gy', [(i, i ^ step) for i in range(column_total)])  10.1 us
    pallas_call x1, Pallas kernels, step_of(): pl.pallas_call(functools.partial(tree_body, leaf_dev, depth), out_shape=j...  7.8 us
    pallas_call x1, Pallas kernels, step_of(): pl.pallas_call(functools.partial(near_body, leaf_dev, depth), out_shape=(...  5.75 us
    pallas_call x1, Pallas kernels, step_of(): pl.pallas_call(solve_body, out_shape=(jax.ShapeDtypeStruct((width, count)...  4.43 us
    unnamed x20, local copies, waits for them, and re-layouts  2.49 us
  transfers between devices with their start and end apart: 10, of which 4 were waited for; matrix products, arithmetic and copies ran while one was open for 0% of the time, Pallas kernels for 10%

profile of v1, /device:TPU:0, one launch (start us, length us, event | category | flops | bytes accessed | tf_op | source)
XLA Modules:
  0.0 77.8 jit_solution(12777177978026547614)
XLA Ops:
  0.6 0.0 copy-start.9
  0.6 0.6 copy-done.9
  1.3 0.0 copy-start
  1.3 0.9 %copy-done = f32[1024,32]{0,1:T(8,128)S(1)} copy-done((f32[1024,32]{0,1:T(8,128)S(1)}, f32[1024,32]{0,1:T(8,128)}, u32[]{:S(2)}) %copy-start) | copy-done | bytes 131096
  2.2 0.0 copy-start.2
  2.2 0.9 %copy-done.2 = bf16[1024,64]{0,1:T(8,128)(2,1)S(1)} copy-done((bf16[1024,64]{0,1:T(8,128)(2,1)S(1)}, bf16[1024,64]{0,1:T(8,128)(2,1)}, u32[]{:S(2)}) %copy-start.2) | copy-done | bytes 131096
  3.1 0.7 skeleton.1
  3.8 15.0 %all_to_all.10.refs_0_ = bf16[8,96,128]{2,1,0:T(8,128)(2,1)S(1)} all-to-all(bf16[8,96,128]{2,1,0:T(8,128)(2,1)S(1)} %get-tuple-element.10), channel_id=1, replica_groups=mesh['gx'=4,'gy'=8] {'gy'}, dimensions={0} | all-to-all | bytes 393216 | tf_op jit(solution)/shard_map/all_to_all | solution.py:267
  18.8 0.0 copy-start.3
  18.8 1.5 %collective-permute-start.1 = (bf16[8,96,128]{2,1,0:T(8,128)(2,1)S(1)}, bf16[8,96,128]{2,1,0:T(8,128)(2,1)S(1)}, u32[]{:S(2)}, u32[]{:S(2)}) collective-permute-start(bf16[8,96,128]{2,1,0:T(8,128)(2,1)S(1)} %all_to_all.10.refs_0_), channel_id=1, source_target_pairs={{0,16},{8,24},{16,0},{24,8},{1,17},{9,25},{17,1},{25,9},{2,18},{10... | collective-permute-start | bytes 589832 | tf_op jit(solution)/shard_map/ppermute | solution.py:272
  20.3 0.0 copy-done.3
  20.3 0.0 copy-start.6
  20.4 0.0 copy-start.8
  20.4 0.8 collective-permute-start.6
  21.1 1.9 %collective-permute-start.8 = (bf16[96,1024]{1,0:T(8,128)(2,1)S(1)}, bf16[96,1024]{1,0:T(8,128)(2,1)S(1)}, u32[]{:S(2)}, u32[]{:S(2)}) collective-permute-start(bf16[96,1024]{1,0:T(8,128)(2,1)S(1)} %pad_maximum_fusion.own_ref), channel_id=1, source_target_pairs={{0,6},{1,7},{2,4},{3,5},{4,2},{5,3},{6,0},{7,1},{8,14},{9,15},{10,... | collective-permute-start | bytes 589832 | tf_op jit(solution)/shard_map/ppermute | solution.py:246
  23.1 0.0 collective-permute-start
  23.1 1.4 %collective-permute-done.1.refs_2_ = bf16[8,96,128]{2,1,0:T(8,128)(2,1)S(1)} collective-permute-done((bf16[8,96,128]{2,1,0:T(8,128)(2,1)S(1)}, bf16[8,96,128]{2,1,0:T(8,128)(2,1)S(1)}, u32[]{:S(2)}, u32[]{:S(2)}) %collective-permute-start.1) | collective-permute-done | bytes 196640 | tf_op jit(solution)/shard_map/ppermute | solution.py:272
  24.5 0.0 collective-permute-start.2
  24.5 1.1 %collective-permute-start.3 = (bf16[96,1024]{1,0:T(8,128)(2,1)S(1)}, bf16[96,1024]{1,0:T(8,128)(2,1)S(1)}, u32[]{:S(2)}, u32[]{:S(2)}) collective-permute-start(bf16[96,1024]{1,0:T(8,128)(2,1)S(1)} %pad_maximum_fusion.own_ref), channel_id=1, source_target_pairs={{0,1},{1,0},{2,3},{3,2},{4,5},{5,4},{6,7},{7,6},{8,9},{9,8},{10,11... | collective-permute-start | bytes 589832 | tf_op jit(solution)/shard_map/ppermute | solution.py:246
  25.5 8.9 %collective-permute-done.6.refs_3_ = bf16[96,1024]{1,0:T(8,128)(2,1)S(1)} collective-permute-done((bf16[96,1024]{1,0:T(8,128)(2,1)S(1)}, bf16[96,1024]{1,0:T(8,128)(2,1)S(1)}, u32[]{:S(2)}, u32[]{:S(2)}) %collective-permute-start.6) | collective-permute-done | bytes 196640 | tf_op jit(solution)/shard_map/ppermute | solution.py:246
  34.4 0.0 collective-permute-start.4
  34.4 0.0 collective-permute-done.8.refs_5_
  34.4 4.3 %collective-permute-start.5 = (bf16[96,1024]{1,0:T(8,128)(2,1)S(1)}, bf16[96,1024]{1,0:T(8,128)(2,1)S(1)}, u32[]{:S(2)}, u32[]{:S(2)}) collective-permute-start(bf16[96,1024]{1,0:T(8,128)(2,1)S(1)} %pad_maximum_fusion.own_ref), channel_id=1, source_target_pairs={{0,3},{1,2},{2,1},{3,0},{4,7},{5,6},{6,5},{7,4},{8,11},{9,10},{10,... | collective-permute-start | bytes 589832 | tf_op jit(solution)/shard_map/ppermute | solution.py:246
  38.8 0.0 collective-permute-done.refs_1_
  38.8 1.8 %collective-permute-start.7 = (bf16[96,1024]{1,0:T(8,128)(2,1)S(1)}, bf16[96,1024]{1,0:T(8,128)(2,1)S(1)}, u32[]{:S(2)}, u32[]{:S(2)}) collective-permute-start(bf16[96,1024]{1,0:T(8,128)(2,1)S(1)} %collective-permute-done.6.refs_3_), channel_id=1, source_target_pairs={{0,1},{1,0},{2,3},{3,2},{4,5},{5,4},{6,7},{7,6},{8,9},{9,8},{10,11... | collective-permute-start | bytes 589832 | tf_op jit(solution)/shard_map/ppermute | solution.py:246
  40.6 0.0 collective-permute-done.2.refs_3_
  40.6 0.2 collective-permute-start.9
  40.8 0.0 copy-done.6
  40.8 0.0 copy-done.8
  40.8 0.0 copy-start.1
  40.8 0.0 copy-start.7
  40.8 7.8 %tree.1.part_ref = f32[32,1024]{1,0:T(8,128)S(1)} custom-call(s32[2,16]{1,0:T(2,128)S(1)} %copy-done.8, s32[31,128]{1,0:T(8,128)S(1)} %copy-done.6, bf16[1024,80]{1,0:T(8,128)(2,1)S(1)} %get-tuple-element.9.left_ref, bf16[96,1024]{1,0:T(8,128)(2,1)S(1)} %pad_maximum_fusion.own_ref, bf16[8,96,128]{2,1,0:T(8,128)(2,1)S(1)} %all_to_all.10.refs_0_, ...), custom_call_target="tpu_custom_call" | custom-call | tf_op jit(solution)/shard_map/tree/pallas_call | solution.py:275
  48.6 0.0 collective-permute-done.3.refs_0_
  48.6 0.0 collective-permute-done.4.refs_1_
  48.7 0.0 collective-permute-done.5.refs_2_
  48.7 0.1 collective-permute-done.7.refs_4_
  48.8 3.7 %collective-permute-done.9.refs_6_ = bf16[96,1024]{1,0:T(8,128)(2,1)S(1)} collective-permute-done((bf16[96,1024]{1,0:T(8,128)(2,1)S(1)}, bf16[96,1024]{1,0:T(8,128)(2,1)S(1)}, u32[]{:S(2)}, u32[]{:S(2)}) %collective-permute-start.9) | collective-permute-done | bytes 196640 | tf_op jit(solution)/shard_map/ppermute | solution.py:246
  52.4 0.0 copy-done.1
  52.4 0.0 copy-done.7
  52.4 5.8 %near.1 = (f32[32,1024]{1,0:T(8,128)}, f32[32,16,128]{2,1,0:T(8,128)S(1)}) custom-call(s32[2,4]{1,0:T(2,128)S(1)} %copy-done.7, bf16[1024,80]{1,0:T(8,128)(2,1)S(1)} %get-tuple-element.9.left_ref, f32[32,1024]{1,0:T(8,128)S(1)} %tree.1.part_ref, f32[32,1024]{1,0:T(8,128)S(1)} %bitcast.8, bf16[96,1024]{1,0:T(8,128)(2,1)S(1)} %collective-permute-done.3.refs_0_, ...), custom_call_target="tpu_custom_call" | custom-call | tf_op jit(solution)/shard_map/near/pallas_call | solution.py:287
  58.2 0.0 copy-start.4
  58.2 0.0 copy-start.5
  58.2 15.2 %all_to_all.11.small_ref = f32[32,16,128]{2,1,0:T(8,128)S(1)} all-to-all(f32[32,16,128]{2,1,0:T(8,128)S(1)} %get-tuple-element.11), channel_id=1, replica_groups=mesh['gx'=4,'gy'=8] {'gx','gy'}, dimensions={0} | all-to-all | bytes 524288 | tf_op jit(solution)/shard_map/all_to_all | solution.py:306
  73.4 0.0 copy-done.4
  73.4 0.0 copy-done.5
  73.4 4.4 %solve.1 = (f32[32,1024]{1,0:T(8,128)}, f32[32,1024]{1,0:T(8,128)}) custom-call(f32[32,16,128]{2,1,0:T(8,128)S(1)} %all_to_all.11.small_ref, f32[32,1024]{1,0:T(8,128)S(1)} %bitcast.12, f32[32,1024]{1,0:T(8,128)S(1)} %bitcast.9, f32[32,1024]{1,0:T(8,128)S(1)} %copy-done.5), custom_call_target="tpu_custom_call" | custom-call | tf_op jit(solution)/shard_map/solve/pallas_call | solution.py:307
  (2 shorter events, 0.0 us)
Async XLA Ops:
  0.6 0.7 copy-start.9
  1.3 0.9 %copy-start = (f32[1024,32]{0,1:T(8,128)S(1)}, f32[1024,32]{0,1:T(8,128)}, u32[]{:S(2)}) copy-start(f32[1024,32]{0,1:T(8,128)} %param.9) | copy-start | bytes 393220
  2.2 0.9 %copy-start.2 = (bf16[1024,64]{0,1:T(8,128)(2,1)S(1)}, bf16[1024,64]{0,1:T(8,128)(2,1)}, u32[]{:S(2)}) copy-start(bf16[1024,64]{0,1:T(8,128)(2,1)} %param.7) | copy-start | bytes 393220
  18.8 1.5 %copy-start.3 = (bf16[1024,64]{0,1:T(8,128)(2,1)S(1)}, bf16[1024,64]{0,1:T(8,128)(2,1)}, u32[]{:S(2)}) copy-start(bf16[1024,64]{0,1:T(8,128)(2,1)} %param.7) | copy-start | bytes 393220
  18.8 5.7 %collective-permute-start.1 = (bf16[8,96,128]{2,1,0:T(8,128)(2,1)S(1)}, bf16[8,96,128]{2,1,0:T(8,128)(2,1)S(1)}, u32[]{:S(2)}, u32[]{:S(2)}) collective-permute-start(bf16[8,96,128]{2,1,0:T(8,128)(2,1)S(1)} %all_to_all.10.refs_0_), channel_id=1, source_target_pairs={{0,16},{8,24},{16,0},{24,8},{1,17},{9,25},{17,1},{25,9},{2,18},{10... | collective-permute-start | bytes 589832 | tf_op jit(solution)/shard_map/ppermute | solution.py:272
  20.3 20.5 %copy-start.6 = (s32[31,128]{1,0:T(8,128)S(1)}, s32[31,128]{1,0:T(8,128)}, u32[]{:S(2)}) copy-start(s32[31,128]{1,0:T(8,128)} %upper_ref.1) | copy-start | bytes 47620
  20.4 20.5 %copy-start.8 = (s32[2,16]{1,0:T(2,128)S(1)}, s32[2,16]{1,0:T(2,128)}, u32[]{:S(2)}) copy-start(s32[2,16]{1,0:T(2,128)} %far_ref.1) | copy-start | bytes 388
  20.4 14.1 %collective-permute-start.6 = (bf16[96,1024]{1,0:T(8,128)(2,1)S(1)}, bf16[96,1024]{1,0:T(8,128)(2,1)S(1)}, u32[]{:S(2)}, u32[]{:S(2)}) collective-permute-start(bf16[96,1024]{1,0:T(8,128)(2,1)S(1)} %pad_maximum_fusion.own_ref), channel_id=1, source_target_pairs={{0,4},{1,5},{2,6},{3,7},{4,0},{5,1},{6,2},{7,3},{8,12},{9,13},{10,... | collective-permute-start | bytes 589832 | tf_op jit(solution)/shard_map/ppermute | solution.py:246
  21.1 13.3 %collective-permute-start.8 = (bf16[96,1024]{1,0:T(8,128)(2,1)S(1)}, bf16[96,1024]{1,0:T(8,128)(2,1)S(1)}, u32[]{:S(2)}, u32[]{:S(2)}) collective-permute-start(bf16[96,1024]{1,0:T(8,128)(2,1)S(1)} %pad_maximum_fusion.own_ref), channel_id=1, source_target_pairs={{0,6},{1,7},{2,4},{3,5},{4,2},{5,3},{6,0},{7,1},{8,14},{9,15},{10,... | collective-permute-start | bytes 589832 | tf_op jit(solution)/shard_map/ppermute | solution.py:246
  23.1 15.7 %collective-permute-start = (bf16[8,96,128]{2,1,0:T(8,128)(2,1)S(1)}, bf16[8,96,128]{2,1,0:T(8,128)(2,1)S(1)}, u32[]{:S(2)}, u32[]{:S(2)}) collective-permute-start(bf16[8,96,128]{2,1,0:T(8,128)(2,1)S(1)} %all_to_all.10.refs_0_), channel_id=1, source_target_pairs={{0,8},{8,0},{16,24},{24,16},{1,9},{9,1},{17,25},{25,17},{2,10},{10... | collective-permute-start | bytes 589832 | tf_op jit(solution)/shard_map/ppermute | solution.py:272
  24.5 16.1 %collective-permute-start.2 = (bf16[8,96,128]{2,1,0:T(8,128)(2,1)S(1)}, bf16[8,96,128]{2,1,0:T(8,128)(2,1)S(1)}, u32[]{:S(2)}, u32[]{:S(2)}) collective-permute-start(bf16[8,96,128]{2,1,0:T(8,128)(2,1)S(1)} %collective-permute-done.1.refs_2_), channel_id=1, source_target_pairs={{0,8},{8,0},{16,24},{24,16},{1,9},{9,1},{17,25},{25,17},{2,10},{10... | collective-permute-start | bytes 589832 | tf_op jit(solution)/shard_map/ppermute | solution.py:272
  24.5 24.2 %collective-permute-start.3 = (bf16[96,1024]{1,0:T(8,128)(2,1)S(1)}, bf16[96,1024]{1,0:T(8,128)(2,1)S(1)}, u32[]{:S(2)}, u32[]{:S(2)}) collective-permute-start(bf16[96,1024]{1,0:T(8,128)(2,1)S(1)} %pad_maximum_fusion.own_ref), channel_id=1, source_target_pairs={{0,1},{1,0},{2,3},{3,2},{4,5},{5,4},{6,7},{7,6},{8,9},{9,8},{10,11... | collective-permute-start | bytes 589832 | tf_op jit(solution)/shard_map/ppermute | solution.py:246
  34.4 14.2 %collective-permute-start.4 = (bf16[96,1024]{1,0:T(8,128)(2,1)S(1)}, bf16[96,1024]{1,0:T(8,128)(2,1)S(1)}, u32[]{:S(2)}, u32[]{:S(2)}) collective-permute-start(bf16[96,1024]{1,0:T(8,128)(2,1)S(1)} %pad_maximum_fusion.own_ref), channel_id=1, source_target_pairs={{0,2},{1,3},{2,0},{3,1},{4,6},{5,7},{6,4},{7,5},{8,10},{9,11},{10,... | collective-permute-start | bytes 589832 | tf_op jit(solution)/shard_map/ppermute | solution.py:246
  34.4 14.2 %collective-permute-start.5 = (bf16[96,1024]{1,0:T(8,128)(2,1)S(1)}, bf16[96,1024]{1,0:T(8,128)(2,1)S(1)}, u32[]{:S(2)}, u32[]{:S(2)}) collective-permute-start(bf16[96,1024]{1,0:T(8,128)(2,1)S(1)} %pad_maximum_fusion.own_ref), channel_id=1, source_target_pairs={{0,3},{1,2},{2,1},{3,0},{4,7},{5,6},{6,5},{7,4},{8,11},{9,10},{10,... | collective-permute-start | bytes 589832 | tf_op jit(solution)/shard_map/ppermute | solution.py:246
  38.8 10.0 %collective-permute-start.7 = (bf16[96,1024]{1,0:T(8,128)(2,1)S(1)}, bf16[96,1024]{1,0:T(8,128)(2,1)S(1)}, u32[]{:S(2)}, u32[]{:S(2)}) collective-permute-start(bf16[96,1024]{1,0:T(8,128)(2,1)S(1)} %collective-permute-done.6.refs_3_), channel_id=1, source_target_pairs={{0,1},{1,0},{2,3},{3,2},{4,5},{5,4},{6,7},{7,6},{8,9},{9,8},{10,11... | collective-permute-start | bytes 589832 | tf_op jit(solution)/shard_map/ppermute | solution.py:246
  40.6 11.8 %collective-permute-start.9 = (bf16[96,1024]{1,0:T(8,128)(2,1)S(1)}, bf16[96,1024]{1,0:T(8,128)(2,1)S(1)}, u32[]{:S(2)}, u32[]{:S(2)}) collective-permute-start(bf16[96,1024]{1,0:T(8,128)(2,1)S(1)} %collective-permute-done.8.refs_5_), channel_id=1, source_target_pairs={{0,1},{1,0},{2,3},{3,2},{4,5},{5,4},{6,7},{7,6},{8,9},{9,8},{10,11... | collective-permute-start | bytes 589832 | tf_op jit(solution)/shard_map/ppermute | solution.py:246
  40.8 11.6 %copy-start.1 = (f32[1024,32]{0,1:T(8,128)S(1)}, f32[1024,32]{0,1:T(8,128)}, u32[]{:S(2)}) copy-start(f32[1024,32]{0,1:T(8,128)} %param.9) | copy-start | bytes 393220
  40.8 11.6 %copy-start.7 = (s32[2,4]{1,0:T(2,128)S(1)}, s32[2,4]{1,0:T(2,128)}, u32[]{:S(2)}) copy-start(s32[2,4]{1,0:T(2,128)} %near_ref.1) | copy-start | bytes 100
  58.2 15.2 %copy-start.4 = (f32[1024,32]{0,1:T(8,128)S(1)}, f32[1024,32]{0,1:T(8,128)}, u32[]{:S(2)}) copy-start(f32[1024,32]{0,1:T(8,128)} %param.8) | copy-start | bytes 393220
  58.2 15.2 %copy-start.5 = (f32[32,1024]{1,0:T(8,128)S(1)}, f32[32,1024]{1,0:T(8,128)}, u32[]{:S(2)}) copy-start(f32[32,1024]{1,0:T(8,128)} %get-tuple-element.12.image_ref) | copy-start | bytes 393220

commit v2 on v1

--- a/solution.py
+++ b/solution.py
@@ -58,7 +58,17 @@
     return jnp.exp2(distance * (-0.5 * math.log2(math.e) / depth))
 
 
-def skeleton_body(pick_ref, points_ref, residual_ref, block_ref, left_ref):
+def fields(sources, right, depth):
+    left = [left_block(source[:depth]) for source in sources]
+    tiles = [kernel_of(block, right, depth).astype(BF) for block in left]
+    sums = [
+        jnp.dot(source[depth:], tile, preferred_element_type=F32)
+        for source, tile in zip(sources, tiles)
+    ]
+    return sum(sums[1:], sums[0])
+
+
+def skeleton_body(pick_ref, points_ref, residual_ref, block_ref, right_ref):
     depth, count = points_ref.shape
     rank = pick_ref.shape[1]
     points = points_ref[...]
@@ -72,7 +82,7 @@
     block = jnp.concatenate([chosen, weights.astype(BF)], axis=0)
     for copy in range(block_ref.shape[0]):
         block_ref[copy] = block
-    left_ref[...] = left_block(points)
+    right_ref[...] = right
 
 
 def tree_nodes(depth, upper_ref, tree_ref, nodes):
@@ -100,8 +110,8 @@
         tree_ref[node] = block
 
 
-def tree_body(leaf_dev, depth, far_ref, upper_ref, left_ref, own_ref, *refs):
-    part_refs, out_ref, tree_ref, acc = refs[:-3], refs[-3], refs[-2], refs[-1]
+def tree_body(leaf_dev, depth, far_ref, upper_ref, right_ref, own_ref, *refs):
+    part_refs, out_ref, tree_ref = refs[:-2], refs[-2], refs[-1]
     row_total = len(part_refs)
     column_total = part_refs[0].shape[0]
     low = row_total * column_total - 1
@@ -128,33 +138,26 @@
         else:
             lax.fori_loop(0, count // size, level, 0)
 
-    leaf = left_ref.shape[0] // leaf_dev
+    leaf = right_ref.shape[1] // leaf_dev
     rank = tree_ref.shape[2]
     far = far_ref.shape[1]
+    each = leaf // rank
     for at in range(leaf_dev):
         where = slice(at * leaf, (at + 1) * leaf)
-        own = own_ref[:, where]
-        right = jnp.concatenate([own[:depth], right_extra(own[:depth])], axis=0)
-        tile = kernel_of(left_ref[where], right, depth).astype(BF)
-        acc[...] = lax.dot_general(tile, own[depth:], NT, preferred_element_type=F32) * (
-            rank / math.sqrt(leaf)
-        )
-
-        def step(group, carry, at=at, where=where):
-            nodes = [tree_ref[far_ref[at, 4 * group + k]] for k in range(4)]
-            both = jnp.concatenate(nodes, axis=1)
-            tile = kernel_of(left_ref[where], both[: depth + EXTRA], depth).astype(BF)
-            acc[...] += lax.dot_general(tile, both[depth + EXTRA :], NT, preferred_element_type=F32)
-            return carry
-
-        lax.fori_loop(0, far // 4, step, 0)
-        out_ref[:, where] = acc[...].T * (1.0 / rank)
-
-
-def near_body(leaf_dev, depth, near_ref, left_ref, part_ref, residual_ref, *refs):
-    block_refs = refs[:-5]
-    image_ref, small_ref, held, sems, acc = refs[-5:]
-    leaf = left_ref.shape[0] // leaf_dev
+        sources = []
+        for first in range(0, far, each):
+            both = jnp.concatenate([tree_ref[far_ref[at, first + k]] for k in range(each)], axis=1)
+            sources.append(jnp.concatenate([both[:depth], both[depth + EXTRA :]], axis=0))
+        right = right_ref[:, where]
+        out_ref[:, where] = fields(sources, right, depth) * (1.0 / rank) + fields(
+            [own_ref[:, where]], right, depth
+        ) * (1.0 / math.sqrt(leaf))
+
+
+def near_body(leaf_dev, depth, near_ref, right_ref, part_ref, residual_ref, *refs):
+    block_refs = refs[:-4]
+    image_ref, small_ref, held, sems = refs[-4:]
+    leaf = right_ref.shape[1] // leaf_dev
     near = near_ref.shape[1]
     mine = lax.axis_index("gy")
     columns = len(block_refs) + 1
@@ -171,25 +174,17 @@
                 pltpu.make_async_copy(source, held.at[request], sems.at[request]).start()
 
     for at in range(leaf_dev):
-        acc[...] = jnp.zeros_like(acc)
-
-        def step(place, carry, at=at):
-            request = at * near + place
+        requests = range(at * near, (at + 1) * near)
+        for request in requests:
             pltpu.make_async_copy(
                 block_refs[0].at[:, :leaf], held.at[request], sems.at[request]
             ).wait()
-            block = held[request]
-            right = jnp.concatenate([block[:depth], right_extra(block[:depth])], axis=0)
-            tile = kernel_of(left_ref[at * leaf : (at + 1) * leaf], right, depth).astype(BF)
-            acc[...] += lax.dot_general(tile, block[depth:], NT, preferred_element_type=F32)
-            return carry
-
-        lax.fori_loop(0, near, step, 0)
         where = slice(at * leaf, (at + 1) * leaf)
+        total = fields([held[request] for request in requests], right_ref[:, where], depth)
         image_ref[:, where] = (
             LAMBDA_RIDGE * residual_ref[:, where]
             + part_ref[:, where]
-            + acc[...].T * (1.0 / math.sqrt(leaf))
+            + total * (1.0 / math.sqrt(leaf))
         )
     image = image_ref[...]
     gram = lax.dot_general(image, image, NT, precision=FULL, preferred_element_type=F32)
@@ -211,16 +206,32 @@
         packed = packed + small_ref[at]
     gram = jnp.concatenate([packed[:, :order], packed[:, order : 2 * order]], axis=0)
     cross = jnp.concatenate([packed[:, 2 * order : 3 * order], packed[:, 3 * order :]], axis=0)
-    work = jnp.concatenate([gram, cross], axis=1)
     rows = lax.broadcasted_iota(jnp.int32, (order, 1), 0)
-    for column in range(order):
-        row = work[column : column + 1]
-        inverse = 1.0 / jnp.sqrt(row[:, column : column + 1])
-        factor = jnp.where(rows == column, 0.0, work[:, column : column + 1] * inverse)
-        work = work - factor * (row * inverse)
     eye = (rows == lax.broadcasted_iota(jnp.int32, (order, order), 1)).astype(F32)
-    diagonal = jnp.sum(work[:, :order] * eye, axis=1, keepdims=True)
-    coeffs = (work[:, order:] / diagonal).T
+    down = lax.rsqrt(jnp.sum(gram * eye, axis=1, keepdims=True))
+    across = lax.rsqrt(jnp.sum(gram * eye, axis=0, keepdims=True))
+    work = jnp.concatenate([gram * down * across, cross * down], axis=1)
+    inverses = []
+    for first in range(0, order, 2):
+        upper, lower = work[first : first + 1], work[first + 1 : first + 2]
+        a, b, c = upper[:, first : first + 1], upper[:, first + 1 : first + 2], lower[:, first + 1 : first + 2]
+        scale = 1.0 / (a * c - b * b)
+        inverse = (c * scale, -b * scale, a * scale)
+        inverses.append(inverse)
+        inside = (rows == first) | (rows == first + 1)
+        left = jnp.where(inside, 0.0, work[:, first : first + 1])
+        right = jnp.where(inside, 0.0, work[:, first + 1 : first + 2])
+        work = (
+            work
+            - (left * inverse[0] + right * inverse[1]) * upper
+            - (left * inverse[1] + right * inverse[2]) * lower
+        )
+    found = []
+    for first, inverse in zip(range(0, order, 2), inverses):
+        upper, lower = work[first : first + 1, order:], work[first + 1 : first + 2, order:]
+        found.append(inverse[0] * upper + inverse[1] * lower)
+        found.append(inverse[1] * upper + inverse[2] * lower)
+    coeffs = (jnp.concatenate(found, axis=0) * down).T
     solution_out[...] = solution_ref[...] + jnp.dot(coeffs, residual_ref[...], precision=FULL, preferred_element_type=F32)
     residual_out[...] = residual_ref[...] - jnp.dot(coeffs, image_ref[...], precision=FULL, preferred_element_type=F32)
 
@@ -253,11 +264,11 @@
             near_blocks[step + 1] = send(1, near_blocks[step])
     deep = depth + EXTRA
 
-    blocks, left = pl.pallas_call(
+    blocks, right = pl.pallas_call(
         skeleton_body,
         out_shape=(
             jax.ShapeDtypeStruct((column_total, depth + width, rank), BF),
-            jax.ShapeDtypeStruct((count, deep), BF),
+            jax.ShapeDtypeStruct((deep, count), BF),
         ),
         in_specs=vmem(3),
         out_specs=tuple(vmem(2)),
@@ -279,11 +290,10 @@
         out_specs=vmem(1)[0],
         scratch_shapes=[
             pltpu.VMEM((2 * device_total - 1, deep + width, rank), BF),
-            pltpu.VMEM((leaf, width), F32),
         ],
         compiler_params=pltpu.CompilerParams(vmem_limit_bytes=GRANT),
     name="tree",
-    )(far_nodes, upper_skeleton, left, near_block, *parts)
+    )(far_nodes, upper_skeleton, right, near_block, *parts)
     image_t, small = pl.pallas_call(
         functools.partial(near_body, leaf_dev, depth),
         out_shape=(
@@ -298,11 +308,10 @@
         scratch_shapes=[
             pltpu.VMEM((leaf_dev * near, depth + width, leaf), BF),
             pltpu.SemaphoreType.DMA((leaf_dev * near,)),
-            pltpu.VMEM((leaf, width), F32),
         ],
         compiler_params=pltpu.CompilerParams(vmem_limit_bytes=GRANT),
         name="near",
-    )(near_leaves, left, partial_t, residual_t, *[near_blocks[step] for step in range(1, column_total)])
+    )(near_leaves, right, partial_t, residual_t, *[near_blocks[step] for step in range(1, column_total)])
     small = lax.all_to_all(small, ("gx", "gy"), 0, 0)
     solution_next, residual_next = pl.pallas_call(
         solve_body,

time: 78.1 us -> 77.9 us (level)
  waiting for transfers between devices: 14 us -> 15.5 us
  Pallas kernels: 18.6 us -> 17.5 us
    pallas_call x1, Pallas kernels: 4.43 us -> 6.19 us  [step_of(): pl.pallas_call(solve_body, out_shape=(jax.ShapeDtypeStruct((width, count)...]
    pallas_call x1, Pallas kernels: 7.8 us -> 6.28 us  [step_of(): pl.pallas_call(functools.partial(tree_body, leaf_dev, depth), out_shape=j...]
    ppermute x7, waiting for transfers between devices: 12.7 us -> 14.2 us  [send(): lax.ppermute(block, 'gy', [(i, i ^ step) for i in range(column_total)])]
    pallas_call x1, Pallas kernels: 5.75 us -> 4.4 us  [step_of(): pl.pallas_call(functools.partial(near_body, leaf_dev, depth), out_shape=(...]
    unnamed x20 -> x18, local copies, waits for them, and re-layouts: 2.49 us -> 2.49 us
  transfers between devices with their start and end apart: 10 -> 10, of which waited for: 4 -> 4; matrix products, arithmetic and copies ran while one was open for 0% -> 0% of each run, Pallas kernels for 10% -> 8%
where the time goes in v2:
time: 77.9 us; the launch traced here: 77.6 us
  blocking collectives  29.7 us (38%)
  Pallas kernels  17.5 us (22%)
  waiting for transfers between devices  15.5 us (20%)
  starting transfers between devices  11.7 us (15%)
  local copies, waits for them, and re-layouts  2.49 us (3%)
    all_to_all x1, blocking collectives, step_of(): mine = lax.all_to_all(blocks, 'gy', 0, 0)  15.1 us
    all_to_all x1, blocking collectives, step_of(): small = lax.all_to_all(small, ('gx', 'gy'), 0, 0)  14.6 us
    ppermute x7, waiting for transfers between devices, send(): lax.ppermute(block, 'gy', [(i, i ^ step) for i in range(column_total)])  14.2 us
    ppermute x7, starting transfers between devices, send(): lax.ppermute(block, 'gy', [(i, i ^ step) for i in range(column_total)])  10.2 us
    pallas_call x1, Pallas kernels, step_of(): pl.pallas_call(functools.partial(tree_body, leaf_dev, depth), out_shape=j...  6.28 us
    pallas_call x1, Pallas kernels, step_of(): pl.pallas_call(solve_body, out_shape=(jax.ShapeDtypeStruct((width, count)...  6.19 us
    pallas_call x1, Pallas kernels, step_of(): pl.pallas_call(functools.partial(near_body, leaf_dev, depth), out_shape=(...  4.4 us
    unnamed x18, local copies, waits for them, and re-layouts  2.49 us
  transfers between devices with their start and end apart: 10, of which 4 were waited for; matrix products, arithmetic and copies ran while one was open for 0% of the time, Pallas kernels for 8%

profile of v2, /device:TPU:0, one launch (start us, length us, event | category | flops | bytes accessed | tf_op | source)
XLA Modules:
  0.0 77.6 jit_solution(2963508625801657231)
XLA Ops:
  0.6 0.0 copy-start.8
  0.6 0.6 copy-done.8
  1.3 0.0 copy-start
  1.3 0.9 %copy-done = f32[1024,32]{0,1:T(8,128)S(1)} copy-done((f32[1024,32]{0,1:T(8,128)S(1)}, f32[1024,32]{0,1:T(8,128)}, u32[]{:S(2)}) %copy-start) | copy-done | bytes 131096
  2.2 0.0 copy-start.2
  2.2 0.9 %copy-done.2 = bf16[1024,64]{0,1:T(8,128)(2,1)S(1)} copy-done((bf16[1024,64]{0,1:T(8,128)(2,1)S(1)}, bf16[1024,64]{0,1:T(8,128)(2,1)}, u32[]{:S(2)}) %copy-start.2) | copy-done | bytes 131096
  3.1 0.6 skeleton.1
  3.7 15.1 %all_to_all.10.refs_0_ = bf16[8,96,128]{2,1,0:T(8,128)(2,1)S(1)} all-to-all(bf16[8,96,128]{2,1,0:T(8,128)(2,1)S(1)} %get-tuple-element.10), channel_id=1, replica_groups=mesh['gx'=4,'gy'=8] {'gy'}, dimensions={0} | all-to-all | bytes 393216 | tf_op jit(solution)/shard_map/all_to_all | solution.py:278
  18.8 1.5 %collective-permute-start.1 = (bf16[8,96,128]{2,1,0:T(8,128)(2,1)S(1)}, bf16[8,96,128]{2,1,0:T(8,128)(2,1)S(1)}, u32[]{:S(2)}, u32[]{:S(2)}) collective-permute-start(bf16[8,96,128]{2,1,0:T(8,128)(2,1)S(1)} %all_to_all.10.refs_0_), channel_id=1, source_target_pairs={{0,16},{8,24},{16,0},{24,8},{1,17},{9,25},{17,1},{25,9},{2,18},{10... | collective-permute-start | bytes 589832 | tf_op jit(solution)/shard_map/ppermute | solution.py:283
  20.3 0.0 copy-start.5
  20.3 0.0 copy-start.7
  20.4 0.8 %collective-permute-start.6 = (bf16[96,1024]{1,0:T(8,128)(2,1)S(1)}, bf16[96,1024]{1,0:T(8,128)(2,1)S(1)}, u32[]{:S(2)}, u32[]{:S(2)}) collective-permute-start(bf16[96,1024]{1,0:T(8,128)(2,1)S(1)} %pad_maximum_fusion.own_ref), channel_id=1, source_target_pairs={{0,4},{1,5},{2,6},{3,7},{4,0},{5,1},{6,2},{7,3},{8,12},{9,13},{10,... | collective-permute-start | bytes 589832 | tf_op jit(solution)/shard_map/ppermute | solution.py:257
  21.1 1.9 %collective-permute-start.8 = (bf16[96,1024]{1,0:T(8,128)(2,1)S(1)}, bf16[96,1024]{1,0:T(8,128)(2,1)S(1)}, u32[]{:S(2)}, u32[]{:S(2)}) collective-permute-start(bf16[96,1024]{1,0:T(8,128)(2,1)S(1)} %pad_maximum_fusion.own_ref), channel_id=1, source_target_pairs={{0,6},{1,7},{2,4},{3,5},{4,2},{5,3},{6,0},{7,1},{8,14},{9,15},{10,... | collective-permute-start | bytes 589832 | tf_op jit(solution)/shard_map/ppermute | solution.py:257
  23.1 0.0 collective-permute-start
  23.1 1.4 %collective-permute-done.1.refs_2_ = bf16[8,96,128]{2,1,0:T(8,128)(2,1)S(1)} collective-permute-done((bf16[8,96,128]{2,1,0:T(8,128)(2,1)S(1)}, bf16[8,96,128]{2,1,0:T(8,128)(2,1)S(1)}, u32[]{:S(2)}, u32[]{:S(2)}) %collective-permute-start.1) | collective-permute-done | bytes 196640 | tf_op jit(solution)/shard_map/ppermute | solution.py:283
  24.4 0.0 collective-permute-start.2
  24.4 1.1 %collective-permute-start.3 = (bf16[96,1024]{1,0:T(8,128)(2,1)S(1)}, bf16[96,1024]{1,0:T(8,128)(2,1)S(1)}, u32[]{:S(2)}, u32[]{:S(2)}) collective-permute-start(bf16[96,1024]{1,0:T(8,128)(2,1)S(1)} %pad_maximum_fusion.own_ref), channel_id=1, source_target_pairs={{0,1},{1,0},{2,3},{3,2},{4,5},{5,4},{6,7},{7,6},{8,9},{9,8},{10,11... | collective-permute-start | bytes 589832 | tf_op jit(solution)/shard_map/ppermute | solution.py:257
  25.5 8.9 %collective-permute-done.6.refs_3_ = bf16[96,1024]{1,0:T(8,128)(2,1)S(1)} collective-permute-done((bf16[96,1024]{1,0:T(8,128)(2,1)S(1)}, bf16[96,1024]{1,0:T(8,128)(2,1)S(1)}, u32[]{:S(2)}, u32[]{:S(2)}) %collective-permute-start.6) | collective-permute-done | bytes 196640 | tf_op jit(solution)/shard_map/ppermute | solution.py:257
  34.4 0.0 collective-permute-start.4
  34.4 0.0 collective-permute-done.8.refs_5_
  34.4 4.3 %collective-permute-start.5 = (bf16[96,1024]{1,0:T(8,128)(2,1)S(1)}, bf16[96,1024]{1,0:T(8,128)(2,1)S(1)}, u32[]{:S(2)}, u32[]{:S(2)}) collective-permute-start(bf16[96,1024]{1,0:T(8,128)(2,1)S(1)} %pad_maximum_fusion.own_ref), channel_id=1, source_target_pairs={{0,3},{1,2},{2,1},{3,0},{4,7},{5,6},{6,5},{7,4},{8,11},{9,10},{10,... | collective-permute-start | bytes 589832 | tf_op jit(solution)/shard_map/ppermute | solution.py:257
  38.8 0.0 collective-permute-done.refs_1_
  38.8 1.8 %collective-permute-start.7 = (bf16[96,1024]{1,0:T(8,128)(2,1)S(1)}, bf16[96,1024]{1,0:T(8,128)(2,1)S(1)}, u32[]{:S(2)}, u32[]{:S(2)}) collective-permute-start(bf16[96,1024]{1,0:T(8,128)(2,1)S(1)} %collective-permute-done.6.refs_3_), channel_id=1, source_target_pairs={{0,1},{1,0},{2,3},{3,2},{4,5},{5,4},{6,7},{7,6},{8,9},{9,8},{10,11... | collective-permute-start | bytes 589832 | tf_op jit(solution)/shard_map/ppermute | solution.py:257
  40.6 0.0 collective-permute-done.2.refs_3_
  40.6 0.2 collective-permute-start.9
  40.8 0.0 copy-done.5
  40.8 0.0 copy-done.7
  40.8 0.0 copy-start.1
  40.8 0.0 copy-start.6
  40.8 6.3 %tree.1.part_ref = f32[32,1024]{1,0:T(8,128)S(1)} custom-call(s32[2,16]{1,0:T(2,128)S(1)} %copy-done.7, s32[31,128]{1,0:T(8,128)S(1)} %copy-done.5, bf16[80,1024]{1,0:T(8,128)(2,1)S(1)} %get-tuple-element.9.right_ref, bf16[96,1024]{1,0:T(8,128)(2,1)S(1)} %pad_maximum_fusion.own_ref, bf16[8,96,128]{2,1,0:T(8,128)(2,1)S(1)} %all_to_all.10.refs_0_, ...), custom_call_target="tpu_custom_call" | custom-call | tf_op jit(solution)/shard_map/tree/pallas_call | solution.py:286
  47.1 0.0 collective-permute-done.3.refs_0_
  47.1 0.0 collective-permute-done.4.refs_1_
  47.1 0.0 collective-permute-done.5.refs_2_
  47.1 1.6 %collective-permute-done.7.refs_4_ = bf16[96,1024]{1,0:T(8,128)(2,1)S(1)} collective-permute-done((bf16[96,1024]{1,0:T(8,128)(2,1)S(1)}, bf16[96,1024]{1,0:T(8,128)(2,1)S(1)}, u32[]{:S(2)}, u32[]{:S(2)}) %collective-permute-start.7) | collective-permute-done | bytes 196640 | tf_op jit(solution)/shard_map/ppermute | solution.py:257
  48.7 3.7 %collective-permute-done.9.refs_6_ = bf16[96,1024]{1,0:T(8,128)(2,1)S(1)} collective-permute-done((bf16[96,1024]{1,0:T(8,128)(2,1)S(1)}, bf16[96,1024]{1,0:T(8,128)(2,1)S(1)}, u32[]{:S(2)}, u32[]{:S(2)}) %collective-permute-start.9) | collective-permute-done | bytes 196640 | tf_op jit(solution)/shard_map/ppermute | solution.py:257
  52.4 0.0 copy-done.1
  52.4 0.0 copy-done.6
  52.4 4.4 %near.1 = (f32[32,1024]{1,0:T(8,128)}, f32[32,16,128]{2,1,0:T(8,128)S(1)}) custom-call(s32[2,4]{1,0:T(2,128)S(1)} %copy-done.6, bf16[80,1024]{1,0:T(8,128)(2,1)S(1)} %get-tuple-element.9.right_ref, f32[32,1024]{1,0:T(8,128)S(1)} %tree.1.part_ref, f32[32,1024]{1,0:T(8,128)S(1)} %bitcast.8, bf16[96,1024]{1,0:T(8,128)(2,1)S(1)} %collective-permute-done.3.refs_0_, ...), custom_call_target="tpu_custom_call" | custom-call | tf_op jit(solution)/shard_map/near/pallas_call | solution.py:297
  56.8 0.0 copy-start.3
  56.8 0.0 copy-start.4
  56.8 14.6 %all_to_all.11.small_ref = f32[32,16,128]{2,1,0:T(8,128)S(1)} all-to-all(f32[32,16,128]{2,1,0:T(8,128)S(1)} %get-tuple-element.11), channel_id=1, replica_groups=mesh['gx'=4,'gy'=8] {'gx','gy'}, dimensions={0} | all-to-all | bytes 524288 | tf_op jit(solution)/shard_map/all_to_all | solution.py:315
  71.4 0.0 copy-done.3
  71.5 0.0 copy-done.4
  71.5 6.2 %solve.1 = (f32[32,1024]{1,0:T(8,128)}, f32[32,1024]{1,0:T(8,128)}) custom-call(f32[32,16,128]{2,1,0:T(8,128)S(1)} %all_to_all.11.small_ref, f32[32,1024]{1,0:T(8,128)S(1)} %bitcast.12, f32[32,1024]{1,0:T(8,128)S(1)} %bitcast.9, f32[32,1024]{1,0:T(8,128)S(1)} %copy-done.4), custom_call_target="tpu_custom_call" | custom-call | tf_op jit(solution)/shard_map/solve/pallas_call | solution.py:316
  (2 shorter events, 0.0 us)
Async XLA Ops:
  0.6 0.7 copy-start.8
  1.3 0.9 %copy-start = (f32[1024,32]{0,1:T(8,128)S(1)}, f32[1024,32]{0,1:T(8,128)}, u32[]{:S(2)}) copy-start(f32[1024,32]{0,1:T(8,128)} %param.9) | copy-start | bytes 393220
  2.2 0.9 %copy-start.2 = (bf16[1024,64]{0,1:T(8,128)(2,1)S(1)}, bf16[1024,64]{0,1:T(8,128)(2,1)}, u32[]{:S(2)}) copy-start(bf16[1024,64]{0,1:T(8,128)(2,1)} %param.7) | copy-start | bytes 393220
  18.8 5.7 %collective-permute-start.1 = (bf16[8,96,128]{2,1,0:T(8,128)(2,1)S(1)}, bf16[8,96,128]{2,1,0:T(8,128)(2,1)S(1)}, u32[]{:S(2)}, u32[]{:S(2)}) collective-permute-start(bf16[8,96,128]{2,1,0:T(8,128)(2,1)S(1)} %all_to_all.10.refs_0_), channel_id=1, source_target_pairs={{0,16},{8,24},{16,0},{24,8},{1,17},{9,25},{17,1},{25,9},{2,18},{10... | collective-permute-start | bytes 589832 | tf_op jit(solution)/shard_map/ppermute | solution.py:283
  20.3 20.5 %copy-start.5 = (s32[31,128]{1,0:T(8,128)S(1)}, s32[31,128]{1,0:T(8,128)}, u32[]{:S(2)}) copy-start(s32[31,128]{1,0:T(8,128)} %upper_ref.1) | copy-start | bytes 47620
  20.3 20.5 %copy-start.7 = (s32[2,16]{1,0:T(2,128)S(1)}, s32[2,16]{1,0:T(2,128)}, u32[]{:S(2)}) copy-start(s32[2,16]{1,0:T(2,128)} %far_ref.1) | copy-start | bytes 388
  20.4 14.1 %collective-permute-start.6 = (bf16[96,1024]{1,0:T(8,128)(2,1)S(1)}, bf16[96,1024]{1,0:T(8,128)(2,1)S(1)}, u32[]{:S(2)}, u32[]{:S(2)}) collective-permute-start(bf16[96,1024]{1,0:T(8,128)(2,1)S(1)} %pad_maximum_fusion.own_ref), channel_id=1, source_target_pairs={{0,4},{1,5},{2,6},{3,7},{4,0},{5,1},{6,2},{7,3},{8,12},{9,13},{10,... | collective-permute-start | bytes 589832 | tf_op jit(solution)/shard_map/ppermute | solution.py:257
  21.1 13.3 %collective-permute-start.8 = (bf16[96,1024]{1,0:T(8,128)(2,1)S(1)}, bf16[96,1024]{1,0:T(8,128)(2,1)S(1)}, u32[]{:S(2)}, u32[]{:S(2)}) collective-permute-start(bf16[96,1024]{1,0:T(8,128)(2,1)S(1)} %pad_maximum_fusion.own_ref), channel_id=1, source_target_pairs={{0,6},{1,7},{2,4},{3,5},{4,2},{5,3},{6,0},{7,1},{8,14},{9,15},{10,... | collective-permute-start | bytes 589832 | tf_op jit(solution)/shard_map/ppermute | solution.py:257
  23.1 15.7 %collective-permute-start = (bf16[8,96,128]{2,1,0:T(8,128)(2,1)S(1)}, bf16[8,96,128]{2,1,0:T(8,128)(2,1)S(1)}, u32[]{:S(2)}, u32[]{:S(2)}) collective-permute-start(bf16[8,96,128]{2,1,0:T(8,128)(2,1)S(1)} %all_to_all.10.refs_0_), channel_id=1, source_target_pairs={{0,8},{8,0},{16,24},{24,16},{1,9},{9,1},{17,25},{25,17},{2,10},{10... | collective-permute-start | bytes 589832 | tf_op jit(solution)/shard_map/ppermute | solution.py:283
  24.4 16.1 %collective-permute-start.2 = (bf16[8,96,128]{2,1,0:T(8,128)(2,1)S(1)}, bf16[8,96,128]{2,1,0:T(8,128)(2,1)S(1)}, u32[]{:S(2)}, u32[]{:S(2)}) collective-permute-start(bf16[8,96,128]{2,1,0:T(8,128)(2,1)S(1)} %collective-permute-done.1.refs_2_), channel_id=1, source_target_pairs={{0,8},{8,0},{16,24},{24,16},{1,9},{9,1},{17,25},{25,17},{2,10},{10... | collective-permute-start | bytes 589832 | tf_op jit(solution)/shard_map/ppermute | solution.py:283
  24.4 22.7 %collective-permute-start.3 = (bf16[96,1024]{1,0:T(8,128)(2,1)S(1)}, bf16[96,1024]{1,0:T(8,128)(2,1)S(1)}, u32[]{:S(2)}, u32[]{:S(2)}) collective-permute-start(bf16[96,1024]{1,0:T(8,128)(2,1)S(1)} %pad_maximum_fusion.own_ref), channel_id=1, source_target_pairs={{0,1},{1,0},{2,3},{3,2},{4,5},{5,4},{6,7},{7,6},{8,9},{9,8},{10,11... | collective-permute-start | bytes 589832 | tf_op jit(solution)/shard_map/ppermute | solution.py:257
  34.4 12.7 %collective-permute-start.4 = (bf16[96,1024]{1,0:T(8,128)(2,1)S(1)}, bf16[96,1024]{1,0:T(8,128)(2,1)S(1)}, u32[]{:S(2)}, u32[]{:S(2)}) collective-permute-start(bf16[96,1024]{1,0:T(8,128)(2,1)S(1)} %pad_maximum_fusion.own_ref), channel_id=1, source_target_pairs={{0,2},{1,3},{2,0},{3,1},{4,6},{5,7},{6,4},{7,5},{8,10},{9,11},{10,... | collective-permute-start | bytes 589832 | tf_op jit(solution)/shard_map/ppermute | solution.py:257
  34.4 12.7 %collective-permute-start.5 = (bf16[96,1024]{1,0:T(8,128)(2,1)S(1)}, bf16[96,1024]{1,0:T(8,128)(2,1)S(1)}, u32[]{:S(2)}, u32[]{:S(2)}) collective-permute-start(bf16[96,1024]{1,0:T(8,128)(2,1)S(1)} %pad_maximum_fusion.own_ref), channel_id=1, source_target_pairs={{0,3},{1,2},{2,1},{3,0},{4,7},{5,6},{6,5},{7,4},{8,11},{9,10},{10,... | collective-permute-start | bytes 589832 | tf_op jit(solution)/shard_map/ppermute | solution.py:257
  38.8 10.0 %collective-permute-start.7 = (bf16[96,1024]{1,0:T(8,128)(2,1)S(1)}, bf16[96,1024]{1,0:T(8,128)(2,1)S(1)}, u32[]{:S(2)}, u32[]{:S(2)}) collective-permute-start(bf16[96,1024]{1,0:T(8,128)(2,1)S(1)} %collective-permute-done.6.refs_3_), channel_id=1, source_target_pairs={{0,1},{1,0},{2,3},{3,2},{4,5},{5,4},{6,7},{7,6},{8,9},{9,8},{10,11... | collective-permute-start | bytes 589832 | tf_op jit(solution)/shard_map/ppermute | solution.py:257
  40.6 11.8 %collective-permute-start.9 = (bf16[96,1024]{1,0:T(8,128)(2,1)S(1)}, bf16[96,1024]{1,0:T(8,128)(2,1)S(1)}, u32[]{:S(2)}, u32[]{:S(2)}) collective-permute-start(bf16[96,1024]{1,0:T(8,128)(2,1)S(1)} %collective-permute-done.8.refs_5_), channel_id=1, source_target_pairs={{0,1},{1,0},{2,3},{3,2},{4,5},{5,4},{6,7},{7,6},{8,9},{9,8},{10,11... | collective-permute-start | bytes 589832 | tf_op jit(solution)/shard_map/ppermute | solution.py:257
  40.8 11.6 %copy-start.1 = (f32[1024,32]{0,1:T(8,128)S(1)}, f32[1024,32]{0,1:T(8,128)}, u32[]{:S(2)}) copy-start(f32[1024,32]{0,1:T(8,128)} %param.9) | copy-start | bytes 393220
  40.8 11.6 %copy-start.6 = (s32[2,4]{1,0:T(2,128)S(1)}, s32[2,4]{1,0:T(2,128)}, u32[]{:S(2)}) copy-start(s32[2,4]{1,0:T(2,128)} %near_ref.1) | copy-start | bytes 100
  56.8 14.6 %copy-start.3 = (f32[1024,32]{0,1:T(8,128)S(1)}, f32[1024,32]{0,1:T(8,128)}, u32[]{:S(2)}) copy-start(f32[1024,32]{0,1:T(8,128)} %param.8) | copy-start | bytes 393220
  56.8 14.6 %copy-start.4 = (f32[32,1024]{1,0:T(8,128)S(1)}, f32[32,1024]{1,0:T(8,128)}, u32[]{:S(2)}) copy-start(f32[32,1024]{1,0:T(8,128)} %get-tuple-element.12.image_ref) | copy-start | bytes 393220

commit v3 on v2

--- a/solution.py
+++ b/solution.py
@@ -15,6 +15,7 @@
 F32 = jnp.float32
 EXTRA = 16
 GROUP = 16
+AHEAD = 4
 GRANT = 24 * 2**20
 NT = (((1,), (1,)), ((), ()))
 
@@ -206,32 +207,24 @@
         packed = packed + small_ref[at]
     gram = jnp.concatenate([packed[:, :order], packed[:, order : 2 * order]], axis=0)
     cross = jnp.concatenate([packed[:, 2 * order : 3 * order], packed[:, 3 * order :]], axis=0)
+    work = jnp.concatenate([gram, cross], axis=1)
     rows = lax.broadcasted_iota(jnp.int32, (order, 1), 0)
+
+    def wide(column):
+        return jnp.broadcast_to(work[:, column : column + 1], work.shape)
+
+    ahead = [wide(column) for column in range(min(order, AHEAD + 1))]
+    for column in range(order):
+        pivots = ahead.pop(0)
+        inverse = 1.0 / pivots[column : column + 1]
+        factor = jnp.where(rows == column, 0.0, pivots)
+        ahead = [later - factor * (later[column : column + 1] * inverse) for later in ahead]
+        work = work - factor * (work[column : column + 1] * inverse)
+        if column + AHEAD + 1 < order:
+            ahead.append(wide(column + AHEAD + 1))
     eye = (rows == lax.broadcasted_iota(jnp.int32, (order, order), 1)).astype(F32)
-    down = lax.rsqrt(jnp.sum(gram * eye, axis=1, keepdims=True))
-    across = lax.rsqrt(jnp.sum(gram * eye, axis=0, keepdims=True))
-    work = jnp.concatenate([gram * down * across, cross * down], axis=1)
-    inverses = []
-    for first in range(0, order, 2):
-        upper, lower = work[first : first + 1], work[first + 1 : first + 2]
-        a, b, c = upper[:, first : first + 1], upper[:, first + 1 : first + 2], lower[:, first + 1 : first + 2]
-        scale = 1.0 / (a * c - b * b)
-        inverse = (c * scale, -b * scale, a * scale)
-        inverses.append(inverse)
-        inside = (rows == first) | (rows == first + 1)
-        left = jnp.where(inside, 0.0, work[:, first : first + 1])
-        right = jnp.where(inside, 0.0, work[:, first + 1 : first + 2])
-        work = (
-            work
-            - (left * inverse[0] + right * inverse[1]) * upper
-            - (left * inverse[1] + right * inverse[2]) * lower
-        )
-    found = []
-    for first, inverse in zip(range(0, order, 2), inverses):
-        upper, lower = work[first : first + 1, order:], work[first + 1 : first + 2, order:]
-        found.append(inverse[0] * upper + inverse[1] * lower)
-        found.append(inverse[1] * upper + inverse[2] * lower)
-    coeffs = (jnp.concatenate(found, axis=0) * down).T
+    diagonal = jnp.sum(work[:, :order] * eye, axis=1, keepdims=True)
+    coeffs = (work[:, order:] / diagonal).T
     solution_out[...] = solution_ref[...] + jnp.dot(coeffs, residual_ref[...], precision=FULL, preferred_element_type=F32)
     residual_out[...] = residual_ref[...] - jnp.dot(coeffs, image_ref[...], precision=FULL, preferred_element_type=F32)
 
@@ -256,8 +249,9 @@
     def send(step, block):
         return lax.ppermute(block, "gy", [(i, i ^ step) for i in range(column_total)])
 
-    near_blocks[top] = send(top, near_block)
-    for step in [*range(top + 2, column_total, 2), *range(1, top)]:
+    for step in [*range(top, column_total, 2), *range(1, min(top, 2))]:
+        near_blocks[step] = send(step, near_block)
+    for step in range(2, top):
         near_blocks[step] = send(step, near_block)
     if top > 1:
         for step in range(top, column_total, 2):

time: 77.9 us -> 73.7 us (0.946)
  Pallas kernels: 17.5 us -> 13.3 us
    pallas_call x1, Pallas kernels: 6.19 us -> 2.05 us  [step_of(): pl.pallas_call(solve_body, out_shape=(jax.ShapeDtypeStruct((width, count)...]
  transfers between devices with their start and end apart: 10 -> 10, of which waited for: 4 -> 4; matrix products, arithmetic and copies ran while one was open for 0% -> 0% of each run, Pallas kernels for 8% -> 9%
where the time goes in v3:
time: 73.7 us; the launch traced here: 73.5 us
  blocking collectives  29.7 us (40%)
  waiting for transfers between devices  15.5 us (21%)
  Pallas kernels  13.3 us (18%)
  starting transfers between devices  11.7 us (16%)
  local copies, waits for them, and re-layouts  2.49 us (3%)
  between operations  0.74 us (1%)
    all_to_all x1, blocking collectives, step_of(): mine = lax.all_to_all(blocks, 'gy', 0, 0)  15.1 us
    all_to_all x1, blocking collectives, step_of(): small = lax.all_to_all(small, ('gx', 'gy'), 0, 0)  14.6 us
    ppermute x7, waiting for transfers between devices, send(): lax.ppermute(block, 'gy', [(i, i ^ step) for i in range(column_total)])  14.2 us
    ppermute x7, starting transfers between devices, send(): lax.ppermute(block, 'gy', [(i, i ^ step) for i in range(column_total)])  10.2 us
    pallas_call x1, Pallas kernels, step_of(): pl.pallas_call(functools.partial(tree_body, leaf_dev, depth), out_shape=j...  6.28 us
    pallas_call x1, Pallas kernels, step_of(): pl.pallas_call(functools.partial(near_body, leaf_dev, depth), out_shape=(...  4.4 us
    unnamed x18, local copies, waits for them, and re-layouts  2.49 us
    pallas_call x1, Pallas kernels, step_of(): pl.pallas_call(solve_body, out_shape=(jax.ShapeDtypeStruct((width, count)...  2.05 us
  transfers between devices with their start and end apart: 10, of which 4 were waited for; matrix products, arithmetic and copies ran while one was open for 0% of the time, Pallas kernels for 9%

profile of v3, /device:TPU:0, one launch (start us, length us, event | category | flops | bytes accessed | tf_op | source)
XLA Modules:
  0.0 73.5 jit_solution(3570672728330689647)
XLA Ops:
  0.6 0.0 copy-start.8
  0.6 0.6 copy-done.8
  1.3 0.0 copy-start
  1.3 0.9 %copy-done = f32[1024,32]{0,1:T(8,128)S(1)} copy-done((f32[1024,32]{0,1:T(8,128)S(1)}, f32[1024,32]{0,1:T(8,128)}, u32[]{:S(2)}) %copy-start) | copy-done | bytes 131096
  2.2 0.0 copy-start.2
  2.2 0.9 %copy-done.2 = bf16[1024,64]{0,1:T(8,128)(2,1)S(1)} copy-done((bf16[1024,64]{0,1:T(8,128)(2,1)S(1)}, bf16[1024,64]{0,1:T(8,128)(2,1)}, u32[]{:S(2)}) %copy-start.2) | copy-done | bytes 131096
  3.1 0.6 skeleton.1
  3.7 15.1 %all_to_all.10.refs_0_ = bf16[8,96,128]{2,1,0:T(8,128)(2,1)S(1)} all-to-all(bf16[8,96,128]{2,1,0:T(8,128)(2,1)S(1)} %get-tuple-element.10), channel_id=1, replica_groups=mesh['gx'=4,'gy'=8] {'gy'}, dimensions={0} | all-to-all | bytes 393216 | tf_op jit(solution)/shard_map/all_to_all | solution.py:272
  18.8 1.5 %collective-permute-start.1 = (bf16[8,96,128]{2,1,0:T(8,128)(2,1)S(1)}, bf16[8,96,128]{2,1,0:T(8,128)(2,1)S(1)}, u32[]{:S(2)}, u32[]{:S(2)}) collective-permute-start(bf16[8,96,128]{2,1,0:T(8,128)(2,1)S(1)} %all_to_all.10.refs_0_), channel_id=1, source_target_pairs={{0,16},{8,24},{16,0},{24,8},{1,17},{9,25},{17,1},{25,9},{2,18},{10... | collective-permute-start | bytes 589832 | tf_op jit(solution)/shard_map/ppermute | solution.py:277
  20.3 0.0 copy-start.5
  20.3 0.0 copy-start.7
  20.4 0.8 %collective-permute-start.6 = (bf16[96,1024]{1,0:T(8,128)(2,1)S(1)}, bf16[96,1024]{1,0:T(8,128)(2,1)S(1)}, u32[]{:S(2)}, u32[]{:S(2)}) collective-permute-start(bf16[96,1024]{1,0:T(8,128)(2,1)S(1)} %pad_maximum_fusion.own_ref), channel_id=1, source_target_pairs={{0,4},{1,5},{2,6},{3,7},{4,0},{5,1},{6,2},{7,3},{8,12},{9,13},{10,... | collective-permute-start | bytes 589832 | tf_op jit(solution)/shard_map/ppermute | solution.py:250
  21.1 1.9 %collective-permute-start.8 = (bf16[96,1024]{1,0:T(8,128)(2,1)S(1)}, bf16[96,1024]{1,0:T(8,128)(2,1)S(1)}, u32[]{:S(2)}, u32[]{:S(2)}) collective-permute-start(bf16[96,1024]{1,0:T(8,128)(2,1)S(1)} %pad_maximum_fusion.own_ref), channel_id=1, source_target_pairs={{0,6},{1,7},{2,4},{3,5},{4,2},{5,3},{6,0},{7,1},{8,14},{9,15},{10,... | collective-permute-start | bytes 589832 | tf_op jit(solution)/shard_map/ppermute | solution.py:250
  23.1 0.0 collective-permute-start
  23.1 1.4 %collective-permute-done.1.refs_2_ = bf16[8,96,128]{2,1,0:T(8,128)(2,1)S(1)} collective-permute-done((bf16[8,96,128]{2,1,0:T(8,128)(2,1)S(1)}, bf16[8,96,128]{2,1,0:T(8,128)(2,1)S(1)}, u32[]{:S(2)}, u32[]{:S(2)}) %collective-permute-start.1) | collective-permute-done | bytes 196640 | tf_op jit(solution)/shard_map/ppermute | solution.py:277
  24.4 0.0 collective-permute-start.2
  24.4 1.1 %collective-permute-start.3 = (bf16[96,1024]{1,0:T(8,128)(2,1)S(1)}, bf16[96,1024]{1,0:T(8,128)(2,1)S(1)}, u32[]{:S(2)}, u32[]{:S(2)}) collective-permute-start(bf16[96,1024]{1,0:T(8,128)(2,1)S(1)} %pad_maximum_fusion.own_ref), channel_id=1, source_target_pairs={{0,1},{1,0},{2,3},{3,2},{4,5},{5,4},{6,7},{7,6},{8,9},{9,8},{10,11... | collective-permute-start | bytes 589832 | tf_op jit(solution)/shard_map/ppermute | solution.py:250
  25.5 8.9 %collective-permute-done.6.refs_3_ = bf16[96,1024]{1,0:T(8,128)(2,1)S(1)} collective-permute-done((bf16[96,1024]{1,0:T(8,128)(2,1)S(1)}, bf16[96,1024]{1,0:T(8,128)(2,1)S(1)}, u32[]{:S(2)}, u32[]{:S(2)}) %collective-permute-start.6) | collective-permute-done | bytes 196640 | tf_op jit(solution)/shard_map/ppermute | solution.py:250
  34.4 0.0 collective-permute-start.4
  34.4 0.0 collective-permute-done.8.refs_5_
  34.4 4.3 %collective-permute-start.5 = (bf16[96,1024]{1,0:T(8,128)(2,1)S(1)}, bf16[96,1024]{1,0:T(8,128)(2,1)S(1)}, u32[]{:S(2)}, u32[]{:S(2)}) collective-permute-start(bf16[96,1024]{1,0:T(8,128)(2,1)S(1)} %pad_maximum_fusion.own_ref), channel_id=1, source_target_pairs={{0,3},{1,2},{2,1},{3,0},{4,7},{5,6},{6,5},{7,4},{8,11},{9,10},{10,... | collective-permute-start | bytes 589832 | tf_op jit(solution)/shard_map/ppermute | solution.py:250
  38.8 0.0 collective-permute-done.refs_1_
  38.8 1.8 %collective-permute-start.7 = (bf16[96,1024]{1,0:T(8,128)(2,1)S(1)}, bf16[96,1024]{1,0:T(8,128)(2,1)S(1)}, u32[]{:S(2)}, u32[]{:S(2)}) collective-permute-start(bf16[96,1024]{1,0:T(8,128)(2,1)S(1)} %collective-permute-done.6.refs_3_), channel_id=1, source_target_pairs={{0,1},{1,0},{2,3},{3,2},{4,5},{5,4},{6,7},{7,6},{8,9},{9,8},{10,11... | collective-permute-start | bytes 589832 | tf_op jit(solution)/shard_map/ppermute | solution.py:250
  40.6 0.0 collective-permute-done.2.refs_3_
  40.6 0.2 collective-permute-start.9
  40.8 0.0 copy-done.5
  40.8 0.0 copy-done.7
  40.8 0.0 copy-start.1
  40.8 0.0 copy-start.6
  40.8 6.3 %tree.1.part_ref = f32[32,1024]{1,0:T(8,128)S(1)} custom-call(s32[2,16]{1,0:T(2,128)S(1)} %copy-done.7, s32[31,128]{1,0:T(8,128)S(1)} %copy-done.5, bf16[80,1024]{1,0:T(8,128)(2,1)S(1)} %get-tuple-element.9.right_ref, bf16[96,1024]{1,0:T(8,128)(2,1)S(1)} %pad_maximum_fusion.own_ref, bf16[8,96,128]{2,1,0:T(8,128)(2,1)S(1)} %all_to_all.10.refs_0_, ...), custom_call_target="tpu_custom_call" | custom-call | tf_op jit(solution)/shard_map/tree/pallas_call | solution.py:280
  47.1 0.0 collective-permute-done.3.refs_0_
  47.1 0.0 collective-permute-done.4.refs_1_
  47.1 0.0 collective-permute-done.5.refs_2_
  47.1 1.6 %collective-permute-done.7.refs_4_ = bf16[96,1024]{1,0:T(8,128)(2,1)S(1)} collective-permute-done((bf16[96,1024]{1,0:T(8,128)(2,1)S(1)}, bf16[96,1024]{1,0:T(8,128)(2,1)S(1)}, u32[]{:S(2)}, u32[]{:S(2)}) %collective-permute-start.7) | collective-permute-done | bytes 196640 | tf_op jit(solution)/shard_map/ppermute | solution.py:250
  48.7 3.7 %collective-permute-done.9.refs_6_ = bf16[96,1024]{1,0:T(8,128)(2,1)S(1)} collective-permute-done((bf16[96,1024]{1,0:T(8,128)(2,1)S(1)}, bf16[96,1024]{1,0:T(8,128)(2,1)S(1)}, u32[]{:S(2)}, u32[]{:S(2)}) %collective-permute-start.9) | collective-permute-done | bytes 196640 | tf_op jit(solution)/shard_map/ppermute | solution.py:250
  52.4 0.0 copy-done.1
  52.4 0.0 copy-done.6
  52.4 4.4 %near.1 = (f32[32,1024]{1,0:T(8,128)}, f32[32,16,128]{2,1,0:T(8,128)S(1)}) custom-call(s32[2,4]{1,0:T(2,128)S(1)} %copy-done.6, bf16[80,1024]{1,0:T(8,128)(2,1)S(1)} %get-tuple-element.9.right_ref, f32[32,1024]{1,0:T(8,128)S(1)} %tree.1.part_ref, f32[32,1024]{1,0:T(8,128)S(1)} %bitcast.8, bf16[96,1024]{1,0:T(8,128)(2,1)S(1)} %collective-permute-done.3.refs_0_, ...), custom_call_target="tpu_custom_call" | custom-call | tf_op jit(solution)/shard_map/near/pallas_call | solution.py:291
  56.8 0.0 copy-start.3
  56.8 0.0 copy-start.4
  56.8 14.6 %all_to_all.11.small_ref = f32[32,16,128]{2,1,0:T(8,128)S(1)} all-to-all(f32[32,16,128]{2,1,0:T(8,128)S(1)} %get-tuple-element.11), channel_id=1, replica_groups=mesh['gx'=4,'gy'=8] {'gx','gy'}, dimensions={0} | all-to-all | bytes 524288 | tf_op jit(solution)/shard_map/all_to_all | solution.py:309
  71.4 0.0 copy-done.3
  71.5 0.0 copy-done.4
  71.5 2.0 %solve.1 = (f32[32,1024]{1,0:T(8,128)}, f32[32,1024]{1,0:T(8,128)}) custom-call(f32[32,16,128]{2,1,0:T(8,128)S(1)} %all_to_all.11.small_ref, f32[32,1024]{1,0:T(8,128)S(1)} %bitcast.12, f32[32,1024]{1,0:T(8,128)S(1)} %bitcast.9, f32[32,1024]{1,0:T(8,128)S(1)} %copy-done.4), custom_call_target="tpu_custom_call" | custom-call | tf_op jit(solution)/shard_map/solve/pallas_call | solution.py:310
  (2 shorter events, 0.0 us)
Async XLA Ops:
  0.6 0.7 copy-start.8
  1.3 0.9 %copy-start = (f32[1024,32]{0,1:T(8,128)S(1)}, f32[1024,32]{0,1:T(8,128)}, u32[]{:S(2)}) copy-start(f32[1024,32]{0,1:T(8,128)} %param.9) | copy-start | bytes 393220
  2.2 0.9 %copy-start.2 = (bf16[1024,64]{0,1:T(8,128)(2,1)S(1)}, bf16[1024,64]{0,1:T(8,128)(2,1)}, u32[]{:S(2)}) copy-start(bf16[1024,64]{0,1:T(8,128)(2,1)} %param.7) | copy-start | bytes 393220
  18.8 5.7 %collective-permute-start.1 = (bf16[8,96,128]{2,1,0:T(8,128)(2,1)S(1)}, bf16[8,96,128]{2,1,0:T(8,128)(2,1)S(1)}, u32[]{:S(2)}, u32[]{:S(2)}) collective-permute-start(bf16[8,96,128]{2,1,0:T(8,128)(2,1)S(1)} %all_to_all.10.refs_0_), channel_id=1, source_target_pairs={{0,16},{8,24},{16,0},{24,8},{1,17},{9,25},{17,1},{25,9},{2,18},{10... | collective-permute-start | bytes 589832 | tf_op jit(solution)/shard_map/ppermute | solution.py:277
  20.3 20.5 %copy-start.5 = (s32[31,128]{1,0:T(8,128)S(1)}, s32[31,128]{1,0:T(8,128)}, u32[]{:S(2)}) copy-start(s32[31,128]{1,0:T(8,128)} %upper_ref.1) | copy-start | bytes 47620
  20.3 20.5 %copy-start.7 = (s32[2,16]{1,0:T(2,128)S(1)}, s32[2,16]{1,0:T(2,128)}, u32[]{:S(2)}) copy-start(s32[2,16]{1,0:T(2,128)} %far_ref.1) | copy-start | bytes 388
  20.4 14.1 %collective-permute-start.6 = (bf16[96,1024]{1,0:T(8,128)(2,1)S(1)}, bf16[96,1024]{1,0:T(8,128)(2,1)S(1)}, u32[]{:S(2)}, u32[]{:S(2)}) collective-permute-start(bf16[96,1024]{1,0:T(8,128)(2,1)S(1)} %pad_maximum_fusion.own_ref), channel_id=1, source_target_pairs={{0,4},{1,5},{2,6},{3,7},{4,0},{5,1},{6,2},{7,3},{8,12},{9,13},{10,... | collective-permute-start | bytes 589832 | tf_op jit(solution)/shard_map/ppermute | solution.py:250
  21.1 13.3 %collective-permute-start.8 = (bf16[96,1024]{1,0:T(8,128)(2,1)S(1)}, bf16[96,1024]{1,0:T(8,128)(2,1)S(1)}, u32[]{:S(2)}, u32[]{:S(2)}) collective-permute-start(bf16[96,1024]{1,0:T(8,128)(2,1)S(1)} %pad_maximum_fusion.own_ref), channel_id=1, source_target_pairs={{0,6},{1,7},{2,4},{3,5},{4,2},{5,3},{6,0},{7,1},{8,14},{9,15},{10,... | collective-permute-start | bytes 589832 | tf_op jit(solution)/shard_map/ppermute | solution.py:250
  23.1 15.7 %collective-permute-start = (bf16[8,96,128]{2,1,0:T(8,128)(2,1)S(1)}, bf16[8,96,128]{2,1,0:T(8,128)(2,1)S(1)}, u32[]{:S(2)}, u32[]{:S(2)}) collective-permute-start(bf16[8,96,128]{2,1,0:T(8,128)(2,1)S(1)} %all_to_all.10.refs_0_), channel_id=1, source_target_pairs={{0,8},{8,0},{16,24},{24,16},{1,9},{9,1},{17,25},{25,17},{2,10},{10... | collective-permute-start | bytes 589832 | tf_op jit(solution)/shard_map/ppermute | solution.py:277
  24.4 16.1 %collective-permute-start.2 = (bf16[8,96,128]{2,1,0:T(8,128)(2,1)S(1)}, bf16[8,96,128]{2,1,0:T(8,128)(2,1)S(1)}, u32[]{:S(2)}, u32[]{:S(2)}) collective-permute-start(bf16[8,96,128]{2,1,0:T(8,128)(2,1)S(1)} %collective-permute-done.1.refs_2_), channel_id=1, source_target_pairs={{0,8},{8,0},{16,24},{24,16},{1,9},{9,1},{17,25},{25,17},{2,10},{10... | collective-permute-start | bytes 589832 | tf_op jit(solution)/shard_map/ppermute | solution.py:277
  24.4 22.7 %collective-permute-start.3 = (bf16[96,1024]{1,0:T(8,128)(2,1)S(1)}, bf16[96,1024]{1,0:T(8,128)(2,1)S(1)}, u32[]{:S(2)}, u32[]{:S(2)}) collective-permute-start(bf16[96,1024]{1,0:T(8,128)(2,1)S(1)} %pad_maximum_fusion.own_ref), channel_id=1, source_target_pairs={{0,1},{1,0},{2,3},{3,2},{4,5},{5,4},{6,7},{7,6},{8,9},{9,8},{10,11... | collective-permute-start | bytes 589832 | tf_op jit(solution)/shard_map/ppermute | solution.py:250
  34.4 12.7 %collective-permute-start.4 = (bf16[96,1024]{1,0:T(8,128)(2,1)S(1)}, bf16[96,1024]{1,0:T(8,128)(2,1)S(1)}, u32[]{:S(2)}, u32[]{:S(2)}) collective-permute-start(bf16[96,1024]{1,0:T(8,128)(2,1)S(1)} %pad_maximum_fusion.own_ref), channel_id=1, source_target_pairs={{0,2},{1,3},{2,0},{3,1},{4,6},{5,7},{6,4},{7,5},{8,10},{9,11},{10,... | collective-permute-start | bytes 589832 | tf_op jit(solution)/shard_map/ppermute | solution.py:250
  34.4 12.7 %collective-permute-start.5 = (bf16[96,1024]{1,0:T(8,128)(2,1)S(1)}, bf16[96,1024]{1,0:T(8,128)(2,1)S(1)}, u32[]{:S(2)}, u32[]{:S(2)}) collective-permute-start(bf16[96,1024]{1,0:T(8,128)(2,1)S(1)} %pad_maximum_fusion.own_ref), channel_id=1, source_target_pairs={{0,3},{1,2},{2,1},{3,0},{4,7},{5,6},{6,5},{7,4},{8,11},{9,10},{10,... | collective-permute-start | bytes 589832 | tf_op jit(solution)/shard_map/ppermute | solution.py:250
  38.8 10.0 %collective-permute-start.7 = (bf16[96,1024]{1,0:T(8,128)(2,1)S(1)}, bf16[96,1024]{1,0:T(8,128)(2,1)S(1)}, u32[]{:S(2)}, u32[]{:S(2)}) collective-permute-start(bf16[96,1024]{1,0:T(8,128)(2,1)S(1)} %collective-permute-done.6.refs_3_), channel_id=1, source_target_pairs={{0,1},{1,0},{2,3},{3,2},{4,5},{5,4},{6,7},{7,6},{8,9},{9,8},{10,11... | collective-permute-start | bytes 589832 | tf_op jit(solution)/shard_map/ppermute | solution.py:250
  40.6 11.8 %collective-permute-start.9 = (bf16[96,1024]{1,0:T(8,128)(2,1)S(1)}, bf16[96,1024]{1,0:T(8,128)(2,1)S(1)}, u32[]{:S(2)}, u32[]{:S(2)}) collective-permute-start(bf16[96,1024]{1,0:T(8,128)(2,1)S(1)} %collective-permute-done.8.refs_5_), channel_id=1, source_target_pairs={{0,1},{1,0},{2,3},{3,2},{4,5},{5,4},{6,7},{7,6},{8,9},{9,8},{10,11... | collective-permute-start | bytes 589832 | tf_op jit(solution)/shard_map/ppermute | solution.py:250
  40.8 11.6 %copy-start.1 = (f32[1024,32]{0,1:T(8,128)S(1)}, f32[1024,32]{0,1:T(8,128)}, u32[]{:S(2)}) copy-start(f32[1024,32]{0,1:T(8,128)} %param.9) | copy-start | bytes 393220
  40.8 11.6 %copy-start.6 = (s32[2,4]{1,0:T(2,128)S(1)}, s32[2,4]{1,0:T(2,128)}, u32[]{:S(2)}) copy-start(s32[2,4]{1,0:T(2,128)} %near_ref.1) | copy-start | bytes 100
  56.8 14.6 %copy-start.3 = (f32[1024,32]{0,1:T(8,128)S(1)}, f32[1024,32]{0,1:T(8,128)}, u32[]{:S(2)}) copy-start(f32[1024,32]{0,1:T(8,128)} %param.8) | copy-start | bytes 393220
  56.8 14.6 %copy-start.4 = (f32[32,1024]{1,0:T(8,128)S(1)}, f32[32,1024]{1,0:T(8,128)}, u32[]{:S(2)}) copy-start(f32[32,1024]{1,0:T(8,128)} %get-tuple-element.12.image_ref) | copy-start | bytes 393220

commit v4 on v3

--- a/solution.py
+++ b/solution.py
@@ -249,13 +249,16 @@
     def send(step, block):
         return lax.ppermute(block, "gy", [(i, i ^ step) for i in range(column_total)])
 
-    for step in [*range(top, column_total, 2), *range(1, min(top, 2))]:
+    near_blocks[top] = send(top, near_block)
+    near_blocks[1] = send(1, near_block)
+    for step in range(top + 2, column_total, 2):
         near_blocks[step] = send(step, near_block)
-    for step in range(2, top):
+    near_blocks[top + 1] = send(1, near_blocks[top])
+    for step in range(2, top, 2):
         near_blocks[step] = send(step, near_block)
-    if top > 1:
-        for step in range(top, column_total, 2):
-            near_blocks[step + 1] = send(1, near_blocks[step])
+        near_blocks[step + 1] = send(step, near_blocks[1])
+    for step in range(top + 2, column_total, 2):
+        near_blocks[step + 1] = send(1, near_blocks[step])
     deep = depth + EXTRA
 
     blocks, right = pl.pallas_call(

time: 73.7 us -> 70.6 us (0.958)
  blocking collectives: 29.7 us -> 17.4 us
  waiting for transfers between devices: 15.5 us -> 20.3 us
  starting transfers between devices: 11.7 us -> 15.3 us
  Pallas kernels: 13.3 us -> 14.1 us
    all_to_all x1 -> x0, blocking collectives: 15.1 us -> none  [step_of(): mine = lax.all_to_all(blocks, 'gy', 0, 0)]
    all_to_all x0 -> x1, waiting for transfers between devices: none -> 7.9 us  [step_of(): mine = lax.all_to_all(blocks, 'gy', 0, 0)]
    all_to_all x0 -> x1, starting transfers between devices: none -> 7.41 us  [step_of(): mine = lax.all_to_all(blocks, 'gy', 0, 0)]
    ppermute x7, starting transfers between devices: 10.2 us -> 6.13 us  [send(): lax.ppermute(block, 'gy', [(i, i ^ step) for i in range(column_total)])]
    all_to_all x1, blocking collectives: 14.6 us -> 17.4 us  [step_of(): small = lax.all_to_all(small, ('gx', 'gy'), 0, 0)]
    ppermute x7, waiting for transfers between devices: 14.2 us -> 12.1 us  [send(): lax.ppermute(block, 'gy', [(i, i ^ step) for i in range(column_total)])]
    ppermute x3, waiting for transfers between devices: 1.37 us -> 0.3 us  [step_of(): lax.ppermute(part, 'gx', swap)]
    pallas_call x1, Pallas kernels: 0.61 us -> 1.35 us  [step_of(): pl.pallas_call(skeleton_body, out_shape=(jax.ShapeDtypeStruct((column_tot...]
  transfers between devices with their start and end apart: 10 -> 11, of which waited for: 4 -> 5; matrix products, arithmetic and copies ran while one was open for 0% -> 0% of each run, Pallas kernels for 9% -> 9%
where the time goes in v4:
time: 70.6 us; the launch traced here: 70.3 us
  waiting for transfers between devices  20.3 us (29%)
  blocking collectives  17.4 us (25%)
  starting transfers between devices  15.3 us (22%)
  Pallas kernels  14.1 us (20%)
  local copies, waits for them, and re-layouts  2.5 us (4%)
  between operations  0.76 us (1%)
    all_to_all x1, blocking collectives, step_of(): small = lax.all_to_all(small, ('gx', 'gy'), 0, 0)  17.4 us
    ppermute x7, waiting for transfers between devices, send(): lax.ppermute(block, 'gy', [(i, i ^ step) for i in range(column_total)])  12.1 us
    all_to_all x1, waiting for transfers between devices, step_of(): mine = lax.all_to_all(blocks, 'gy', 0, 0)  7.9 us
    all_to_all x1, starting transfers between devices, step_of(): mine = lax.all_to_all(blocks, 'gy', 0, 0)  7.41 us
    pallas_call x1, Pallas kernels, step_of(): pl.pallas_call(functools.partial(tree_body, leaf_dev, depth), out_shape=j...  6.29 us
    ppermute x7, starting transfers between devices, send(): lax.ppermute(block, 'gy', [(i, i ^ step) for i in range(column_total)])  6.13 us
    pallas_call x1, Pallas kernels, step_of(): pl.pallas_call(functools.partial(near_body, leaf_dev, depth), out_shape=(...  4.4 us
    unnamed x20, local copies, waits for them, and re-layouts  2.5 us
  transfers between devices with their start and end apart: 11, of which 5 were waited for; matrix products, arithmetic and copies ran while one was open for 0% of the time, Pallas kernels for 9%

profile of v4, /device:TPU:0, one launch (start us, length us, event | category | flops | bytes accessed | tf_op | source)
XLA Modules:
  0.0 70.3 jit_solution(14340231524526187904)
XLA Ops:
  0.6 0.0 copy-start.9
  0.6 0.6 copy-done.9
  1.3 0.0 copy-start
  1.3 0.9 %copy-done = f32[1024,32]{0,1:T(8,128)S(1)} copy-done((f32[1024,32]{0,1:T(8,128)S(1)}, f32[1024,32]{0,1:T(8,128)}, u32[]{:S(2)}) %copy-start) | copy-done | bytes 131096
  2.2 0.0 copy-start.2
  2.2 0.9 %copy-done.2 = bf16[1024,64]{0,1:T(8,128)(2,1)S(1)} copy-done((bf16[1024,64]{0,1:T(8,128)(2,1)S(1)}, bf16[1024,64]{0,1:T(8,128)(2,1)}, u32[]{:S(2)}) %copy-start.2) | copy-done | bytes 131096
  3.1 1.4 %skeleton.1 = (bf16[8,96,128]{2,1,0:T(8,128)(2,1)}, bf16[80,1024]{1,0:T(8,128)(2,1)S(1)}) custom-call(s32[1,128]{1,0:T(1,128)S(1)} %copy-done.9, bf16[64,1024]{1,0:T(8,128)(2,1)S(1)} %bitcast.10, f32[32,1024]{1,0:T(8,128)S(1)} %bitcast.7), custom_call_target="tpu_custom_call" | custom-call | tf_op jit(solution)/shard_map/skeleton/pallas_call | solution.py:264
  4.4 0.0 copy-start.1
  4.4 7.4 %all-to-all-start = ((bf16[8,96,128]{2,1,0:T(8,128)(2,1)}), bf16[8,96,128]{2,1,0:T(8,128)(2,1)S(1)}, u32[]{:S(2)}, u32[]{:S(2)}) async-start(bf16[8,96,128]{2,1,0:T(8,128)(2,1)} %get-tuple-element.10), calls=%async_computation | async-start | bytes 393216 | tf_op jit(solution)/shard_map/all_to_all | solution.py:275
  11.9 0.0 copy-done.1
  11.9 0.0 copy-start.3
  11.9 0.0 copy-start.6
  11.9 7.9 %all-to-all-done.refs_0_ = bf16[8,96,128]{2,1,0:T(8,128)(2,1)S(1)} async-done(((bf16[8,96,128]{2,1,0:T(8,128)(2,1)}), bf16[8,96,128]{2,1,0:T(8,128)(2,1)S(1)}, u32[]{:S(2)}, u32[]{:S(2)}) %all-to-all-start) | async-done | bytes 196640 | tf_op jit(solution)/shard_map/all_to_all | solution.py:275
  19.8 1.5 %collective-permute-start.1 = (bf16[8,96,128]{2,1,0:T(8,128)(2,1)S(1)}, bf16[8,96,128]{2,1,0:T(8,128)(2,1)S(1)}, u32[]{:S(2)}, u32[]{:S(2)}) collective-permute-start(bf16[8,96,128]{2,1,0:T(8,128)(2,1)S(1)} %all-to-all-done.refs_0_), channel_id=1, source_target_pairs={{0,16},{8,24},{16,0},{24,8},{1,17},{9,25},{17,1},{25,9},{2,18},{10... | collective-permute-start | bytes 589832 | tf_op jit(solution)/shard_map/ppermute | solution.py:280
  21.3 0.0 copy-done.3
  21.4 0.0 copy-start.8
  21.4 1.1 %collective-permute-start.3 = (bf16[96,1024]{1,0:T(8,128)(2,1)S(1)}, bf16[96,1024]{1,0:T(8,128)(2,1)S(1)}, u32[]{:S(2)}, u32[]{:S(2)}) collective-permute-start(bf16[96,1024]{1,0:T(8,128)(2,1)S(1)} %pad_maximum_fusion.own_ref), channel_id=1, source_target_pairs={{0,1},{1,0},{2,3},{3,2},{4,5},{5,4},{6,7},{7,6},{8,9},{9,8},{10,11... | collective-permute-start | bytes 589832 | tf_op jit(solution)/shard_map/ppermute | solution.py:250
  22.5 0.0 collective-permute-start.6
  22.5 2.7 %collective-permute-start.8 = (bf16[96,1024]{1,0:T(8,128)(2,1)S(1)}, bf16[96,1024]{1,0:T(8,128)(2,1)S(1)}, u32[]{:S(2)}, u32[]{:S(2)}) collective-permute-start(bf16[96,1024]{1,0:T(8,128)(2,1)S(1)} %pad_maximum_fusion.own_ref), channel_id=1, source_target_pairs={{0,6},{1,7},{2,4},{3,5},{4,2},{5,3},{6,0},{7,1},{8,14},{9,15},{10,... | collective-permute-start | bytes 589832 | tf_op jit(solution)/shard_map/ppermute | solution.py:250
  25.2 0.0 collective-permute-start
  25.2 0.3 collective-permute-done.1.refs_2_
  25.5 0.2 collective-permute-start.2
  25.7 1.4 %collective-permute-done.3.refs_0_ = bf16[96,1024]{1,0:T(8,128)(2,1)S(1)} collective-permute-done((bf16[96,1024]{1,0:T(8,128)(2,1)S(1)}, bf16[96,1024]{1,0:T(8,128)(2,1)S(1)}, u32[]{:S(2)}, u32[]{:S(2)}) %collective-permute-start.3) | collective-permute-done | bytes 196640 | tf_op jit(solution)/shard_map/ppermute | solution.py:250
  27.1 0.3 collective-permute-start.4
  27.4 9.1 %collective-permute-done.6.refs_3_ = bf16[96,1024]{1,0:T(8,128)(2,1)S(1)} collective-permute-done((bf16[96,1024]{1,0:T(8,128)(2,1)S(1)}, bf16[96,1024]{1,0:T(8,128)(2,1)S(1)}, u32[]{:S(2)}, u32[]{:S(2)}) %collective-permute-start.6) | collective-permute-done | bytes 196640 | tf_op jit(solution)/shard_map/ppermute | solution.py:250
  36.5 0.0 collective-permute-start.5
  36.5 0.0 collective-permute-done.8.refs_5_
  36.5 0.7 %collective-permute-start.7 = (bf16[96,1024]{1,0:T(8,128)(2,1)S(1)}, bf16[96,1024]{1,0:T(8,128)(2,1)S(1)}, u32[]{:S(2)}, u32[]{:S(2)}) collective-permute-start(bf16[96,1024]{1,0:T(8,128)(2,1)S(1)} %collective-permute-done.6.refs_3_), channel_id=1, source_target_pairs={{0,1},{1,0},{2,3},{3,2},{4,5},{5,4},{6,7},{7,6},{8,9},{9,8},{10,11... | collective-permute-start | bytes 589832 | tf_op jit(solution)/shard_map/ppermute | solution.py:250
  37.2 0.0 collective-permute-done.refs_1_
  37.2 1.3 %collective-permute-start.9 = (bf16[96,1024]{1,0:T(8,128)(2,1)S(1)}, bf16[96,1024]{1,0:T(8,128)(2,1)S(1)}, u32[]{:S(2)}, u32[]{:S(2)}) collective-permute-start(bf16[96,1024]{1,0:T(8,128)(2,1)S(1)} %collective-permute-done.8.refs_5_), channel_id=1, source_target_pairs={{0,1},{1,0},{2,3},{3,2},{4,5},{5,4},{6,7},{7,6},{8,9},{9,8},{10,11... | collective-permute-start | bytes 589832 | tf_op jit(solution)/shard_map/ppermute | solution.py:250
  38.6 0.0 collective-permute-done.2.refs_3_
  38.6 0.0 copy-done.6
  38.6 0.0 copy-done.8
  38.6 0.0 copy-start.7
  38.6 6.3 %tree.1.part_ref = f32[32,1024]{1,0:T(8,128)S(1)} custom-call(s32[2,16]{1,0:T(2,128)S(1)} %copy-done.8, s32[31,128]{1,0:T(8,128)S(1)} %copy-done.6, bf16[80,1024]{1,0:T(8,128)(2,1)S(1)} %get-tuple-element.9.right_ref, bf16[96,1024]{1,0:T(8,128)(2,1)S(1)} %pad_maximum_fusion.own_ref, bf16[8,96,128]{2,1,0:T(8,128)(2,1)S(1)} %all-to-all-done.refs_0_, ...), custom_call_target="tpu_custom_call" | custom-call | tf_op jit(solution)/shard_map/tree/pallas_call | solution.py:283
  44.9 0.0 collective-permute-done.4.refs_1_
  44.9 0.0 collective-permute-done.5.refs_2_
  44.9 0.0 collective-permute-done.7.refs_4_
  44.9 1.5 %collective-permute-done.9.refs_6_ = bf16[96,1024]{1,0:T(8,128)(2,1)S(1)} collective-permute-done((bf16[96,1024]{1,0:T(8,128)(2,1)S(1)}, bf16[96,1024]{1,0:T(8,128)(2,1)S(1)}, u32[]{:S(2)}, u32[]{:S(2)}) %collective-permute-start.9) | collective-permute-done | bytes 196640 | tf_op jit(solution)/shard_map/ppermute | solution.py:250
  46.4 0.0 copy-done.7
  46.4 4.4 %near.1 = (f32[32,1024]{1,0:T(8,128)}, f32[32,16,128]{2,1,0:T(8,128)S(1)}) custom-call(s32[2,4]{1,0:T(2,128)S(1)} %copy-done.7, bf16[80,1024]{1,0:T(8,128)(2,1)S(1)} %get-tuple-element.9.right_ref, f32[32,1024]{1,0:T(8,128)S(1)} %tree.1.part_ref, f32[32,1024]{1,0:T(8,128)S(1)} %bitcast.8, bf16[96,1024]{1,0:T(8,128)(2,1)S(1)} %collective-permute-done.3.refs_0_, ...), custom_call_target="tpu_custom_call" | custom-call | tf_op jit(solution)/shard_map/near/pallas_call | solution.py:294
  50.8 0.0 copy-start.4
  50.9 0.0 copy-start.5
  50.9 17.4 %all_to_all.10.small_ref = f32[32,16,128]{2,1,0:T(8,128)S(1)} all-to-all(f32[32,16,128]{2,1,0:T(8,128)S(1)} %get-tuple-element.11), channel_id=1, replica_groups=mesh['gx'=4,'gy'=8] {'gx','gy'}, dimensions={0} | all-to-all | bytes 524288 | tf_op jit(solution)/shard_map/all_to_all | solution.py:312
  68.2 0.0 copy-done.4
  68.2 0.0 copy-done.5
  68.2 2.1 %solve.1 = (f32[32,1024]{1,0:T(8,128)}, f32[32,1024]{1,0:T(8,128)}) custom-call(f32[32,16,128]{2,1,0:T(8,128)S(1)} %all_to_all.10.small_ref, f32[32,1024]{1,0:T(8,128)S(1)} %bitcast.12, f32[32,1024]{1,0:T(8,128)S(1)} %bitcast.9, f32[32,1024]{1,0:T(8,128)S(1)} %copy-done.5), custom_call_target="tpu_custom_call" | custom-call | tf_op jit(solution)/shard_map/solve/pallas_call | solution.py:313
  (2 shorter events, 0.0 us)
Async XLA Ops:
  0.6 0.7 copy-start.9
  1.3 0.9 %copy-start = (f32[1024,32]{0,1:T(8,128)S(1)}, f32[1024,32]{0,1:T(8,128)}, u32[]{:S(2)}) copy-start(f32[1024,32]{0,1:T(8,128)} %param.9) | copy-start | bytes 393220
  2.2 0.9 %copy-start.2 = (bf16[1024,64]{0,1:T(8,128)(2,1)S(1)}, bf16[1024,64]{0,1:T(8,128)(2,1)}, u32[]{:S(2)}) copy-start(bf16[1024,64]{0,1:T(8,128)(2,1)} %param.7) | copy-start | bytes 393220
  4.4 7.4 %copy-start.1 = (f32[1024,32]{0,1:T(8,128)S(1)}, f32[1024,32]{0,1:T(8,128)}, u32[]{:S(2)}) copy-start(f32[1024,32]{0,1:T(8,128)} %param.9) | copy-start | bytes 393220
  4.4 15.4 %all-to-all-start = ((bf16[8,96,128]{2,1,0:T(8,128)(2,1)}), bf16[8,96,128]{2,1,0:T(8,128)(2,1)S(1)}, u32[]{:S(2)}, u32[]{:S(2)}) async-start(bf16[8,96,128]{2,1,0:T(8,128)(2,1)} %get-tuple-element.10), calls=%async_computation | async-start | bytes 393216 | tf_op jit(solution)/shard_map/all_to_all | solution.py:275
  11.9 9.5 %copy-start.3 = (bf16[1024,64]{0,1:T(8,128)(2,1)S(1)}, bf16[1024,64]{0,1:T(8,128)(2,1)}, u32[]{:S(2)}) copy-start(bf16[1024,64]{0,1:T(8,128)(2,1)} %param.7) | copy-start | bytes 393220
  11.9 26.7 %copy-start.6 = (s32[31,128]{1,0:T(8,128)S(1)}, s32[31,128]{1,0:T(8,128)}, u32[]{:S(2)}) copy-start(s32[31,128]{1,0:T(8,128)} %upper_ref.1) | copy-start | bytes 47620
  19.8 5.7 %collective-permute-start.1 = (bf16[8,96,128]{2,1,0:T(8,128)(2,1)S(1)}, bf16[8,96,128]{2,1,0:T(8,128)(2,1)S(1)}, u32[]{:S(2)}, u32[]{:S(2)}) collective-permute-start(bf16[8,96,128]{2,1,0:T(8,128)(2,1)S(1)} %all-to-all-done.refs_0_), channel_id=1, source_target_pairs={{0,16},{8,24},{16,0},{24,8},{1,17},{9,25},{17,1},{25,9},{2,18},{10... | collective-permute-start | bytes 589832 | tf_op jit(solution)/shard_map/ppermute | solution.py:280
  21.4 17.2 %copy-start.8 = (s32[2,16]{1,0:T(2,128)S(1)}, s32[2,16]{1,0:T(2,128)}, u32[]{:S(2)}) copy-start(s32[2,16]{1,0:T(2,128)} %far_ref.1) | copy-start | bytes 388
  21.4 5.7 %collective-permute-start.3 = (bf16[96,1024]{1,0:T(8,128)(2,1)S(1)}, bf16[96,1024]{1,0:T(8,128)(2,1)S(1)}, u32[]{:S(2)}, u32[]{:S(2)}) collective-permute-start(bf16[96,1024]{1,0:T(8,128)(2,1)S(1)} %pad_maximum_fusion.own_ref), channel_id=1, source_target_pairs={{0,1},{1,0},{2,3},{3,2},{4,5},{5,4},{6,7},{7,6},{8,9},{9,8},{10,11... | collective-permute-start | bytes 589832 | tf_op jit(solution)/shard_map/ppermute | solution.py:250
  22.5 14.0 %collective-permute-start.6 = (bf16[96,1024]{1,0:T(8,128)(2,1)S(1)}, bf16[96,1024]{1,0:T(8,128)(2,1)S(1)}, u32[]{:S(2)}, u32[]{:S(2)}) collective-permute-start(bf16[96,1024]{1,0:T(8,128)(2,1)S(1)} %pad_maximum_fusion.own_ref), channel_id=1, source_target_pairs={{0,4},{1,5},{2,6},{3,7},{4,0},{5,1},{6,2},{7,3},{8,12},{9,13},{10,... | collective-permute-start | bytes 589832 | tf_op jit(solution)/shard_map/ppermute | solution.py:250
  22.5 14.0 %collective-permute-start.8 = (bf16[96,1024]{1,0:T(8,128)(2,1)S(1)}, bf16[96,1024]{1,0:T(8,128)(2,1)S(1)}, u32[]{:S(2)}, u32[]{:S(2)}) collective-permute-start(bf16[96,1024]{1,0:T(8,128)(2,1)S(1)} %pad_maximum_fusion.own_ref), channel_id=1, source_target_pairs={{0,6},{1,7},{2,4},{3,5},{4,2},{5,3},{6,0},{7,1},{8,14},{9,15},{10,... | collective-permute-start | bytes 589832 | tf_op jit(solution)/shard_map/ppermute | solution.py:250
  25.2 12.1 %collective-permute-start = (bf16[8,96,128]{2,1,0:T(8,128)(2,1)S(1)}, bf16[8,96,128]{2,1,0:T(8,128)(2,1)S(1)}, u32[]{:S(2)}, u32[]{:S(2)}) collective-permute-start(bf16[8,96,128]{2,1,0:T(8,128)(2,1)S(1)} %all-to-all-done.refs_0_), channel_id=1, source_target_pairs={{0,8},{8,0},{16,24},{24,16},{1,9},{9,1},{17,25},{25,17},{2,10},{10... | collective-permute-start | bytes 589832 | tf_op jit(solution)/shard_map/ppermute | solution.py:280
  25.5 13.1 %collective-permute-start.2 = (bf16[8,96,128]{2,1,0:T(8,128)(2,1)S(1)}, bf16[8,96,128]{2,1,0:T(8,128)(2,1)S(1)}, u32[]{:S(2)}, u32[]{:S(2)}) collective-permute-start(bf16[8,96,128]{2,1,0:T(8,128)(2,1)S(1)} %collective-permute-done.1.refs_2_), channel_id=1, source_target_pairs={{0,8},{8,0},{16,24},{24,16},{1,9},{9,1},{17,25},{25,17},{2,10},{10... | collective-permute-start | bytes 589832 | tf_op jit(solution)/shard_map/ppermute | solution.py:280
  27.1 17.8 %collective-permute-start.4 = (bf16[96,1024]{1,0:T(8,128)(2,1)S(1)}, bf16[96,1024]{1,0:T(8,128)(2,1)S(1)}, u32[]{:S(2)}, u32[]{:S(2)}) collective-permute-start(bf16[96,1024]{1,0:T(8,128)(2,1)S(1)} %pad_maximum_fusion.own_ref), channel_id=1, source_target_pairs={{0,2},{1,3},{2,0},{3,1},{4,6},{5,7},{6,4},{7,5},{8,10},{9,11},{10,... | collective-permute-start | bytes 589832 | tf_op jit(solution)/shard_map/ppermute | solution.py:250
  36.5 8.4 %collective-permute-start.5 = (bf16[96,1024]{1,0:T(8,128)(2,1)S(1)}, bf16[96,1024]{1,0:T(8,128)(2,1)S(1)}, u32[]{:S(2)}, u32[]{:S(2)}) collective-permute-start(bf16[96,1024]{1,0:T(8,128)(2,1)S(1)} %collective-permute-done.3.refs_0_), channel_id=1, source_target_pairs={{0,2},{1,3},{2,0},{3,1},{4,6},{5,7},{6,4},{7,5},{8,10},{9,11},{10,... | collective-permute-start | bytes 589832 | tf_op jit(solution)/shard_map/ppermute | solution.py:250
  36.5 8.4 %collective-permute-start.7 = (bf16[96,1024]{1,0:T(8,128)(2,1)S(1)}, bf16[96,1024]{1,0:T(8,128)(2,1)S(1)}, u32[]{:S(2)}, u32[]{:S(2)}) collective-permute-start(bf16[96,1024]{1,0:T(8,128)(2,1)S(1)} %collective-permute-done.6.refs_3_), channel_id=1, source_target_pairs={{0,1},{1,0},{2,3},{3,2},{4,5},{5,4},{6,7},{7,6},{8,9},{9,8},{10,11... | collective-permute-start | bytes 589832 | tf_op jit(solution)/shard_map/ppermute | solution.py:250
  37.2 9.2 %collective-permute-start.9 = (bf16[96,1024]{1,0:T(8,128)(2,1)S(1)}, bf16[96,1024]{1,0:T(8,128)(2,1)S(1)}, u32[]{:S(2)}, u32[]{:S(2)}) collective-permute-start(bf16[96,1024]{1,0:T(8,128)(2,1)S(1)} %collective-permute-done.8.refs_5_), channel_id=1, source_target_pairs={{0,1},{1,0},{2,3},{3,2},{4,5},{5,4},{6,7},{7,6},{8,9},{9,8},{10,11... | collective-permute-start | bytes 589832 | tf_op jit(solution)/shard_map/ppermute | solution.py:250
  38.6 7.9 %copy-start.7 = (s32[2,4]{1,0:T(2,128)S(1)}, s32[2,4]{1,0:T(2,128)}, u32[]{:S(2)}) copy-start(s32[2,4]{1,0:T(2,128)} %near_ref.1) | copy-start | bytes 100
  50.8 17.4 %copy-start.4 = (f32[1024,32]{0,1:T(8,128)S(1)}, f32[1024,32]{0,1:T(8,128)}, u32[]{:S(2)}) copy-start(f32[1024,32]{0,1:T(8,128)} %param.8) | copy-start | bytes 393220
  50.9 17.4 %copy-start.5 = (f32[32,1024]{1,0:T(8,128)S(1)}, f32[32,1024]{1,0:T(8,128)}, u32[]{:S(2)}) copy-start(f32[32,1024]{1,0:T(8,128)} %get-tuple-element.12.image_ref) | copy-start | bytes 393220

commit v5 on v4

--- a/solution.py
+++ b/solution.py
@@ -86,11 +86,10 @@
     right_ref[...] = right
 
 
-def tree_nodes(depth, upper_ref, tree_ref, nodes):
-    rank = upper_ref.shape[1]
-    lanes = lax.broadcasted_iota(jnp.int32, (2 * rank, rank), 0)
+def tree_nodes(depth, pick_ref, tree_ref, nodes):
+    rank = tree_ref.shape[2]
     both = [jnp.concatenate([tree_ref[2 * n + 1], tree_ref[2 * n + 2]], axis=1) for n in nodes]
-    picks = [(lanes == upper_ref[pl.ds(n, 1), :]).astype(F32).astype(BF) for n in nodes]
+    picks = [pick_ref[n] for n in nodes]
     chosen = [
         jnp.dot(b[:depth], pick, preferred_element_type=F32).astype(BF) for b, pick in zip(both, picks)
     ]
@@ -111,7 +110,24 @@
         tree_ref[node] = block
 
 
-def tree_body(leaf_dev, depth, far_ref, upper_ref, right_ref, own_ref, *refs):
+def own_body(leaf_dev, depth, upper_ref, right_ref, own_ref, part_ref, pick_ref):
+    leaf = right_ref.shape[1] // leaf_dev
+    nodes, rank = upper_ref.shape
+    for at in range(leaf_dev):
+        where = slice(at * leaf, (at + 1) * leaf)
+        part_ref[:, where] = fields([own_ref[:, where]], right_ref[:, where], depth) * (
+            1.0 / math.sqrt(leaf)
+        )
+    lanes = lax.broadcasted_iota(jnp.int32, (2 * rank, rank), 0)
+
+    def pick(node, carry):
+        pick_ref[node] = (lanes == upper_ref[pl.ds(node, 1), :]).astype(F32).astype(BF)
+        return carry
+
+    lax.fori_loop(0, nodes, pick, 0)
+
+
+def tree_body(leaf_dev, depth, far_ref, pick_ref, right_ref, own_ref, *refs):
     part_refs, out_ref, tree_ref = refs[:-2], refs[-2], refs[-1]
     row_total = len(part_refs)
     column_total = part_refs[0].shape[0]
@@ -131,7 +147,7 @@
         size = min(count, GROUP)
 
         def level(step, carry, low=low, size=size):
-            tree_nodes(depth, upper_ref, tree_ref, [low + step * size + k for k in range(size)])
+            tree_nodes(depth, pick_ref, tree_ref, [low + step * size + k for k in range(size)])
             return carry
 
         if count == size:
@@ -149,10 +165,7 @@
         for first in range(0, far, each):
             both = jnp.concatenate([tree_ref[far_ref[at, first + k]] for k in range(each)], axis=1)
             sources.append(jnp.concatenate([both[:depth], both[depth + EXTRA :]], axis=0))
-        right = right_ref[:, where]
-        out_ref[:, where] = fields(sources, right, depth) * (1.0 / rank) + fields(
-            [own_ref[:, where]], right, depth
-        ) * (1.0 / math.sqrt(leaf))
+        out_ref[:, where] = own_ref[:, where] + fields(sources, right_ref[:, where], depth) * (1.0 / rank)
 
 
 def near_body(leaf_dev, depth, near_ref, right_ref, part_ref, residual_ref, *refs):
@@ -251,14 +264,6 @@
 
     near_blocks[top] = send(top, near_block)
     near_blocks[1] = send(1, near_block)
-    for step in range(top + 2, column_total, 2):
-        near_blocks[step] = send(step, near_block)
-    near_blocks[top + 1] = send(1, near_blocks[top])
-    for step in range(2, top, 2):
-        near_blocks[step] = send(step, near_block)
-        near_blocks[step + 1] = send(step, near_blocks[1])
-    for step in range(top + 2, column_total, 2):
-        near_blocks[step + 1] = send(1, near_blocks[step])
     deep = depth + EXTRA
 
     blocks, right = pl.pallas_call(
@@ -273,6 +278,15 @@
     name="skeleton",
     )(node_skeleton, points_t, residual_t)
     mine = lax.all_to_all(blocks, "gy", 0, 0)
+    mine, late_block = lax.optimization_barrier((mine, near_block))
+    for step in range(top + 2, column_total, 2):
+        near_blocks[step] = send(step, late_block)
+    near_blocks[top + 1] = send(1, near_blocks[top])
+    for step in range(2, top, 2):
+        near_blocks[step] = send(step, near_block)
+        near_blocks[step + 1] = send(step, near_blocks[1])
+    for step in range(top + 2, column_total, 2):
+        near_blocks[step + 1] = send(1, near_blocks[step])
     parts = {0: mine}
     step = row_total // 2
     while step:
@@ -280,6 +294,17 @@
         parts.update({slot ^ step: lax.ppermute(part, "gx", swap) for slot, part in parts.items()})
         step //= 2
     parts = [parts[slot] for slot in range(row_total)]
+    own_part, picks = pl.pallas_call(
+        functools.partial(own_body, leaf_dev, depth),
+        out_shape=(
+            jax.ShapeDtypeStruct((width, count), F32),
+            jax.ShapeDtypeStruct((device_total - 1, 2 * rank, rank), BF),
+        ),
+        in_specs=vmem(3),
+        out_specs=tuple(vmem(2)),
+        compiler_params=pltpu.CompilerParams(vmem_limit_bytes=GRANT),
+        name="own",
+    )(upper_skeleton, right, near_block)
     partial_t = pl.pallas_call(
         functools.partial(tree_body, leaf_dev, depth),
         out_shape=jax.ShapeDtypeStruct((width, count), F32),
@@ -290,7 +315,7 @@
         ],
         compiler_params=pltpu.CompilerParams(vmem_limit_bytes=GRANT),
     name="tree",
-    )(far_nodes, upper_skeleton, right, near_block, *parts)
+    )(far_nodes, picks, right, own_part, *parts)
     image_t, small = pl.pallas_call(
         functools.partial(near_body, leaf_dev, depth),
         out_shape=(

time: 70.6 us -> 69.2 us (0.980)
  blocking collectives: 17.4 us -> 13.9 us
  waiting for transfers between devices: 20.3 us -> 18 us
  local copies, waits for them, and re-layouts: 2.5 us -> 4.77 us
  other arithmetic: 0.02 us -> 1.87 us
    all_to_all x1, blocking collectives: 17.4 us -> 13.9 us  [step_of(): small = lax.all_to_all(small, ('gx', 'gy'), 0, 0)]
    unnamed x20 -> x18, local copies, waits for them, and re-layouts: 2.5 us -> 4.77 us
    all_to_all x1, waiting for transfers between devices: 7.9 us -> 6.06 us  [step_of(): mine = lax.all_to_all(blocks, 'gy', 0, 0)]
    pallas_call x0 -> x1, Pallas kernels: none -> 1.23 us  [step_of(): pl.pallas_call(functools.partial(own_body, leaf_dev, depth), out_shape=(j...]
    concatenate x1, other arithmetic: 0.01 us -> 0.95 us  [step_of(): near_block = jnp.concatenate([points_t, residual_t.astype(BF)], axis=0)]
    convert_element_type x1, other arithmetic: 0.01 us -> 0.91 us  [step_of(): near_block = jnp.concatenate([points_t, residual_t.astype(BF)], axis=0)]
  transfers between devices with their start and end apart: 11 -> 11, of which waited for: 5 -> 4; matrix products, arithmetic and copies ran while one was open for 0% -> 3% of each run, Pallas kernels for 9% -> 10%
where the time goes in v5:
time: 69.2 us; the launch traced here: 68.8 us
  waiting for transfers between devices  18 us (26%)
  starting transfers between devices  14.9 us (22%)
  Pallas kernels  14.7 us (21%)
  blocking collectives  13.9 us (20%)
  local copies, waits for them, and re-layouts  4.77 us (7%)
  other arithmetic  1.87 us (3%)
  between operations  0.76 us (1%)
    all_to_all x1, blocking collectives, step_of(): small = lax.all_to_all(small, ('gx', 'gy'), 0, 0)  13.9 us
    ppermute x7, waiting for transfers between devices, send(): lax.ppermute(block, 'gy', [(i, i ^ step) for i in range(column_total)])  11.5 us
    all_to_all x1, starting transfers between devices, step_of(): mine = lax.all_to_all(blocks, 'gy', 0, 0)  7.28 us
    ppermute x7, starting transfers between devices, send(): lax.ppermute(block, 'gy', [(i, i ^ step) for i in range(column_total)])  6.07 us
    all_to_all x1, waiting for transfers between devices, step_of(): mine = lax.all_to_all(blocks, 'gy', 0, 0)  6.06 us
    pallas_call x1, Pallas kernels, step_of(): pl.pallas_call(functools.partial(tree_body, leaf_dev, depth), out_shape=j...  5.63 us
    unnamed x18, local copies, waits for them, and re-layouts  4.77 us
    pallas_call x1, Pallas kernels, step_of(): pl.pallas_call(functools.partial(near_body, leaf_dev, depth), out_shape=(...  4.39 us
  transfers between devices with their start and end apart: 11, of which 4 were waited for; matrix products, arithmetic and copies ran while one was open for 3% of the time, Pallas kernels for 10%

profile of v5, /device:TPU:0, one launch (start us, length us, event | category | flops | bytes accessed | tf_op | source)
XLA Modules:
  0.0 68.8 jit_solution(6482571672634740847)
XLA Ops:
  0.6 0.0 copy-start
  0.6 0.9 %copy-done = f32[1024,32]{0,1:T(8,128)S(1)} copy-done((f32[1024,32]{0,1:T(8,128)S(1)}, f32[1024,32]{0,1:T(8,128)}, u32[]{:S(2)}) %copy-start) | copy-done | bytes 131096
  1.5 0.0 copy-start.2
  1.5 0.9 %copy-done.2 = bf16[1024,64]{0,1:T(8,128)(2,1)S(1)} copy-done((bf16[1024,64]{0,1:T(8,128)(2,1)S(1)}, bf16[1024,64]{0,1:T(8,128)(2,1)}, u32[]{:S(2)}) %copy-start.2) | copy-done | bytes 131096
  2.4 0.0 copy-start.8
  2.4 0.7 copy-done.8
  3.1 1.3 %skeleton.1 = (bf16[8,96,128]{2,1,0:T(8,128)(2,1)}, bf16[80,1024]{1,0:T(8,128)(2,1)S(1)}) custom-call(s32[1,128]{1,0:T(1,128)S(1)} %copy-done.8, bf16[64,1024]{1,0:T(8,128)(2,1)S(1)} %bitcast.11, f32[32,1024]{1,0:T(8,128)S(1)} %bitcast.7), custom_call_target="tpu_custom_call" | custom-call | tf_op jit(solution)/shard_map/skeleton/pallas_call | solution.py:269
  4.4 7.3 %all-to-all-start = ((bf16[8,96,128]{2,1,0:T(8,128)(2,1)}), bf16[8,96,128]{2,1,0:T(8,128)(2,1)S(1)}, u32[]{:S(2)}, u32[]{:S(2)}) async-start(bf16[8,96,128]{2,1,0:T(8,128)(2,1)} %get-tuple-element.16), calls=%async_computation | async-start | bytes 393216 | tf_op jit(solution)/shard_map/all_to_all | solution.py:280
  11.7 0.9 %bitcast_convert_fusion = bf16[32,1024]{1,0:T(8,128)(2,1)S(1)} fusion(f32[1024,32]{0,1:T(8,128)} %param.9), kind=kLoop, calls=%fused_computation.1 | loop fusion | flops 32768 | bytes 196608 | tf_op jit(solution)/shard_map/convert_element_type | solution.py:258
  12.6 0.0 copy-start.1
  12.6 0.0 copy-start.7
  12.7 1.0 %pad_maximum_fusion.own_ref = bf16[96,1024]{1,0:T(8,128)(2,1)S(1)} fusion(bf16[32,1024]{1,0:T(8,128)(2,1)S(1)} %bitcast_convert_fusion, bf16[64,1024]{1,0:T(8,128)(2,1)} %bitcast.10), kind=kLoop, calls=%fused_computation | loop fusion | flops 393216 | bytes 393216 | tf_op jit(solution)/shard_map/concatenate | solution.py:258
  13.6 6.1 %all-to-all-done.refs_0_ = bf16[8,96,128]{2,1,0:T(8,128)(2,1)S(1)} async-done(((bf16[8,96,128]{2,1,0:T(8,128)(2,1)}), bf16[8,96,128]{2,1,0:T(8,128)(2,1)S(1)}, u32[]{:S(2)}, u32[]{:S(2)}) %all-to-all-start) | async-done | bytes 196640 | tf_op jit(solution)/shard_map/all_to_all | solution.py:280
  19.7 1.5 %collective-permute-start.1 = (bf16[8,96,128]{2,1,0:T(8,128)(2,1)S(1)}, bf16[8,96,128]{2,1,0:T(8,128)(2,1)S(1)}, u32[]{:S(2)}, u32[]{:S(2)}) collective-permute-start(bf16[8,96,128]{2,1,0:T(8,128)(2,1)S(1)} %all-to-all-done.refs_0_), channel_id=1, source_target_pairs={{0,16},{8,24},{16,0},{24,8},{1,17},{9,25},{17,1},{25,9},{2,18},{10... | collective-permute-start | bytes 589832 | tf_op jit(solution)/shard_map/ppermute | solution.py:294
  21.2 1.1 %collective-permute-start.3 = (bf16[96,1024]{1,0:T(8,128)(2,1)S(1)}, bf16[96,1024]{1,0:T(8,128)(2,1)S(1)}, u32[]{:S(2)}, u32[]{:S(2)}) collective-permute-start(bf16[96,1024]{1,0:T(8,128)(2,1)S(1)} %pad_maximum_fusion.own_ref), channel_id=1, source_target_pairs={{0,1},{1,0},{2,3},{3,2},{4,5},{5,4},{6,7},{7,6},{8,9},{9,8},{10,11... | collective-permute-start | bytes 589832 | tf_op jit(solution)/shard_map/ppermute | solution.py:263
  22.3 0.0 collective-permute-start.6
  22.3 0.0 collective-permute-start
  22.3 2.7 %collective-permute-start.8 = (bf16[96,1024]{1,0:T(8,128)(2,1)S(1)}, bf16[96,1024]{1,0:T(8,128)(2,1)S(1)}, u32[]{:S(2)}, u32[]{:S(2)}) collective-permute-start(bf16[96,1024]{1,0:T(8,128)(2,1)S(1)} %pad_maximum_fusion.own_ref), channel_id=1, source_target_pairs={{0,6},{1,7},{2,4},{3,5},{4,2},{5,3},{6,0},{7,1},{8,14},{9,15},{10,... | collective-permute-start | bytes 589832 | tf_op jit(solution)/shard_map/ppermute | solution.py:263
  25.0 0.4 collective-permute-done.1.refs_2_
  25.4 0.0 collective-permute-start.2
  25.4 1.5 %collective-permute-done.3.refs_0_ = bf16[96,1024]{1,0:T(8,128)(2,1)S(1)} collective-permute-done((bf16[96,1024]{1,0:T(8,128)(2,1)S(1)}, bf16[96,1024]{1,0:T(8,128)(2,1)S(1)}, u32[]{:S(2)}, u32[]{:S(2)}) %collective-permute-start.3) | collective-permute-done | bytes 196640 | tf_op jit(solution)/shard_map/ppermute | solution.py:263
  26.9 0.3 collective-permute-start.4
  27.2 10.0 %collective-permute-done.6.refs_3_ = bf16[96,1024]{1,0:T(8,128)(2,1)S(1)} collective-permute-done((bf16[96,1024]{1,0:T(8,128)(2,1)S(1)}, bf16[96,1024]{1,0:T(8,128)(2,1)S(1)}, u32[]{:S(2)}, u32[]{:S(2)}) %collective-permute-start.6) | collective-permute-done | bytes 196640 | tf_op jit(solution)/shard_map/ppermute | solution.py:263
  37.2 0.0 collective-permute-start.5
  37.2 0.0 collective-permute-done.refs_1_
  37.2 0.9 %collective-permute-start.7 = (bf16[96,1024]{1,0:T(8,128)(2,1)S(1)}, bf16[96,1024]{1,0:T(8,128)(2,1)S(1)}, u32[]{:S(2)}, u32[]{:S(2)}) collective-permute-start(bf16[96,1024]{1,0:T(8,128)(2,1)S(1)} %collective-permute-done.6.refs_3_), channel_id=1, source_target_pairs={{0,1},{1,0},{2,3},{3,2},{4,5},{5,4},{6,7},{7,6},{8,9},{9,8},{10,11... | collective-permute-start | bytes 589832 | tf_op jit(solution)/shard_map/ppermute | solution.py:263
  38.1 0.0 collective-permute-done.8.refs_5_
  38.1 1.1 %collective-permute-start.9 = (bf16[96,1024]{1,0:T(8,128)(2,1)S(1)}, bf16[96,1024]{1,0:T(8,128)(2,1)S(1)}, u32[]{:S(2)}, u32[]{:S(2)}) collective-permute-start(bf16[96,1024]{1,0:T(8,128)(2,1)S(1)} %collective-permute-done.8.refs_5_), channel_id=1, source_target_pairs={{0,1},{1,0},{2,3},{3,2},{4,5},{5,4},{6,7},{7,6},{8,9},{9,8},{10,11... | collective-permute-start | bytes 589832 | tf_op jit(solution)/shard_map/ppermute | solution.py:263
  39.2 0.0 copy-start.5
  39.2 0.7 %copy-done.5 = s32[31,128]{1,0:T(8,128)S(1)} copy-done((s32[31,128]{1,0:T(8,128)S(1)}, s32[31,128]{1,0:T(8,128)}, u32[]{:S(2)}) %copy-start.5) | copy-done | bytes 15896
  39.9 1.2 %own.1 = (f32[32,1024]{1,0:T(8,128)S(1)}, bf16[31,256,128]{2,1,0:T(8,128)(2,1)S(1)}) custom-call(s32[31,128]{1,0:T(8,128)S(1)} %copy-done.5, bf16[80,1024]{1,0:T(8,128)(2,1)S(1)} %get-tuple-element.13.right_ref, bf16[96,1024]{1,0:T(8,128)(2,1)S(1)} %pad_maximum_fusion.own_ref), custom_call_target="tpu_custom_call" | custom-call | tf_op jit(solution)/shard_map/own/pallas_call | solution.py:297
  41.2 0.0 collective-permute-done.2.refs_3_
  41.2 0.0 copy-start.6
  41.2 0.7 copy-done.6
  41.9 0.0 copy-start.3
  41.9 5.6 %tree.1.part_ref = f32[32,1024]{1,0:T(8,128)S(1)} custom-call(s32[2,16]{1,0:T(2,128)S(1)} %copy-done.6, bf16[31,256,128]{2,1,0:T(8,128)(2,1)S(1)} %get-tuple-element.14.pick_ref, bf16[80,1024]{1,0:T(8,128)(2,1)S(1)} %get-tuple-element.13.right_ref, f32[32,1024]{1,0:T(8,128)S(1)} %get-tuple-element.15.own_ref, bf16[8,96,128]{2,1,0:T(8,128)(2,1)S(1)} %all-to-all-done.refs_0_, ...), custom_call_target="tpu_custom_call" | custom-call | tf_op jit(solution)/shard_map/tree/pallas_call | solution.py:308
  47.5 0.0 collective-permute-done.4.refs_1_
  47.5 0.0 collective-permute-done.5.refs_2_
  47.5 0.0 collective-permute-done.7.refs_4_
  47.5 0.0 collective-permute-done.9.refs_6_
  47.5 0.0 copy-done.1
  47.5 0.0 copy-done.7
  47.6 4.4 %near.1 = (f32[32,1024]{1,0:T(8,128)}, f32[32,16,128]{2,1,0:T(8,128)S(1)}) custom-call(s32[2,4]{1,0:T(2,128)S(1)} %copy-done.7, bf16[80,1024]{1,0:T(8,128)(2,1)S(1)} %get-tuple-element.13.right_ref, f32[32,1024]{1,0:T(8,128)S(1)} %tree.1.part_ref, f32[32,1024]{1,0:T(8,128)S(1)} %bitcast.8, bf16[96,1024]{1,0:T(8,128)(2,1)S(1)} %collective-permute-done.3.refs_0_, ...), custom_call_target="tpu_custom_call" | custom-call | tf_op jit(solution)/shard_map/near/pallas_call | solution.py:319
  52.0 13.9 %all_to_all.10.small_ref = f32[32,16,128]{2,1,0:T(8,128)S(1)} all-to-all(f32[32,16,128]{2,1,0:T(8,128)S(1)} %get-tuple-element.19), channel_id=1, replica_groups=mesh['gx'=4,'gy'=8] {'gx','gy'}, dimensions={0} | all-to-all | bytes 524288 | tf_op jit(solution)/shard_map/all_to_all | solution.py:337
  65.8 0.0 copy-done.3
  65.8 0.0 copy-start.4
  65.8 0.9 %copy-done.4 = f32[32,1024]{1,0:T(8,128)S(1)} copy-done((f32[32,1024]{1,0:T(8,128)S(1)}, f32[32,1024]{1,0:T(8,128)}, u32[]{:S(2)}) %copy-start.4) | copy-done | bytes 131096
  66.7 2.1 %solve.1 = (f32[32,1024]{1,0:T(8,128)}, f32[32,1024]{1,0:T(8,128)}) custom-call(f32[32,16,128]{2,1,0:T(8,128)S(1)} %all_to_all.10.small_ref, f32[32,1024]{1,0:T(8,128)S(1)} %bitcast.12, f32[32,1024]{1,0:T(8,128)S(1)} %bitcast.9, f32[32,1024]{1,0:T(8,128)S(1)} %copy-done.4), custom_call_target="tpu_custom_call" | custom-call | tf_op jit(solution)/shard_map/solve/pallas_call | solution.py:338
Async XLA Ops:
  0.6 0.9 %copy-start = (f32[1024,32]{0,1:T(8,128)S(1)}, f32[1024,32]{0,1:T(8,128)}, u32[]{:S(2)}) copy-start(f32[1024,32]{0,1:T(8,128)} %param.9) | copy-start | bytes 393220
  1.5 0.9 %copy-start.2 = (bf16[1024,64]{0,1:T(8,128)(2,1)S(1)}, bf16[1024,64]{0,1:T(8,128)(2,1)}, u32[]{:S(2)}) copy-start(bf16[1024,64]{0,1:T(8,128)(2,1)} %param.7) | copy-start | bytes 393220
  2.4 0.7 copy-start.8
  4.4 15.2 %all-to-all-start = ((bf16[8,96,128]{2,1,0:T(8,128)(2,1)}), bf16[8,96,128]{2,1,0:T(8,128)(2,1)S(1)}, u32[]{:S(2)}, u32[]{:S(2)}) async-start(bf16[8,96,128]{2,1,0:T(8,128)(2,1)} %get-tuple-element.16), calls=%async_computation | async-start | bytes 393216 | tf_op jit(solution)/shard_map/all_to_all | solution.py:280
  12.6 34.9 %copy-start.1 = (f32[1024,32]{0,1:T(8,128)S(1)}, f32[1024,32]{0,1:T(8,128)}, u32[]{:S(2)}) copy-start(f32[1024,32]{0,1:T(8,128)} %param.9) | copy-start | bytes 393220
  12.6 34.9 %copy-start.7 = (s32[2,4]{1,0:T(2,128)S(1)}, s32[2,4]{1,0:T(2,128)}, u32[]{:S(2)}) copy-start(s32[2,4]{1,0:T(2,128)} %near_ref.1) | copy-start | bytes 100
  19.7 5.7 %collective-permute-start.1 = (bf16[8,96,128]{2,1,0:T(8,128)(2,1)S(1)}, bf16[8,96,128]{2,1,0:T(8,128)(2,1)S(1)}, u32[]{:S(2)}, u32[]{:S(2)}) collective-permute-start(bf16[8,96,128]{2,1,0:T(8,128)(2,1)S(1)} %all-to-all-done.refs_0_), channel_id=1, source_target_pairs={{0,16},{8,24},{16,0},{24,8},{1,17},{9,25},{17,1},{25,9},{2,18},{10... | collective-permute-start | bytes 589832 | tf_op jit(solution)/shard_map/ppermute | solution.py:294
  21.2 5.7 %collective-permute-start.3 = (bf16[96,1024]{1,0:T(8,128)(2,1)S(1)}, bf16[96,1024]{1,0:T(8,128)(2,1)S(1)}, u32[]{:S(2)}, u32[]{:S(2)}) collective-permute-start(bf16[96,1024]{1,0:T(8,128)(2,1)S(1)} %pad_maximum_fusion.own_ref), channel_id=1, source_target_pairs={{0,1},{1,0},{2,3},{3,2},{4,5},{5,4},{6,7},{7,6},{8,9},{9,8},{10,11... | collective-permute-start | bytes 589832 | tf_op jit(solution)/shard_map/ppermute | solution.py:263
  22.3 14.9 %collective-permute-start.6 = (bf16[96,1024]{1,0:T(8,128)(2,1)S(1)}, bf16[96,1024]{1,0:T(8,128)(2,1)S(1)}, u32[]{:S(2)}, u32[]{:S(2)}) collective-permute-start(bf16[96,1024]{1,0:T(8,128)(2,1)S(1)} %pad_maximum_fusion.own_ref), channel_id=1, source_target_pairs={{0,4},{1,5},{2,6},{3,7},{4,0},{5,1},{6,2},{7,3},{8,12},{9,13},{10,... | collective-permute-start | bytes 589832 | tf_op jit(solution)/shard_map/ppermute | solution.py:263
  22.3 14.9 %collective-permute-start = (bf16[8,96,128]{2,1,0:T(8,128)(2,1)S(1)}, bf16[8,96,128]{2,1,0:T(8,128)(2,1)S(1)}, u32[]{:S(2)}, u32[]{:S(2)}) collective-permute-start(bf16[8,96,128]{2,1,0:T(8,128)(2,1)S(1)} %all-to-all-done.refs_0_), channel_id=1, source_target_pairs={{0,8},{8,0},{16,24},{24,16},{1,9},{9,1},{17,25},{25,17},{2,10},{10... | collective-permute-start | bytes 589832 | tf_op jit(solution)/shard_map/ppermute | solution.py:294
  22.3 15.8 %collective-permute-start.8 = (bf16[96,1024]{1,0:T(8,128)(2,1)S(1)}, bf16[96,1024]{1,0:T(8,128)(2,1)S(1)}, u32[]{:S(2)}, u32[]{:S(2)}) collective-permute-start(bf16[96,1024]{1,0:T(8,128)(2,1)S(1)} %pad_maximum_fusion.own_ref), channel_id=1, source_target_pairs={{0,6},{1,7},{2,4},{3,5},{4,2},{5,3},{6,0},{7,1},{8,14},{9,15},{10,... | collective-permute-start | bytes 589832 | tf_op jit(solution)/shard_map/ppermute | solution.py:263
  25.4 15.8 %collective-permute-start.2 = (bf16[8,96,128]{2,1,0:T(8,128)(2,1)S(1)}, bf16[8,96,128]{2,1,0:T(8,128)(2,1)S(1)}, u32[]{:S(2)}, u32[]{:S(2)}) collective-permute-start(bf16[8,96,128]{2,1,0:T(8,128)(2,1)S(1)} %collective-permute-done.1.refs_2_), channel_id=1, source_target_pairs={{0,8},{8,0},{16,24},{24,16},{1,9},{9,1},{17,25},{25,17},{2,10},{10... | collective-permute-start | bytes 589832 | tf_op jit(solution)/shard_map/ppermute | solution.py:294
  26.9 20.6 %collective-permute-start.4 = (bf16[96,1024]{1,0:T(8,128)(2,1)S(1)}, bf16[96,1024]{1,0:T(8,128)(2,1)S(1)}, u32[]{:S(2)}, u32[]{:S(2)}) collective-permute-start(bf16[96,1024]{1,0:T(8,128)(2,1)S(1)} %pad_maximum_fusion.own_ref), channel_id=1, source_target_pairs={{0,2},{1,3},{2,0},{3,1},{4,6},{5,7},{6,4},{7,5},{8,10},{9,11},{10,... | collective-permute-start | bytes 589832 | tf_op jit(solution)/shard_map/ppermute | solution.py:263
  37.2 10.3 %collective-permute-start.5 = (bf16[96,1024]{1,0:T(8,128)(2,1)S(1)}, bf16[96,1024]{1,0:T(8,128)(2,1)S(1)}, u32[]{:S(2)}, u32[]{:S(2)}) collective-permute-start(bf16[96,1024]{1,0:T(8,128)(2,1)S(1)} %collective-permute-done.3.refs_0_), channel_id=1, source_target_pairs={{0,2},{1,3},{2,0},{3,1},{4,6},{5,7},{6,4},{7,5},{8,10},{9,11},{10,... | collective-permute-start | bytes 589832 | tf_op jit(solution)/shard_map/ppermute | solution.py:263
  37.2 10.3 %collective-permute-start.7 = (bf16[96,1024]{1,0:T(8,128)(2,1)S(1)}, bf16[96,1024]{1,0:T(8,128)(2,1)S(1)}, u32[]{:S(2)}, u32[]{:S(2)}) collective-permute-start(bf16[96,1024]{1,0:T(8,128)(2,1)S(1)} %collective-permute-done.6.refs_3_), channel_id=1, source_target_pairs={{0,1},{1,0},{2,3},{3,2},{4,5},{5,4},{6,7},{7,6},{8,9},{9,8},{10,11... | collective-permute-start | bytes 589832 | tf_op jit(solution)/shard_map/ppermute | solution.py:263
  38.1 9.4 %collective-permute-start.9 = (bf16[96,1024]{1,0:T(8,128)(2,1)S(1)}, bf16[96,1024]{1,0:T(8,128)(2,1)S(1)}, u32[]{:S(2)}, u32[]{:S(2)}) collective-permute-start(bf16[96,1024]{1,0:T(8,128)(2,1)S(1)} %collective-permute-done.8.refs_5_), channel_id=1, source_target_pairs={{0,1},{1,0},{2,3},{3,2},{4,5},{5,4},{6,7},{7,6},{8,9},{9,8},{10,11... | collective-permute-start | bytes 589832 | tf_op jit(solution)/shard_map/ppermute | solution.py:263
  39.2 0.7 %copy-start.5 = (s32[31,128]{1,0:T(8,128)S(1)}, s32[31,128]{1,0:T(8,128)}, u32[]{:S(2)}) copy-start(s32[31,128]{1,0:T(8,128)} %upper_ref.1) | copy-start | bytes 47620
  41.2 0.7 copy-start.6
  41.9 24.0 %copy-start.3 = (f32[1024,32]{0,1:T(8,128)S(1)}, f32[1024,32]{0,1:T(8,128)}, u32[]{:S(2)}) copy-start(f32[1024,32]{0,1:T(8,128)} %param.8) | copy-start | bytes 393220
  65.8 0.9 %copy-start.4 = (f32[32,1024]{1,0:T(8,128)S(1)}, f32[32,1024]{1,0:T(8,128)}, u32[]{:S(2)}) copy-start(f32[32,1024]{1,0:T(8,128)} %get-tuple-element.20.image_ref) | copy-start | bytes 393220

commit v6 on v5

--- a/solution.py
+++ b/solution.py
@@ -69,16 +69,16 @@
     return sum(sums[1:], sums[0])
 
 
-def skeleton_body(pick_ref, points_ref, residual_ref, block_ref, right_ref):
-    depth, count = points_ref.shape
+def skeleton_body(depth, pick_ref, near_ref, block_ref, right_ref):
+    count = near_ref.shape[1]
     rank = pick_ref.shape[1]
-    points = points_ref[...]
+    points = near_ref[:depth]
     onehot = (lax.broadcasted_iota(jnp.int32, (count, rank), 0) == pick_ref[...]).astype(F32).astype(BF)
     chosen = jnp.dot(points, onehot, preferred_element_type=F32).astype(BF)
     right = jnp.concatenate([points, right_extra(points)], axis=0)
     tile = kernel_of(left_block(chosen), right, depth).astype(BF)
     weights = lax.dot_general(
-        residual_ref[...].astype(BF), tile, NT, preferred_element_type=F32
+        near_ref[depth:], tile, NT, preferred_element_type=F32
     ) * (1.0 / math.sqrt(count))
     block = jnp.concatenate([chosen, weights.astype(BF)], axis=0)
     for copy in range(block_ref.shape[0]):
@@ -86,10 +86,11 @@
     right_ref[...] = right
 
 
-def tree_nodes(depth, pick_ref, tree_ref, nodes):
+def tree_nodes(depth, upper_ref, tree_ref, nodes):
     rank = tree_ref.shape[2]
+    lanes = lax.broadcasted_iota(jnp.int32, (2 * rank, rank), 0)
     both = [jnp.concatenate([tree_ref[2 * n + 1], tree_ref[2 * n + 2]], axis=1) for n in nodes]
-    picks = [pick_ref[n] for n in nodes]
+    picks = [(lanes == upper_ref[pl.ds(n, 1), :]).astype(F32).astype(BF) for n in nodes]
     chosen = [
         jnp.dot(b[:depth], pick, preferred_element_type=F32).astype(BF) for b, pick in zip(both, picks)
     ]
@@ -110,24 +111,16 @@
         tree_ref[node] = block
 
 
-def own_body(leaf_dev, depth, upper_ref, right_ref, own_ref, part_ref, pick_ref):
+def own_body(leaf_dev, depth, right_ref, own_ref, part_ref):
     leaf = right_ref.shape[1] // leaf_dev
-    nodes, rank = upper_ref.shape
     for at in range(leaf_dev):
         where = slice(at * leaf, (at + 1) * leaf)
         part_ref[:, where] = fields([own_ref[:, where]], right_ref[:, where], depth) * (
             1.0 / math.sqrt(leaf)
         )
-    lanes = lax.broadcasted_iota(jnp.int32, (2 * rank, rank), 0)
-
-    def pick(node, carry):
-        pick_ref[node] = (lanes == upper_ref[pl.ds(node, 1), :]).astype(F32).astype(BF)
-        return carry
-
-    lax.fori_loop(0, nodes, pick, 0)
-
-
-def tree_body(leaf_dev, depth, far_ref, pick_ref, right_ref, own_ref, *refs):
+
+
+def tree_body(leaf_dev, depth, far_ref, upper_ref, right_ref, own_ref, *refs):
     part_refs, out_ref, tree_ref = refs[:-2], refs[-2], refs[-1]
     row_total = len(part_refs)
     column_total = part_refs[0].shape[0]
@@ -147,7 +140,7 @@
         size = min(count, GROUP)
 
         def level(step, carry, low=low, size=size):
-            tree_nodes(depth, pick_ref, tree_ref, [low + step * size + k for k in range(size)])
+            tree_nodes(depth, upper_ref, tree_ref, [low + step * size + k for k in range(size)])
             return carry
 
         if count == size:
@@ -169,8 +162,8 @@
 
 
 def near_body(leaf_dev, depth, near_ref, right_ref, part_ref, residual_ref, *refs):
-    block_refs = refs[:-4]
-    image_ref, small_ref, held, sems = refs[-4:]
+    block_refs = refs[:-5]
+    image_ref, kept_ref, small_ref, held, sems = refs[-5:]
     leaf = right_ref.shape[1] // leaf_dev
     near = near_ref.shape[1]
     mine = lax.axis_index("gy")
@@ -201,6 +194,7 @@
             + total * (1.0 / math.sqrt(leaf))
         )
     image = image_ref[...]
+    kept_ref[...] = image
     gram = lax.dot_general(image, image, NT, precision=FULL, preferred_element_type=F32)
     cross = lax.dot_general(image, residual_ref[...], NT, precision=FULL, preferred_element_type=F32)
     half = gram.shape[0] // 2
@@ -264,26 +258,28 @@
 
     near_blocks[top] = send(top, near_block)
     near_blocks[1] = send(1, near_block)
+    near_blocks[2] = send(2, near_block)
     deep = depth + EXTRA
 
     blocks, right = pl.pallas_call(
-        skeleton_body,
+        functools.partial(skeleton_body, depth),
         out_shape=(
             jax.ShapeDtypeStruct((column_total, depth + width, rank), BF),
             jax.ShapeDtypeStruct((deep, count), BF),
         ),
-        in_specs=vmem(3),
+        in_specs=vmem(2),
         out_specs=tuple(vmem(2)),
         compiler_params=pltpu.CompilerParams(vmem_limit_bytes=GRANT),
     name="skeleton",
-    )(node_skeleton, points_t, residual_t)
+    )(node_skeleton, near_block)
     mine = lax.all_to_all(blocks, "gy", 0, 0)
     mine, late_block = lax.optimization_barrier((mine, near_block))
     for step in range(top + 2, column_total, 2):
         near_blocks[step] = send(step, late_block)
     near_blocks[top + 1] = send(1, near_blocks[top])
     for step in range(2, top, 2):
-        near_blocks[step] = send(step, near_block)
+        if step > 2:
+            near_blocks[step] = send(step, near_block)
         near_blocks[step + 1] = send(step, near_blocks[1])
     for step in range(top + 2, column_total, 2):
         near_blocks[step + 1] = send(1, near_blocks[step])
@@ -294,17 +290,14 @@
         parts.update({slot ^ step: lax.ppermute(part, "gx", swap) for slot, part in parts.items()})
         step //= 2
     parts = [parts[slot] for slot in range(row_total)]
-    own_part, picks = pl.pallas_call(
+    own_part = pl.pallas_call(
         functools.partial(own_body, leaf_dev, depth),
-        out_shape=(
-            jax.ShapeDtypeStruct((width, count), F32),
-            jax.ShapeDtypeStruct((device_total - 1, 2 * rank, rank), BF),
-        ),
-        in_specs=vmem(3),
-        out_specs=tuple(vmem(2)),
+        out_shape=jax.ShapeDtypeStruct((width, count), F32),
+        in_specs=vmem(2),
+        out_specs=vmem(1)[0],
         compiler_params=pltpu.CompilerParams(vmem_limit_bytes=GRANT),
         name="own",
-    )(upper_skeleton, right, near_block)
+    )(right, near_block)
     partial_t = pl.pallas_call(
         functools.partial(tree_body, leaf_dev, depth),
         out_shape=jax.ShapeDtypeStruct((width, count), F32),
@@ -315,10 +308,11 @@
         ],
         compiler_params=pltpu.CompilerParams(vmem_limit_bytes=GRANT),
     name="tree",
-    )(far_nodes, picks, right, own_part, *parts)
-    image_t, small = pl.pallas_call(
+    )(far_nodes, upper_skeleton, right, own_part, *parts)
+    image_t, kept_t, small = pl.pallas_call(
         functools.partial(near_body, leaf_dev, depth),
         out_shape=(
+            jax.ShapeDtypeStruct((width, count), F32),
             jax.ShapeDtypeStruct((width, count), F32),
             jax.ShapeDtypeStruct((device_total, width // 2, 4 * width), F32),
         ),
@@ -326,7 +320,7 @@
             pl.BlockSpec(memory_space=pltpu.SMEM),
             *vmem(3 + column_total - 1),
         ],
-        out_specs=tuple(vmem(2)),
+        out_specs=tuple(vmem(3)),
         scratch_shapes=[
             pltpu.VMEM((leaf_dev * near, depth + width, leaf), BF),
             pltpu.SemaphoreType.DMA((leaf_dev * near,)),
@@ -342,7 +336,7 @@
         out_specs=tuple(vmem(2)),
         compiler_params=pltpu.CompilerParams(vmem_limit_bytes=GRANT),
         name="solve",
-    )(small, solution_t, residual_t, image_t)
+    )(small, solution_t, residual_t, kept_t)
     return (solution_next.T, residual_next.T, image_t.T)
 
 

time: 69.2 us -> 65.4 us (0.945)
  blocking collectives: 13.9 us -> 29.1 us
  starting transfers between devices: 14.9 us -> 7.6 us
  waiting for transfers between devices: 18 us -> 11.9 us
  local copies, waits for them, and re-layouts: 4.77 us -> 1.27 us
  Pallas kernels: 14.7 us -> 13.5 us
  other arithmetic: 1.87 us -> 0.97 us
    all_to_all x0 -> x1, blocking collectives: none -> 15.1 us  [step_of(): mine = lax.all_to_all(blocks, 'gy', 0, 0)]
    all_to_all x1 -> x0, starting transfers between devices: 7.28 us -> none  [step_of(): mine = lax.all_to_all(blocks, 'gy', 0, 0)]
    all_to_all x1 -> x0, waiting for transfers between devices: 6.06 us -> none  [step_of(): mine = lax.all_to_all(blocks, 'gy', 0, 0)]
    unnamed x18 -> x14, local copies, waits for them, and re-layouts: 4.77 us -> 1.27 us
    pallas_call x2, Pallas kernels: 2.58 us -> 1.4 us  [the longest x1 0.79 us: step_of(): pl.pallas_call(functools.partial(own_body, leaf_dev, depth), out_shape=ja...]
    concatenate x1, other arithmetic: 0.95 us -> 0.02 us  [step_of(): near_block = jnp.concatenate([points_t, residual_t.astype(BF)], axis=0)]
  transfers between devices with their start and end apart: 11 -> 10, of which waited for: 4 -> 3; matrix products, arithmetic and copies ran while one was open for 3% -> 0% of each run, Pallas kernels for 10% -> 10%
where the time goes in v6:
time: 65.4 us; the launch traced here: 65.2 us
  blocking collectives  29.1 us (44%)
  Pallas kernels  13.5 us (21%)
  waiting for transfers between devices  11.9 us (18%)
  starting transfers between devices  7.6 us (12%)
  local copies, waits for them, and re-layouts  1.27 us (2%)
  other arithmetic  0.97 us (1%)
  between operations  0.77 us (1%)
    all_to_all x1, blocking collectives, step_of(): mine = lax.all_to_all(blocks, 'gy', 0, 0)  15.1 us
    all_to_all x1, blocking collectives, step_of(): small = lax.all_to_all(small, ('gx', 'gy'), 0, 0)  14.1 us
    ppermute x7, waiting for transfers between devices, send(): lax.ppermute(block, 'gy', [(i, i ^ step) for i in range(column_total)])  11.5 us
    ppermute x7, starting transfers between devices, send(): lax.ppermute(block, 'gy', [(i, i ^ step) for i in range(column_total)])  6.07 us
    pallas_call x1, Pallas kernels, step_of(): pl.pallas_call(functools.partial(tree_body, leaf_dev, depth), out_shape=j...  5.67 us
    pallas_call x1, Pallas kernels, step_of(): pl.pallas_call(functools.partial(near_body, leaf_dev, depth), out_shape=(...  4.39 us
    pallas_call x1, Pallas kernels, step_of(): pl.pallas_call(solve_body, out_shape=(jax.ShapeDtypeStruct((width, count)...  2.06 us
    ppermute x3, starting transfers between devices, step_of(): lax.ppermute(part, 'gx', swap)  1.53 us
  transfers between devices with their start and end apart: 10, of which 3 were waited for; matrix products, arithmetic and copies ran while one was open for 0% of the time, Pallas kernels for 10%

profile of v6, /device:TPU:0, one launch (start us, length us, event | category | flops | bytes accessed | tf_op | source)
XLA Modules:
  0.0 65.2 jit_solution(10455320976352890747)
XLA Ops:
  0.6 0.0 copy-start.6
  0.6 0.9 %bitcast_convert_fusion = bf16[32,1024]{1,0:T(8,128)(2,1)S(1)} fusion(f32[1024,32]{0,1:T(8,128)} %param.9), kind=kLoop, calls=%fused_computation.1 | loop fusion | flops 32768 | bytes 196608 | tf_op jit(solution)/shard_map/convert_element_type | solution.py:252
  1.6 0.0 copy-done.6
  1.6 0.0 copy-start.5
  1.6 0.6 copy-done.5
  2.3 0.6 skeleton.1
  2.9 15.1 %all_to_all.10.refs_0_ = bf16[8,96,128]{2,1,0:T(8,128)(2,1)S(1)} all-to-all(bf16[8,96,128]{2,1,0:T(8,128)(2,1)S(1)} %get-tuple-element.13), channel_id=1, replica_groups=mesh['gx'=4,'gy'=8] {'gy'}, dimensions={0} | all-to-all | bytes 393216 | tf_op jit(solution)/shard_map/all_to_all | solution.py:275
  17.9 1.5 %collective-permute-start.1 = (bf16[8,96,128]{2,1,0:T(8,128)(2,1)S(1)}, bf16[8,96,128]{2,1,0:T(8,128)(2,1)S(1)}, u32[]{:S(2)}, u32[]{:S(2)}) collective-permute-start(bf16[8,96,128]{2,1,0:T(8,128)(2,1)S(1)} %all_to_all.10.refs_0_), channel_id=1, source_target_pairs={{0,16},{8,24},{16,0},{24,8},{1,17},{9,25},{17,1},{25,9},{2,18},{10... | collective-permute-start | bytes 589832 | tf_op jit(solution)/shard_map/ppermute | solution.py:290
  19.5 1.1 %collective-permute-start.3 = (bf16[96,1024]{1,0:T(8,128)(2,1)S(1)}, bf16[96,1024]{1,0:T(8,128)(2,1)S(1)}, u32[]{:S(2)}, u32[]{:S(2)}) collective-permute-start(bf16[96,1024]{1,0:T(8,128)(2,1)S(1)} %pad_maximum_fusion.near_ref.own_ref), channel_id=1, source_target_pairs={{0,1},{1,0},{2,3},{3,2},{4,5},{5,4},{6,7},{7,6},{8,9},{9,8},{10,11... | collective-permute-start | bytes 589832 | tf_op jit(solution)/shard_map/ppermute | solution.py:257
  20.5 0.0 collective-permute-start.6
  20.5 0.0 collective-permute-start
  20.5 2.7 %collective-permute-start.8 = (bf16[96,1024]{1,0:T(8,128)(2,1)S(1)}, bf16[96,1024]{1,0:T(8,128)(2,1)S(1)}, u32[]{:S(2)}, u32[]{:S(2)}) collective-permute-start(bf16[96,1024]{1,0:T(8,128)(2,1)S(1)} %pad_maximum_fusion.near_ref.own_ref), channel_id=1, source_target_pairs={{0,6},{1,7},{2,4},{3,5},{4,2},{5,3},{6,0},{7,1},{8,14},{9,15},{10,... | collective-permute-start | bytes 589832 | tf_op jit(solution)/shard_map/ppermute | solution.py:257
  23.2 0.4 collective-permute-done.1.refs_2_
  23.6 0.0 collective-permute-start.2
  23.6 1.5 %collective-permute-done.3.refs_0_ = bf16[96,1024]{1,0:T(8,128)(2,1)S(1)} collective-permute-done((bf16[96,1024]{1,0:T(8,128)(2,1)S(1)}, bf16[96,1024]{1,0:T(8,128)(2,1)S(1)}, u32[]{:S(2)}, u32[]{:S(2)}) %collective-permute-start.3) | collective-permute-done | bytes 196640 | tf_op jit(solution)/shard_map/ppermute | solution.py:257
  25.1 0.3 collective-permute-start.4
  25.4 10.0 %collective-permute-done.6.refs_3_ = bf16[96,1024]{1,0:T(8,128)(2,1)S(1)} collective-permute-done((bf16[96,1024]{1,0:T(8,128)(2,1)S(1)}, bf16[96,1024]{1,0:T(8,128)(2,1)S(1)}, u32[]{:S(2)}, u32[]{:S(2)}) %collective-permute-start.6) | collective-permute-done | bytes 196640 | tf_op jit(solution)/shard_map/ppermute | solution.py:257
  35.4 0.0 collective-permute-start.5
  35.4 0.0 collective-permute-done.refs_1_
  35.4 0.9 %collective-permute-start.7 = (bf16[96,1024]{1,0:T(8,128)(2,1)S(1)}, bf16[96,1024]{1,0:T(8,128)(2,1)S(1)}, u32[]{:S(2)}, u32[]{:S(2)}) collective-permute-start(bf16[96,1024]{1,0:T(8,128)(2,1)S(1)} %collective-permute-done.6.refs_3_), channel_id=1, source_target_pairs={{0,1},{1,0},{2,3},{3,2},{4,5},{5,4},{6,7},{7,6},{8,9},{9,8},{10,11... | collective-permute-start | bytes 589832 | tf_op jit(solution)/shard_map/ppermute | solution.py:257
  36.4 0.0 collective-permute-done.8.refs_5_
  36.4 1.1 %collective-permute-start.9 = (bf16[96,1024]{1,0:T(8,128)(2,1)S(1)}, bf16[96,1024]{1,0:T(8,128)(2,1)S(1)}, u32[]{:S(2)}, u32[]{:S(2)}) collective-permute-start(bf16[96,1024]{1,0:T(8,128)(2,1)S(1)} %collective-permute-done.8.refs_5_), channel_id=1, source_target_pairs={{0,1},{1,0},{2,3},{3,2},{4,5},{5,4},{6,7},{7,6},{8,9},{9,8},{10,11... | collective-permute-start | bytes 589832 | tf_op jit(solution)/shard_map/ppermute | solution.py:257
  37.5 0.0 copy-start.2
  37.5 0.0 copy-start.4
  37.5 0.8 %own.1.own_ref = f32[32,1024]{1,0:T(8,128)S(1)} custom-call(bf16[80,1024]{1,0:T(8,128)(2,1)S(1)} %get-tuple-element.12.right_ref, bf16[96,1024]{1,0:T(8,128)(2,1)S(1)} %pad_maximum_fusion.near_ref.own_ref), custom_call_target="tpu_custom_call" | custom-call | tf_op jit(solution)/shard_map/own/pallas_call | solution.py:293
  38.3 0.0 copy-start
  38.3 0.0 collective-permute-done.2.refs_3_
  38.3 0.0 copy-done.2
  38.3 0.0 copy-done.4
  38.3 5.7 %tree.1.part_ref = f32[32,1024]{1,0:T(8,128)S(1)} custom-call(s32[2,16]{1,0:T(2,128)S(1)} %copy-done.4, s32[31,128]{1,0:T(8,128)S(1)} %copy-done.2, bf16[80,1024]{1,0:T(8,128)(2,1)S(1)} %get-tuple-element.12.right_ref, f32[32,1024]{1,0:T(8,128)S(1)} %own.1.own_ref, bf16[8,96,128]{2,1,0:T(8,128)(2,1)S(1)} %all_to_all.10.refs_0_, ...), custom_call_target="tpu_custom_call" | custom-call | tf_op jit(solution)/shard_map/tree/pallas_call | solution.py:301
  44.0 0.0 copy-start.3
  44.0 0.0 collective-permute-done.4.refs_1_
  44.0 0.0 collective-permute-done.5.refs_2_
  44.0 0.0 collective-permute-done.7.refs_4_
  44.0 0.0 collective-permute-done.9.refs_6_
  44.0 0.0 copy-done
  44.0 0.6 copy-done.3
  44.7 4.4 %near.1 = (f32[32,1024]{1,0:T(8,128)}, f32[32,1024]{1,0:T(8,128)S(1)}, f32[32,16,128]{2,1,0:T(8,128)S(1)}) custom-call(s32[2,4]{1,0:T(2,128)S(1)} %copy-done.3, bf16[80,1024]{1,0:T(8,128)(2,1)S(1)} %get-tuple-element.12.right_ref, f32[32,1024]{1,0:T(8,128)S(1)} %tree.1.part_ref, f32[32,1024]{1,0:T(8,128)S(1)} %bitcast.7, ...), custom_call_target="tpu_custom_call" | custom-call | tf_op jit(solution)/shard_map/near/pallas_call | solution.py:312
  49.1 0.0 copy-start.1
  49.1 14.1 %all_to_all.11.small_ref = f32[32,16,128]{2,1,0:T(8,128)S(1)} all-to-all(f32[32,16,128]{2,1,0:T(8,128)S(1)} %get-tuple-element.16), channel_id=1, replica_groups=mesh['gx'=4,'gy'=8] {'gx','gy'}, dimensions={0} | all-to-all | bytes 524288 | tf_op jit(solution)/shard_map/all_to_all | solution.py:331
  63.1 0.0 copy-done.1
  63.1 2.1 %solve.1 = (f32[32,1024]{1,0:T(8,128)}, f32[32,1024]{1,0:T(8,128)}) custom-call(f32[32,16,128]{2,1,0:T(8,128)S(1)} %all_to_all.11.small_ref, f32[32,1024]{1,0:T(8,128)S(1)} %bitcast.9, f32[32,1024]{1,0:T(8,128)S(1)} %bitcast.8, f32[32,1024]{1,0:T(8,128)S(1)} %get-tuple-element.17.image_ref), custom_call_target="tpu_custom_call" | custom-call | tf_op jit(solution)/shard_map/solve/pallas_call | solution.py:332
  (1 shorter events, 0.0 us)
Async XLA Ops:
  0.6 1.0 %copy-start.6 = (bf16[1024,64]{0,1:T(8,128)(2,1)S(1)}, bf16[1024,64]{0,1:T(8,128)(2,1)}, u32[]{:S(2)}) copy-start(bf16[1024,64]{0,1:T(8,128)(2,1)} %param.7) | copy-start | bytes 393220
  1.6 0.7 %copy-start.5 = (s32[1,128]{1,0:T(1,128)S(1)}, s32[1,128]{1,0:T(1,128)}, u32[]{:S(2)}) copy-start(s32[1,128]{1,0:T(1,128)} %pick_ref.1) | copy-start | bytes 1540
  17.9 5.7 %collective-permute-start.1 = (bf16[8,96,128]{2,1,0:T(8,128)(2,1)S(1)}, bf16[8,96,128]{2,1,0:T(8,128)(2,1)S(1)}, u32[]{:S(2)}, u32[]{:S(2)}) collective-permute-start(bf16[8,96,128]{2,1,0:T(8,128)(2,1)S(1)} %all_to_all.10.refs_0_), channel_id=1, source_target_pairs={{0,16},{8,24},{16,0},{24,8},{1,17},{9,25},{17,1},{25,9},{2,18},{10... | collective-permute-start | bytes 589832 | tf_op jit(solution)/shard_map/ppermute | solution.py:290
  19.5 5.7 %collective-permute-start.3 = (bf16[96,1024]{1,0:T(8,128)(2,1)S(1)}, bf16[96,1024]{1,0:T(8,128)(2,1)S(1)}, u32[]{:S(2)}, u32[]{:S(2)}) collective-permute-start(bf16[96,1024]{1,0:T(8,128)(2,1)S(1)} %pad_maximum_fusion.near_ref.own_ref), channel_id=1, source_target_pairs={{0,1},{1,0},{2,3},{3,2},{4,5},{5,4},{6,7},{7,6},{8,9},{9,8},{10,11... | collective-permute-start | bytes 589832 | tf_op jit(solution)/shard_map/ppermute | solution.py:257
  20.5 14.9 %collective-permute-start.6 = (bf16[96,1024]{1,0:T(8,128)(2,1)S(1)}, bf16[96,1024]{1,0:T(8,128)(2,1)S(1)}, u32[]{:S(2)}, u32[]{:S(2)}) collective-permute-start(bf16[96,1024]{1,0:T(8,128)(2,1)S(1)} %pad_maximum_fusion.near_ref.own_ref), channel_id=1, source_target_pairs={{0,4},{1,5},{2,6},{3,7},{4,0},{5,1},{6,2},{7,3},{8,12},{9,13},{10,... | collective-permute-start | bytes 589832 | tf_op jit(solution)/shard_map/ppermute | solution.py:257
  20.5 14.9 %collective-permute-start = (bf16[8,96,128]{2,1,0:T(8,128)(2,1)S(1)}, bf16[8,96,128]{2,1,0:T(8,128)(2,1)S(1)}, u32[]{:S(2)}, u32[]{:S(2)}) collective-permute-start(bf16[8,96,128]{2,1,0:T(8,128)(2,1)S(1)} %all_to_all.10.refs_0_), channel_id=1, source_target_pairs={{0,8},{8,0},{16,24},{24,16},{1,9},{9,1},{17,25},{25,17},{2,10},{10... | collective-permute-start | bytes 589832 | tf_op jit(solution)/shard_map/ppermute | solution.py:290
  20.5 15.8 %collective-permute-start.8 = (bf16[96,1024]{1,0:T(8,128)(2,1)S(1)}, bf16[96,1024]{1,0:T(8,128)(2,1)S(1)}, u32[]{:S(2)}, u32[]{:S(2)}) collective-permute-start(bf16[96,1024]{1,0:T(8,128)(2,1)S(1)} %pad_maximum_fusion.near_ref.own_ref), channel_id=1, source_target_pairs={{0,6},{1,7},{2,4},{3,5},{4,2},{5,3},{6,0},{7,1},{8,14},{9,15},{10,... | collective-permute-start | bytes 589832 | tf_op jit(solution)/shard_map/ppermute | solution.py:257
  23.6 14.7 %collective-permute-start.2 = (bf16[8,96,128]{2,1,0:T(8,128)(2,1)S(1)}, bf16[8,96,128]{2,1,0:T(8,128)(2,1)S(1)}, u32[]{:S(2)}, u32[]{:S(2)}) collective-permute-start(bf16[8,96,128]{2,1,0:T(8,128)(2,1)S(1)} %collective-permute-done.1.refs_2_), channel_id=1, source_target_pairs={{0,8},{8,0},{16,24},{24,16},{1,9},{9,1},{17,25},{25,17},{2,10},{10... | collective-permute-start | bytes 589832 | tf_op jit(solution)/shard_map/ppermute | solution.py:290
  25.1 18.9 %collective-permute-start.4 = (bf16[96,1024]{1,0:T(8,128)(2,1)S(1)}, bf16[96,1024]{1,0:T(8,128)(2,1)S(1)}, u32[]{:S(2)}, u32[]{:S(2)}) collective-permute-start(bf16[96,1024]{1,0:T(8,128)(2,1)S(1)} %pad_maximum_fusion.near_ref.own_ref), channel_id=1, source_target_pairs={{0,2},{1,3},{2,0},{3,1},{4,6},{5,7},{6,4},{7,5},{8,10},{9,11},{10,... | collective-permute-start | bytes 589832 | tf_op jit(solution)/shard_map/ppermute | solution.py:257
  35.4 8.6 %collective-permute-start.5 = (bf16[96,1024]{1,0:T(8,128)(2,1)S(1)}, bf16[96,1024]{1,0:T(8,128)(2,1)S(1)}, u32[]{:S(2)}, u32[]{:S(2)}) collective-permute-start(bf16[96,1024]{1,0:T(8,128)(2,1)S(1)} %collective-permute-done.3.refs_0_), channel_id=1, source_target_pairs={{0,2},{1,3},{2,0},{3,1},{4,6},{5,7},{6,4},{7,5},{8,10},{9,11},{10,... | collective-permute-start | bytes 589832 | tf_op jit(solution)/shard_map/ppermute | solution.py:257
  35.4 8.6 %collective-permute-start.7 = (bf16[96,1024]{1,0:T(8,128)(2,1)S(1)}, bf16[96,1024]{1,0:T(8,128)(2,1)S(1)}, u32[]{:S(2)}, u32[]{:S(2)}) collective-permute-start(bf16[96,1024]{1,0:T(8,128)(2,1)S(1)} %collective-permute-done.6.refs_3_), channel_id=1, source_target_pairs={{0,1},{1,0},{2,3},{3,2},{4,5},{5,4},{6,7},{7,6},{8,9},{9,8},{10,11... | collective-permute-start | bytes 589832 | tf_op jit(solution)/shard_map/ppermute | solution.py:257
  36.4 7.7 %collective-permute-start.9 = (bf16[96,1024]{1,0:T(8,128)(2,1)S(1)}, bf16[96,1024]{1,0:T(8,128)(2,1)S(1)}, u32[]{:S(2)}, u32[]{:S(2)}) collective-permute-start(bf16[96,1024]{1,0:T(8,128)(2,1)S(1)} %collective-permute-done.8.refs_5_), channel_id=1, source_target_pairs={{0,1},{1,0},{2,3},{3,2},{4,5},{5,4},{6,7},{7,6},{8,9},{9,8},{10,11... | collective-permute-start | bytes 589832 | tf_op jit(solution)/shard_map/ppermute | solution.py:257
  37.5 0.8 %copy-start.2 = (s32[31,128]{1,0:T(8,128)S(1)}, s32[31,128]{1,0:T(8,128)}, u32[]{:S(2)}) copy-start(s32[31,128]{1,0:T(8,128)} %upper_ref.1) | copy-start | bytes 47620
  37.5 0.8 %copy-start.4 = (s32[2,16]{1,0:T(2,128)S(1)}, s32[2,16]{1,0:T(2,128)}, u32[]{:S(2)}) copy-start(s32[2,16]{1,0:T(2,128)} %far_ref.1) | copy-start | bytes 388
  38.3 5.8 %copy-start = (f32[1024,32]{0,1:T(8,128)S(1)}, f32[1024,32]{0,1:T(8,128)}, u32[]{:S(2)}) copy-start(f32[1024,32]{0,1:T(8,128)} %param.9) | copy-start | bytes 393220
  44.0 0.7 %copy-start.3 = (s32[2,4]{1,0:T(2,128)S(1)}, s32[2,4]{1,0:T(2,128)}, u32[]{:S(2)}) copy-start(s32[2,4]{1,0:T(2,128)} %near_ref.1) | copy-start | bytes 100
  49.1 14.1 %copy-start.1 = (f32[1024,32]{0,1:T(8,128)S(1)}, f32[1024,32]{0,1:T(8,128)}, u32[]{:S(2)}) copy-start(f32[1024,32]{0,1:T(8,128)} %param.8) | copy-start | bytes 393220

commit v7 on v6

--- a/solution.py
+++ b/solution.py
@@ -120,7 +120,7 @@
         )
 
 
-def tree_body(leaf_dev, depth, far_ref, upper_ref, right_ref, own_ref, *refs):
+def tree_body(leaf_dev, depth, far_ref, near_ref, upper_ref, right_ref, own_ref, *refs):
     part_refs, out_ref, tree_ref = refs[:-2], refs[-2], refs[-1]
     row_total = len(part_refs)
     column_total = part_refs[0].shape[0]
@@ -301,14 +301,14 @@
     partial_t = pl.pallas_call(
         functools.partial(tree_body, leaf_dev, depth),
         out_shape=jax.ShapeDtypeStruct((width, count), F32),
-        in_specs=[pl.BlockSpec(memory_space=pltpu.SMEM), *vmem(3 + row_total)],
+        in_specs=[*[pl.BlockSpec(memory_space=pltpu.SMEM)] * 2, *vmem(3 + row_total)],
         out_specs=vmem(1)[0],
         scratch_shapes=[
             pltpu.VMEM((2 * device_total - 1, deep + width, rank), BF),
         ],
         compiler_params=pltpu.CompilerParams(vmem_limit_bytes=GRANT),
     name="tree",
-    )(far_nodes, upper_skeleton, right, own_part, *parts)
+    )(far_nodes, near_leaves, upper_skeleton, right, own_part, *parts)
     image_t, kept_t, small = pl.pallas_call(
         functools.partial(near_body, leaf_dev, depth),
         out_shape=(

time: 65.4 us -> 65.4 us (level)
  no operation moved by 1% of the time
where the time goes in v7:
time: 65.4 us; the launch traced here: 65.2 us
  blocking collectives  29.7 us (45%)
  Pallas kernels  13.5 us (21%)
  waiting for transfers between devices  11.9 us (18%)
  starting transfers between devices  7.6 us (12%)
  other arithmetic  0.97 us (1%)
  between operations  0.77 us (1%)
  local copies, waits for them, and re-layouts  0.66 us (1%)
    all_to_all x1, blocking collectives, step_of(): mine = lax.all_to_all(blocks, 'gy', 0, 0)  15.1 us
    all_to_all x1, blocking collectives, step_of(): small = lax.all_to_all(small, ('gx', 'gy'), 0, 0)  14.6 us
    ppermute x7, waiting for transfers between devices, send(): lax.ppermute(block, 'gy', [(i, i ^ step) for i in range(column_total)])  11.5 us
    ppermute x7, starting transfers between devices, send(): lax.ppermute(block, 'gy', [(i, i ^ step) for i in range(column_total)])  6.07 us
    pallas_call x1, Pallas kernels, step_of(): pl.pallas_call(functools.partial(tree_body, leaf_dev, depth), out_shape=j...  5.67 us
    pallas_call x1, Pallas kernels, step_of(): pl.pallas_call(functools.partial(near_body, leaf_dev, depth), out_shape=(...  4.41 us
    pallas_call x1, Pallas kernels, step_of(): pl.pallas_call(solve_body, out_shape=(jax.ShapeDtypeStruct((width, count)...  2.06 us
    ppermute x3, starting transfers between devices, step_of(): lax.ppermute(part, 'gx', swap)  1.53 us
  transfers between devices with their start and end apart: 10, of which 3 were waited for; matrix products, arithmetic and copies ran while one was open for 0% of the time, Pallas kernels for 10%

profile of v7, /device:TPU:0, one launch (start us, length us, event | category | flops | bytes accessed | tf_op | source)
XLA Modules:
  0.0 65.2 jit_solution(12863624944534310104)
XLA Ops:
  0.6 0.0 copy-start.6
  0.6 0.9 %bitcast_convert_fusion = bf16[32,1024]{1,0:T(8,128)(2,1)S(1)} fusion(f32[1024,32]{0,1:T(8,128)} %param.9), kind=kLoop, calls=%fused_computation.1 | loop fusion | flops 32768 | bytes 196608 | tf_op jit(solution)/shard_map/convert_element_type | solution.py:252
  1.6 0.0 copy-done.6
  1.6 0.0 copy-start.5
  1.6 0.6 copy-done.5
  2.3 0.6 skeleton.1
  2.9 15.1 %all_to_all.10.refs_0_ = bf16[8,96,128]{2,1,0:T(8,128)(2,1)S(1)} all-to-all(bf16[8,96,128]{2,1,0:T(8,128)(2,1)S(1)} %get-tuple-element.13), channel_id=1, replica_groups=mesh['gx'=4,'gy'=8] {'gy'}, dimensions={0} | all-to-all | bytes 393216 | tf_op jit(solution)/shard_map/all_to_all | solution.py:275
  17.9 1.5 %collective-permute-start.1 = (bf16[8,96,128]{2,1,0:T(8,128)(2,1)S(1)}, bf16[8,96,128]{2,1,0:T(8,128)(2,1)S(1)}, u32[]{:S(2)}, u32[]{:S(2)}) collective-permute-start(bf16[8,96,128]{2,1,0:T(8,128)(2,1)S(1)} %all_to_all.10.refs_0_), channel_id=1, source_target_pairs={{0,16},{8,24},{16,0},{24,8},{1,17},{9,25},{17,1},{25,9},{2,18},{10... | collective-permute-start | bytes 589832 | tf_op jit(solution)/shard_map/ppermute | solution.py:290
  19.5 1.1 %collective-permute-start.3 = (bf16[96,1024]{1,0:T(8,128)(2,1)S(1)}, bf16[96,1024]{1,0:T(8,128)(2,1)S(1)}, u32[]{:S(2)}, u32[]{:S(2)}) collective-permute-start(bf16[96,1024]{1,0:T(8,128)(2,1)S(1)} %pad_maximum_fusion.near_ref.own_ref), channel_id=1, source_target_pairs={{0,1},{1,0},{2,3},{3,2},{4,5},{5,4},{6,7},{7,6},{8,9},{9,8},{10,11... | collective-permute-start | bytes 589832 | tf_op jit(solution)/shard_map/ppermute | solution.py:257
  20.5 0.0 collective-permute-start.6
  20.5 0.0 collective-permute-start
  20.5 2.7 %collective-permute-start.8 = (bf16[96,1024]{1,0:T(8,128)(2,1)S(1)}, bf16[96,1024]{1,0:T(8,128)(2,1)S(1)}, u32[]{:S(2)}, u32[]{:S(2)}) collective-permute-start(bf16[96,1024]{1,0:T(8,128)(2,1)S(1)} %pad_maximum_fusion.near_ref.own_ref), channel_id=1, source_target_pairs={{0,6},{1,7},{2,4},{3,5},{4,2},{5,3},{6,0},{7,1},{8,14},{9,15},{10,... | collective-permute-start | bytes 589832 | tf_op jit(solution)/shard_map/ppermute | solution.py:257
  23.2 0.4 collective-permute-done.1.refs_2_
  23.6 0.0 collective-permute-start.2
  23.6 1.5 %collective-permute-done.3.refs_0_ = bf16[96,1024]{1,0:T(8,128)(2,1)S(1)} collective-permute-done((bf16[96,1024]{1,0:T(8,128)(2,1)S(1)}, bf16[96,1024]{1,0:T(8,128)(2,1)S(1)}, u32[]{:S(2)}, u32[]{:S(2)}) %collective-permute-start.3) | collective-permute-done | bytes 196640 | tf_op jit(solution)/shard_map/ppermute | solution.py:257
  25.1 0.3 collective-permute-start.4
  25.4 10.0 %collective-permute-done.6.refs_3_ = bf16[96,1024]{1,0:T(8,128)(2,1)S(1)} collective-permute-done((bf16[96,1024]{1,0:T(8,128)(2,1)S(1)}, bf16[96,1024]{1,0:T(8,128)(2,1)S(1)}, u32[]{:S(2)}, u32[]{:S(2)}) %collective-permute-start.6) | collective-permute-done | bytes 196640 | tf_op jit(solution)/shard_map/ppermute | solution.py:257
  35.4 0.0 collective-permute-start.5
  35.4 0.0 collective-permute-done.refs_1_
  35.4 0.9 %collective-permute-start.7 = (bf16[96,1024]{1,0:T(8,128)(2,1)S(1)}, bf16[96,1024]{1,0:T(8,128)(2,1)S(1)}, u32[]{:S(2)}, u32[]{:S(2)}) collective-permute-start(bf16[96,1024]{1,0:T(8,128)(2,1)S(1)} %collective-permute-done.6.refs_3_), channel_id=1, source_target_pairs={{0,1},{1,0},{2,3},{3,2},{4,5},{5,4},{6,7},{7,6},{8,9},{9,8},{10,11... | collective-permute-start | bytes 589832 | tf_op jit(solution)/shard_map/ppermute | solution.py:257
  36.4 0.0 collective-permute-done.8.refs_5_
  36.4 1.1 %collective-permute-start.9 = (bf16[96,1024]{1,0:T(8,128)(2,1)S(1)}, bf16[96,1024]{1,0:T(8,128)(2,1)S(1)}, u32[]{:S(2)}, u32[]{:S(2)}) collective-permute-start(bf16[96,1024]{1,0:T(8,128)(2,1)S(1)} %collective-permute-done.8.refs_5_), channel_id=1, source_target_pairs={{0,1},{1,0},{2,3},{3,2},{4,5},{5,4},{6,7},{7,6},{8,9},{9,8},{10,11... | collective-permute-start | bytes 589832 | tf_op jit(solution)/shard_map/ppermute | solution.py:257
  37.5 0.0 copy-start.2
  37.5 0.0 copy-start.3
  37.5 0.0 copy-start.4
  37.5 0.8 %own.1.own_ref = f32[32,1024]{1,0:T(8,128)S(1)} custom-call(bf16[80,1024]{1,0:T(8,128)(2,1)S(1)} %get-tuple-element.12.right_ref, bf16[96,1024]{1,0:T(8,128)(2,1)S(1)} %pad_maximum_fusion.near_ref.own_ref), custom_call_target="tpu_custom_call" | custom-call | tf_op jit(solution)/shard_map/own/pallas_call | solution.py:293
  38.3 0.0 copy-start
  38.3 0.0 collective-permute-done.2.refs_3_
  38.3 0.0 copy-done.2
  38.3 0.0 copy-done.3
  38.3 0.0 copy-done.4
  38.3 5.7 %tree.1.part_ref = f32[32,1024]{1,0:T(8,128)S(1)} custom-call(s32[2,16]{1,0:T(2,128)S(1)} %copy-done.4, s32[2,4]{1,0:T(2,128)S(1)} %copy-done.3, s32[31,128]{1,0:T(8,128)S(1)} %copy-done.2, bf16[80,1024]{1,0:T(8,128)(2,1)S(1)} %get-tuple-element.12.right_ref, f32[32,1024]{1,0:T(8,128)S(1)} %own.1.own_ref, bf16[8,96,128]{2,1,0:T(8,128)(2,1)S(1)} %all_to_all.10.refs_0_, ...), custom_call_target="tpu_custom_call" | custom-call | tf_op jit(solution)/shard_map/tree/pallas_call | solution.py:301
  44.0 0.0 collective-permute-done.4.refs_1_
  44.0 0.0 collective-permute-done.5.refs_2_
  44.0 0.0 collective-permute-done.7.refs_4_
  44.0 0.0 collective-permute-done.9.refs_6_
  44.0 0.0 copy-done
  44.0 4.4 %near.1 = (f32[32,1024]{1,0:T(8,128)}, f32[32,1024]{1,0:T(8,128)S(1)}, f32[32,16,128]{2,1,0:T(8,128)S(1)}) custom-call(s32[2,4]{1,0:T(2,128)S(1)} %copy-done.3, bf16[80,1024]{1,0:T(8,128)(2,1)S(1)} %get-tuple-element.12.right_ref, f32[32,1024]{1,0:T(8,128)S(1)} %tree.1.part_ref, f32[32,1024]{1,0:T(8,128)S(1)} %bitcast.7, ...), custom_call_target="tpu_custom_call" | custom-call | tf_op jit(solution)/shard_map/near/pallas_call | solution.py:312
  48.5 0.0 copy-start.1
  48.5 14.6 %all_to_all.11.small_ref = f32[32,16,128]{2,1,0:T(8,128)S(1)} all-to-all(f32[32,16,128]{2,1,0:T(8,128)S(1)} %get-tuple-element.16), channel_id=1, replica_groups=mesh['gx'=4,'gy'=8] {'gx','gy'}, dimensions={0} | all-to-all | bytes 524288 | tf_op jit(solution)/shard_map/all_to_all | solution.py:331
  63.1 0.0 copy-done.1
  63.1 2.1 %solve.1 = (f32[32,1024]{1,0:T(8,128)}, f32[32,1024]{1,0:T(8,128)}) custom-call(f32[32,16,128]{2,1,0:T(8,128)S(1)} %all_to_all.11.small_ref, f32[32,1024]{1,0:T(8,128)S(1)} %bitcast.9, f32[32,1024]{1,0:T(8,128)S(1)} %bitcast.8, f32[32,1024]{1,0:T(8,128)S(1)} %get-tuple-element.17.image_ref), custom_call_target="tpu_custom_call" | custom-call | tf_op jit(solution)/shard_map/solve/pallas_call | solution.py:332
  (1 shorter events, 0.0 us)
Async XLA Ops:
  0.6 1.0 %copy-start.6 = (bf16[1024,64]{0,1:T(8,128)(2,1)S(1)}, bf16[1024,64]{0,1:T(8,128)(2,1)}, u32[]{:S(2)}) copy-start(bf16[1024,64]{0,1:T(8,128)(2,1)} %param.7) | copy-start | bytes 393220
  1.6 0.7 %copy-start.5 = (s32[1,128]{1,0:T(1,128)S(1)}, s32[1,128]{1,0:T(1,128)}, u32[]{:S(2)}) copy-start(s32[1,128]{1,0:T(1,128)} %pick_ref.1) | copy-start | bytes 1540
  17.9 5.7 %collective-permute-start.1 = (bf16[8,96,128]{2,1,0:T(8,128)(2,1)S(1)}, bf16[8,96,128]{2,1,0:T(8,128)(2,1)S(1)}, u32[]{:S(2)}, u32[]{:S(2)}) collective-permute-start(bf16[8,96,128]{2,1,0:T(8,128)(2,1)S(1)} %all_to_all.10.refs_0_), channel_id=1, source_target_pairs={{0,16},{8,24},{16,0},{24,8},{1,17},{9,25},{17,1},{25,9},{2,18},{10... | collective-permute-start | bytes 589832 | tf_op jit(solution)/shard_map/ppermute | solution.py:290
  19.5 5.7 %collective-permute-start.3 = (bf16[96,1024]{1,0:T(8,128)(2,1)S(1)}, bf16[96,1024]{1,0:T(8,128)(2,1)S(1)}, u32[]{:S(2)}, u32[]{:S(2)}) collective-permute-start(bf16[96,1024]{1,0:T(8,128)(2,1)S(1)} %pad_maximum_fusion.near_ref.own_ref), channel_id=1, source_target_pairs={{0,1},{1,0},{2,3},{3,2},{4,5},{5,4},{6,7},{7,6},{8,9},{9,8},{10,11... | collective-permute-start | bytes 589832 | tf_op jit(solution)/shard_map/ppermute | solution.py:257
  20.5 14.9 %collective-permute-start.6 = (bf16[96,1024]{1,0:T(8,128)(2,1)S(1)}, bf16[96,1024]{1,0:T(8,128)(2,1)S(1)}, u32[]{:S(2)}, u32[]{:S(2)}) collective-permute-start(bf16[96,1024]{1,0:T(8,128)(2,1)S(1)} %pad_maximum_fusion.near_ref.own_ref), channel_id=1, source_target_pairs={{0,4},{1,5},{2,6},{3,7},{4,0},{5,1},{6,2},{7,3},{8,12},{9,13},{10,... | collective-permute-start | bytes 589832 | tf_op jit(solution)/shard_map/ppermute | solution.py:257
  20.5 14.9 %collective-permute-start = (bf16[8,96,128]{2,1,0:T(8,128)(2,1)S(1)}, bf16[8,96,128]{2,1,0:T(8,128)(2,1)S(1)}, u32[]{:S(2)}, u32[]{:S(2)}) collective-permute-start(bf16[8,96,128]{2,1,0:T(8,128)(2,1)S(1)} %all_to_all.10.refs_0_), channel_id=1, source_target_pairs={{0,8},{8,0},{16,24},{24,16},{1,9},{9,1},{17,25},{25,17},{2,10},{10... | collective-permute-start | bytes 589832 | tf_op jit(solution)/shard_map/ppermute | solution.py:290
  20.5 15.8 %collective-permute-start.8 = (bf16[96,1024]{1,0:T(8,128)(2,1)S(1)}, bf16[96,1024]{1,0:T(8,128)(2,1)S(1)}, u32[]{:S(2)}, u32[]{:S(2)}) collective-permute-start(bf16[96,1024]{1,0:T(8,128)(2,1)S(1)} %pad_maximum_fusion.near_ref.own_ref), channel_id=1, source_target_pairs={{0,6},{1,7},{2,4},{3,5},{4,2},{5,3},{6,0},{7,1},{8,14},{9,15},{10,... | collective-permute-start | bytes 589832 | tf_op jit(solution)/shard_map/ppermute | solution.py:257
  23.6 14.7 %collective-permute-start.2 = (bf16[8,96,128]{2,1,0:T(8,128)(2,1)S(1)}, bf16[8,96,128]{2,1,0:T(8,128)(2,1)S(1)}, u32[]{:S(2)}, u32[]{:S(2)}) collective-permute-start(bf16[8,96,128]{2,1,0:T(8,128)(2,1)S(1)} %collective-permute-done.1.refs_2_), channel_id=1, source_target_pairs={{0,8},{8,0},{16,24},{24,16},{1,9},{9,1},{17,25},{25,17},{2,10},{10... | collective-permute-start | bytes 589832 | tf_op jit(solution)/shard_map/ppermute | solution.py:290
  25.1 18.9 %collective-permute-start.4 = (bf16[96,1024]{1,0:T(8,128)(2,1)S(1)}, bf16[96,1024]{1,0:T(8,128)(2,1)S(1)}, u32[]{:S(2)}, u32[]{:S(2)}) collective-permute-start(bf16[96,1024]{1,0:T(8,128)(2,1)S(1)} %pad_maximum_fusion.near_ref.own_ref), channel_id=1, source_target_pairs={{0,2},{1,3},{2,0},{3,1},{4,6},{5,7},{6,4},{7,5},{8,10},{9,11},{10,... | collective-permute-start | bytes 589832 | tf_op jit(solution)/shard_map/ppermute | solution.py:257
  35.4 8.6 %collective-permute-start.5 = (bf16[96,1024]{1,0:T(8,128)(2,1)S(1)}, bf16[96,1024]{1,0:T(8,128)(2,1)S(1)}, u32[]{:S(2)}, u32[]{:S(2)}) collective-permute-start(bf16[96,1024]{1,0:T(8,128)(2,1)S(1)} %collective-permute-done.3.refs_0_), channel_id=1, source_target_pairs={{0,2},{1,3},{2,0},{3,1},{4,6},{5,7},{6,4},{7,5},{8,10},{9,11},{10,... | collective-permute-start | bytes 589832 | tf_op jit(solution)/shard_map/ppermute | solution.py:257
  35.4 8.6 %collective-permute-start.7 = (bf16[96,1024]{1,0:T(8,128)(2,1)S(1)}, bf16[96,1024]{1,0:T(8,128)(2,1)S(1)}, u32[]{:S(2)}, u32[]{:S(2)}) collective-permute-start(bf16[96,1024]{1,0:T(8,128)(2,1)S(1)} %collective-permute-done.6.refs_3_), channel_id=1, source_target_pairs={{0,1},{1,0},{2,3},{3,2},{4,5},{5,4},{6,7},{7,6},{8,9},{9,8},{10,11... | collective-permute-start | bytes 589832 | tf_op jit(solution)/shard_map/ppermute | solution.py:257
  36.4 7.7 %collective-permute-start.9 = (bf16[96,1024]{1,0:T(8,128)(2,1)S(1)}, bf16[96,1024]{1,0:T(8,128)(2,1)S(1)}, u32[]{:S(2)}, u32[]{:S(2)}) collective-permute-start(bf16[96,1024]{1,0:T(8,128)(2,1)S(1)} %collective-permute-done.8.refs_5_), channel_id=1, source_target_pairs={{0,1},{1,0},{2,3},{3,2},{4,5},{5,4},{6,7},{7,6},{8,9},{9,8},{10,11... | collective-permute-start | bytes 589832 | tf_op jit(solution)/shard_map/ppermute | solution.py:257
  37.5 0.8 %copy-start.2 = (s32[31,128]{1,0:T(8,128)S(1)}, s32[31,128]{1,0:T(8,128)}, u32[]{:S(2)}) copy-start(s32[31,128]{1,0:T(8,128)} %upper_ref.1) | copy-start | bytes 47620
  37.5 0.8 %copy-start.3 = (s32[2,4]{1,0:T(2,128)S(1)}, s32[2,4]{1,0:T(2,128)}, u32[]{:S(2)}) copy-start(s32[2,4]{1,0:T(2,128)} %near_ref.3) | copy-start | bytes 100
  37.5 0.8 %copy-start.4 = (s32[2,16]{1,0:T(2,128)S(1)}, s32[2,16]{1,0:T(2,128)}, u32[]{:S(2)}) copy-start(s32[2,16]{1,0:T(2,128)} %far_ref.1) | copy-start | bytes 388
  38.3 5.8 %copy-start = (f32[1024,32]{0,1:T(8,128)S(1)}, f32[1024,32]{0,1:T(8,128)}, u32[]{:S(2)}) copy-start(f32[1024,32]{0,1:T(8,128)} %param.9) | copy-start | bytes 393220
  48.5 14.7 %copy-start.1 = (f32[1024,32]{0,1:T(8,128)S(1)}, f32[1024,32]{0,1:T(8,128)}, u32[]{:S(2)}) copy-start(f32[1024,32]{0,1:T(8,128)} %param.8) | copy-start | bytes 393220
